TPU v7x, 32 devices: a whole 2x2x4 slice. The times are simulated.
32 devices in a mesh: shard: 4 (over z), ctx: 4 (over x, core), tp: 2 (over y).
Axes of the slice: x: 2, y: 2, z: 4, core: 2. Of those that a mesh axis runs over, the one named last changes fastest.
Arguments:
- inputs: bfloat16 [4, 2048, 2048], P('shard', 'ctx'), may hold values from -6 to 6
- cotangent: bfloat16 [4, 2048, 2048], P('shard', 'ctx'), may hold values from -6 to 6
- query_weight: bfloat16 [2048, 2048], P('shard', 'tp'), may hold values from -0.1875 to 0.1875
- key_weight: bfloat16 [2048, 2048], P('shard', 'tp'), may hold values from -0.1875 to 0.1875
- value_weight: bfloat16 [2048, 2048], P('shard', 'tp'), may hold values from -0.125 to 0.125
- output_weight: bfloat16 [2048, 2048], P('shard', 'tp'), may hold values from -0.75 to 0.75
- up_weight: bfloat16 [2048, 8192], P('shard', 'tp'), may hold values from -0.125 to 0.125
- down_weight: bfloat16 [2048, 8192], P('shard', 'tp'), may hold values from -0.0625 to 0.0625
- query_value_bias: bfloat16 [2, 16, 128], P(None, 'tp', 'shard'), may hold values from -3 to 3
- up_bias: bfloat16 [64, 128], P('tp', 'shard'), may hold values from -3 to 3
- norm_gains: bfloat16 [2, 16, 128], P(None, 'tp', 'shard'), may hold values from 0.25 to 1.75
- other_biases: bfloat16 [4, 16, 128], P(None, 'tp', 'shard'), may hold values from -2 to 2
Outputs:
- outputs: bfloat16 [4, 2048, 2048], P('shard', 'ctx')
- input_grad: bfloat16 [4, 2048, 2048], P('shard', 'ctx')
- grad_query: float32 [2048, 2048], P('shard', 'tp')
- grad_key: float32 [2048, 2048], P('shard', 'tp')
- grad_value: float32 [2048, 2048], P('shard', 'tp')
- grad_output: float32 [2048, 2048], P('shard', 'tp')
- grad_up: float32 [2048, 8192], P('shard', 'tp')
- grad_down: float32 [2048, 8192], P('shard', 'tp')
- grad_qv_bias: float32 [2, 16, 128], P(None, 'tp', 'shard')
- grad_up_bias: float32 [64, 128], P('tp', 'shard')
- grad_gains: float32 [2, 16, 128], P(None, 'tp', 'shard')
- grad_biases: float32 [4, 16, 128], P(None, 'tp', 'shard')
- root_squares: float32 [3], replicated
All inputs are finite; a program needn't handle non-finite values.
Results may differ from a plain program's by a relative error of at most 0.024.
Values may be sent and summed in bfloat16 or wider, within the bound.
No kernel may reach another device: no remote copies, remote signals or barrier semaphores. Data moves between devices by JAX's collectives and lax.ppermute only.
A program may use at most 320 MiB of HBM per device.

v0:
```python
import jax
import jax.numpy as jnp
from jax import lax
from jax.experimental import pallas as pl
from jax.experimental.pallas import tpu as pltpu
from jax.sharding import PartitionSpec as P


D = 2048
H = 16
DH = 128
SCALE = DH ** (-0.5)
BF = jnp.bfloat16
F32 = jnp.float32


epsilon = 1e-12


def product(left, right):
    return jnp.dot(left, right, preferred_element_type=F32)


def transposed_times(left, right):
    return lax.dot_general(left, right, (((0,), (0,)), ((), ())), preferred_element_type=F32)


def normalize(stream):
    center = stream - jnp.mean(stream, axis=-1, keepdims=True)
    factor = lax.rsqrt(jnp.mean(center * center, axis=-1, keepdims=True) + epsilon)
    return (center * factor, factor)


def norm_backward(grad_norm, normed, factor):
    return factor * (
        grad_norm
        - jnp.mean(grad_norm, axis=-1, keepdims=True)
        - normed * jnp.mean(grad_norm * normed, axis=-1, keepdims=True)
    )


def gelu_tanh(values):
    return jax.nn.gelu(values, approximate=True)


def contract(left, right, left_axis, right_axis):
    return lax.dot_general(
        left, right, (((left_axis,), (right_axis,)), ((), ())), preferred_element_type=F32
    )


def forward_kernel(q_ref, kh_ref, kn_ref, vh_ref, vn_ref, out_ref, log_ref):
    q = q_ref[...]
    near = contract(kh_ref[...], q, 1, 1) * SCALE
    far = contract(kn_ref[...], q, 1, 1) * SCALE
    peak = jnp.maximum(jnp.max(near, axis=0, keepdims=True), jnp.max(far, axis=0, keepdims=True))
    near = jnp.exp(near - peak)
    far = jnp.exp(far - peak)
    total = jnp.sum(near, axis=0, keepdims=True) + jnp.sum(far, axis=0, keepdims=True)
    out = contract(vh_ref[...], near.astype(BF), 0, 0) + contract(vn_ref[...], far.astype(BF), 0, 0)
    out_ref[...] = (out / total).T.astype(BF)
    log_ref[0] = peak + jnp.log(total)


def backward_kernel(q_ref, kh_ref, kn_ref, vh_ref, vn_ref, grad_ref, log_ref, dq_ref, dkh_ref, dkn_ref, dvh_ref, dvn_ref, *sums):
    step = pl.program_id(1)
    q = q_ref[...]
    grad = grad_ref[...]
    logsum = log_ref[0]
    probs, d_probs = [], []
    for k_ref, v_ref in ((kh_ref, vh_ref), (kn_ref, vn_ref)):
        probs.append(jnp.exp(contract(k_ref[...], q, 1, 1) * SCALE - logsum))
        d_probs.append(contract(v_ref[...], grad, 1, 1))
    inner = sum(jnp.sum(p * d, axis=0, keepdims=True) for p, d in zip(probs, d_probs))
    dq = 0.0
    for at, k_ref in enumerate((kh_ref, kn_ref)):
        d_scores = (probs[at] * (d_probs[at] - inner)).astype(BF)
        dq = dq + contract(k_ref[...], d_scores, 0, 0)
        dk = contract(d_scores, q, 1, 0)
        dv = contract(probs[at].astype(BF), grad, 1, 0)

        @pl.when(step == 0)
        def _():
            sums[at][...] = dk
            sums[2 + at][...] = dv

        @pl.when(step > 0)
        def _():
            sums[at][...] += dk
            sums[2 + at][...] += dv
    dq_ref[...] = (dq * SCALE).T.astype(BF)

    @pl.when(step == pl.num_programs(1) - 1)
    def _():
        dkh_ref[...] = (sums[0][...] * SCALE).astype(BF)
        dkn_ref[...] = (sums[1][...] * SCALE).astype(BF)
        dvh_ref[...] = sums[2][...].astype(BF)
        dvn_ref[...] = sums[3][...].astype(BF)


def kv_specs(rows, heads):
    k = pl.BlockSpec((rows, DH), lambda h, b: (0, h))
    v = pl.BlockSpec((rows, DH), lambda h, b: (0, heads + h))
    return k, k, v, v


def attention(q, kvh, kvn, block=None):
    rows, width = q.shape
    block = block or rows
    heads = width // DH
    row = pl.BlockSpec((block, DH), lambda h, b: (b, h))
    log = pl.BlockSpec((1, 1, block), lambda h, b: (h, 0, b))
    return pl.pallas_call(forward_kernel, grid=(heads, rows // block),
        in_specs=[row, *kv_specs(kvh.shape[0], heads)], out_specs=[row, log],
        out_shape=[jax.ShapeDtypeStruct((rows, width), BF), jax.ShapeDtypeStruct((heads, 1, rows), F32)],
        name="attention_forward")(q, kvh, kvn, kvh, kvn)


def attention_back(q, kvh, kvn, grad, logsum, block=None):
    rows, width = q.shape
    block = block or rows
    heads = width // DH
    keys = kvh.shape[0]
    row = pl.BlockSpec((block, DH), lambda h, b: (b, h))
    log = pl.BlockSpec((1, 1, block), lambda h, b: (h, 0, b))
    k = pl.BlockSpec((keys, DH), lambda h, b: (0, h))
    return pl.pallas_call(backward_kernel, grid=(heads, rows // block),
        in_specs=[row, *kv_specs(keys, heads), row, log],
        out_specs=[row, k, k, k, k],
        out_shape=[jax.ShapeDtypeStruct((rows, width), BF)] + [jax.ShapeDtypeStruct((keys, width), BF)] * 4,
        scratch_shapes=[pltpu.VMEM((keys, DH), F32)] * 4,
        name="attention_backward")(q, kvh, kvn, kvh, kvn, grad, logsum)


def sum_kernel(*refs):
    count = (len(refs) - 1) // 2
    total = 0.0
    for at in range(count):
        total = total + contract(refs[at][...], refs[count + at][...], 1, 1)
    refs[-1][...] = total.astype(refs[-1].dtype)


def sum_products(lefts, rights, block=256):
    rows = lefts[0].shape[0]
    width = rights[0].shape[0]
    return pl.pallas_call(
        sum_kernel,
        grid=(width // block,),
        in_specs=[pl.BlockSpec(left.shape, lambda n: (0, 0)) for left in lefts]
        + [pl.BlockSpec((block, right.shape[1]), lambda n: (n, 0)) for right in rights],
        out_specs=pl.BlockSpec((rows, block), lambda n: (0, n)),
        out_shape=jax.ShapeDtypeStruct((rows, width), BF),
        name="sum_products",
    )(*lefts, *rights)


def after(value, *others):
    return lax.optimization_barrier((value,) + others)[0]


def across(array, step, axis="ctx"):
    size = lax.axis_size(axis)
    return lax.ppermute(array, axis, [(at, at ^ step) for at in range(size)])


def collect(piece):
    return lax.all_gather(piece, "shard", axis=0, tiled=True)


def scatter(total):
    return lax.psum_scatter(total, "shard", scatter_dimension=0, tiled=True)


def scatter_direct(total):
    size = lax.axis_size("shard")
    rows = total.shape[0] // size
    index = lax.axis_index("shard")

    def block(step):
        return lax.dynamic_slice_in_dim(total, ((index + step) % size) * rows, rows, 0)

    got = [
        lax.ppermute(block(step), "shard", [(at, (at + step) % size) for at in range(size)])
        for step in range(1, size)
    ]
    return block(0), got


def sum_direct(mine, got):
    return sum([item.astype(F32) for item in got], mine.astype(F32)).astype(BF)


def fill(own, far):
    return [own, across(own, 1), far, across(far, 1)]


def spread(own):
    return fill(own, across(own, 2))


def near_sums(parts):
    return [
        (parts[q].astype(F32) + across(parts[q + 1], 1).astype(F32)).astype(BF) for q in (0, 2)
    ]


def far_sum(own, far, *hold):
    got = across(far, 2)
    if hold:
        got = after(got, *hold)
    return (own.astype(F32) + got.astype(F32)).astype(BF)


def join_pair(own, far):
    return fill(far_sum(own, far), far_sum(far, own))


def ordered(pieces, bits):
    low, high = bits
    swapped = [jnp.where(high, pieces[q ^ 2], pieces[q]) for q in range(4)]
    return [jnp.where(low, swapped[q ^ 1], swapped[q]) for q in range(4)]


def tp_sum(low):
    return low.astype(F32) + across(low, 1, "tp").astype(F32)


def butterfly(flat, axes):
    for axis in axes:
        step = 1
        while step < lax.axis_size(axis):
            flat = flat + across(flat, step, axis)
            step *= 2
    return flat


def shards(
    inputs,
    cotangent,
    query_weight,
    key_weight,
    value_weight,
    output_weight,
    up_weight,
    down_weight,
    query_value_bias,
    up_bias,
    norm_gains,
    other_biases,
):
    local_rows = inputs.shape[1]
    member = lax.axis_index("ctx")
    relative = jnp.arange(4) ^ member
    bits = ((member & 1) == 1, (member & 2) == 2)
    n_shard = lax.axis_size("shard")
    n_tp = lax.axis_size("tp")

    def own_columns(weight, step=0):
        width = weight.shape[1] // 4
        return lax.dynamic_slice_in_dim(weight, (member ^ step) * width, width, 1)

    tokens = inputs.reshape(local_rows, D)
    tokens_far = across(tokens, 2)
    grad_out = cotangent.reshape(local_rows, D).astype(F32)

    small = (query_value_bias, norm_gains, other_biases, up_bias)
    packed = jnp.concatenate([item.reshape(1, -1) for item in small], axis=1)
    tp_index = lax.axis_index("tp")
    slot = lax.axis_index("shard") * n_tp + tp_index
    packed_all = lax.dynamic_update_slice_in_dim(
        jnp.zeros((n_shard * n_tp, packed.shape[1]), BF), packed, slot, 0
    )
    packed_all = butterfly(packed_all, ("tp", "shard"))
    packed_all = packed_all.reshape(n_shard, n_tp, packed.shape[1])
    at = 0
    small_all = []
    for item in small:
        part = packed_all[:, :, at : at + item.size].reshape((n_shard, n_tp) + item.shape)
        at += item.size
        small_all.append(part)
    qv_all = lax.dynamic_index_in_dim(small_all[0], tp_index, 1, False)
    qv_half = qv_all.transpose(1, 2, 0, 3).reshape(2, 4, -1).astype(F32)
    qv_vector = jnp.take(qv_half, relative, axis=1)
    gains = small_all[1].transpose(2, 1, 3, 0, 4).reshape(2, D).astype(F32)
    biases = small_all[2].transpose(2, 1, 3, 0, 4).reshape(4, D).astype(F32)
    up_all = lax.dynamic_index_in_dim(small_all[3], tp_index, 1, False)
    up_vector = jnp.take(up_all.transpose(1, 0, 2).reshape(4, -1).astype(F32), relative, axis=0)

    kv_width = key_weight.shape[1] // 4
    heads_each = kv_width // DH
    heads_here = 4 * heads_each
    ff_half = up_weight.shape[1] // 8
    kv_own = collect(jnp.concatenate([own_columns(key_weight), own_columns(value_weight)], axis=1))
    query_own = collect(own_columns(query_weight))
    output_own = collect(own_columns(output_weight))
    up_piece = own_columns(up_weight)
    down_piece = own_columns(down_weight)
    up_own = [collect(up_piece[:, half * ff_half : (half + 1) * ff_half]) for half in range(2)]
    down_own = [collect(down_piece[:, half * ff_half : (half + 1) * ff_half]) for half in range(2)]
    down_far = collect(own_columns(down_weight, 2)[:, ff_half:])
    key_value_w = fill(kv_own, across(after(kv_own, tokens_far), 2))
    query_w = spread(query_own)

    tokens_two = jnp.concatenate([tokens, tokens_far], axis=0)
    zero_row = jnp.zeros((kv_width,), F32)
    kv_here = [
        (
            product(tokens_two, key_value_w[q]) + jnp.concatenate([zero_row, qv_vector[1, q]])
        ).astype(BF)
        for q in range(4)
    ]
    output_w = spread(after(output_own, kv_here[3]))
    kv_near = [across(kv_here[q ^ 1], 1) for q in range(4)]
    queries = [(product(tokens, query_w[q]) + qv_vector[0, q]).astype(BF) for q in range(4)]
    attended, logsums = [], []
    for q in range(4):
        out, log = attention(queries[q], kv_here[q], kv_near[q])
        attended.append(out)
        logsums.append(log)
    attn_low = sum_products(attended, output_w)
    up_far = across(up_own[0], 2)
    up_w = [fill(up_own[0], up_far), spread(after(up_own[1], attended[3]))]
    attn_branch = tp_sum(attn_low) + biases[0]
    normed_one, factor_one = normalize(tokens.astype(F32) + attn_branch)
    hidden_one = normed_one * gains[0] + biases[1]
    hidden_low = hidden_one.astype(BF)

    pairs = [(half, q) for half in range(2) for q in range(4)]
    up_rows = up_vector.reshape(4, 2, ff_half)
    pre_act = [product(hidden_low, up_w[half][q]) + up_rows[q, half] for half, q in pairs]
    activated = [gelu_tanh(item).astype(BF) for item in pre_act]
    down_w = [
        spread(after(down_own[0], activated[0])),
        fill(down_own[1], down_far),
    ]
    mlp_low = sum_products(activated, [down_w[half][q] for half, q in pairs])
    mlp_branch = tp_sum(mlp_low) + biases[2]
    second = hidden_one + mlp_branch
    normed_two, factor_two = normalize(second)
    result = normed_two * gains[1] + biases[3]
    grad_second = norm_backward(grad_out * gains[1], normed_two, factor_two)
    grad_mlp = grad_second.astype(BF)
    down_parts = [transposed_times(grad_mlp, item).astype(BF) for item in activated]
    down_late = near_sums(down_parts[4:8])
    down_early = near_sums(down_parts[0:4])
    grad_mlp_then = after(grad_mlp, *down_late, *down_early)
    down_second = [scatter(item) for item in down_late]
    grad_pre = []
    for at, (half, q) in enumerate(pairs):
        _, gelu_pull = jax.vjp(gelu_tanh, pre_act[at])
        grad_pre.append(gelu_pull(product(grad_mlp_then, down_w[half][q]))[0].astype(BF))
    hidden_part = sum_products(grad_pre, [up_w[half][q] for half, q in pairs])
    down_first = scatter(far_sum(*down_early, hidden_part))
    grad_hidden = grad_second + tp_sum(hidden_part)
    up_parts = [transposed_times(hidden_low, item).astype(BF) for item in grad_pre]
    up_late = near_sums(up_parts[4:8])
    up_second = [scatter(item) for item in up_late]
    up_early = near_sums(up_parts[0:4])
    grad_first = norm_backward(grad_hidden * gains[0], normed_one, factor_one)
    grad_branch = grad_first.astype(BF)
    grad_attended = [product(grad_branch, output_w[q]).astype(BF) for q in range(4)]
    up_total = far_sum(*up_early, grad_branch)
    up_first = scatter(up_total)
    output_early = near_sums(
        [transposed_times(grad_branch, attended[q]).astype(BF) for q in range(4)]
    )
    grad_attended[2:] = lax.optimization_barrier((*grad_attended[2:], up_total))[:-1]
    grad_q, here_parts, near_parts = [], [], []
    for q in range(4):
        dq, dk_here, dk_near, dv_here, dv_near = attention_back(
            queries[q], kv_here[q], kv_near[q], grad_attended[q], logsums[q]
        )
        grad_q.append(dq)
        here_parts.append((dk_here, dv_here))
        near_parts.append((across(dk_near, 1), across(dv_near, 1)))
    two_sums = [
        jnp.concatenate(
            [
                (here_parts[q][at].astype(F32) + near_parts[q ^ 1][at].astype(F32)).astype(BF)
                for at in range(2)
            ],
            axis=1,
        )
        for q in range(4)
    ]
    far_sums = [across(two_sums[q][local_rows:], 2) for q in range(4)]
    grad_kv = [
        (two_sums[q][:local_rows].astype(F32) + far_sums[q ^ 2].astype(F32)).astype(BF)
        for q in range(4)
    ]
    output_direct = scatter_direct(far_sum(*output_early, *grad_q))
    query_early = near_sums([transposed_times(tokens, grad_q[q]).astype(BF) for q in range(4)])
    kv_total = far_sum(
        *near_sums([transposed_times(tokens, grad_kv[q]).astype(BF) for q in range(4)])
    )
    kv_mine = scatter(kv_total)
    query_mine, query_got = scatter_direct(far_sum(*query_early, kv_total))
    output_mine, output_got = lax.optimization_barrier((*output_direct, kv_total))[:2]
    down_first, up_first, grad_q_then = (
        after(item, kv_total) for item in (down_first, up_first, grad_q[0])
    )
    down_second = [after(item, kv_total) for item in down_second]
    up_second = [after(item, kv_total) for item in up_second]
    down_grads = [spread(down_first), join_pair(*down_second)]
    up_grads = [spread(up_first), join_pair(*up_second)]
    output_grads = spread(sum_direct(output_mine, output_got))
    query_grads = spread(sum_direct(query_mine, query_got))
    kv_grads = spread(kv_mine)
    input_part = sum_products([grad_q_then] + grad_q[1:] + grad_kv, query_w + key_value_w)
    input_grad = grad_first + tp_sum(input_part)

    def canonical(rows):
        return jnp.take(jnp.stack(rows), relative, axis=0).reshape(-1)

    def column_sums(array):
        return jnp.sum(array.astype(F32), axis=0)

    pieces = [
        canonical([column_sums(grad_q[q]) for q in range(4)]),
        canonical([column_sums(grad_kv[q][:, kv_width:]) for q in range(4)]),
        canonical(
            [
                jnp.concatenate([column_sums(grad_pre[q]), column_sums(grad_pre[4 + q])])
                for q in range(4)
            ]
        ),
        jnp.sum(grad_hidden * normed_one, axis=0),
        jnp.sum(grad_out * normed_two, axis=0),
        column_sums(grad_branch),
        jnp.sum(grad_hidden, axis=0),
        column_sums(grad_mlp),
        jnp.sum(grad_out, axis=0),
        jnp.stack(
            [
                jnp.sum(second * second),
                jnp.sum(attn_branch * attn_branch),
                jnp.sum(mlp_branch * mlp_branch),
            ]
        ),
    ]
    sizes = [item.shape[0] for item in pieces]
    flat = jnp.concatenate(pieces + [jnp.zeros((-sum(sizes) % 1024,), F32)]).reshape(-1, 128)
    flat = butterfly(after(flat, kv_total), ("ctx", "shard")).reshape(-1)
    totals = []
    at = 0
    for size in sizes:
        totals.append(flat[at : at + size])
        at += size
    shard_index = lax.axis_index("shard")
    piece = DH // n_shard
    heads_part = H // n_tp

    def last_piece(array, axis):
        return lax.dynamic_slice_in_dim(array, shard_index * piece, piece, axis)

    grad_qv_bias = last_piece(jnp.stack(totals[0:2]).reshape(2, heads_here, DH), 2)
    grad_up_bias = last_piece(totals[2].reshape(-1, DH), 1)

    def feature_rows(rows):
        stacked = jnp.stack(rows).reshape(len(rows), H, DH)
        return last_piece(
            lax.dynamic_slice_in_dim(stacked, tp_index * heads_part, heads_part, 1), 2
        )

    grad_gains = feature_rows(totals[3:5])
    grad_biases = feature_rows(totals[5:9])
    count_all = local_rows * n_shard * lax.axis_size("ctx") * D
    root_squares = jnp.sqrt(totals[9] / count_all)

    def whole(parts):
        return jnp.concatenate(ordered(parts, bits), axis=1).astype(F32)

    def whole_halves(parts):
        placed = [ordered(half, bits) for half in parts]
        return jnp.concatenate(
            [placed[half][q] for q in range(4) for half in range(2)], axis=1
        ).astype(F32)

    return (
        result.astype(BF).reshape(1, local_rows, D),
        input_grad.astype(BF).reshape(1, local_rows, D),
        whole(query_grads),
        whole([item[:, :kv_width] for item in kv_grads]),
        whole([item[:, kv_width:] for item in kv_grads]),
        whole(output_grads),
        whole_halves(up_grads),
        whole_halves(down_grads),
        grad_qv_bias,
        grad_up_bias,
        grad_gains,
        grad_biases,
        root_squares,
    )


def solution(mesh):
    if mesh.shape["ctx"] != 4 or mesh.shape["tp"] != 2:
        raise ValueError("unexpected mesh")
    placed = (
        P("shard", "ctx", None),
        P("shard", "ctx", None),
        P("shard", "tp"),
        P("shard", "tp"),
        P("shard", "tp"),
        P("shard", "tp"),
        P("shard", "tp"),
        P("shard", "tp"),
        P(None, "tp", "shard"),
        P("tp", "shard"),
        P(None, "tp", "shard"),
        P(None, "tp", "shard"),
    )
    return jax.shard_map(
        shards,
        mesh=mesh,
        in_specs=placed,
        out_specs=(
            P("shard", "ctx", None),
            P("shard", "ctx", None),
            P("shard", "tp"),
            P("shard", "tp"),
            P("shard", "tp"),
            P("shard", "tp"),
            P("shard", "tp"),
            P("shard", "tp"),
            P(None, "tp", "shard"),
            P("tp", "shard"),
            P(None, "tp", "shard"),
            P(None, "tp", "shard"),
            P(),
        ),
        check_vma=False,
    )
```

profile of v0, /device:TPU:0, one launch (start us, length us, event | category | flops | bytes accessed | tf_op | source)
XLA Modules:
  0.0 1071.3 jit_solution(6090487517288881297)
XLA Ops:
  20.6 43.1 %collective-permute-done.3 = bf16[512,2048]{1,0:T(8,128)(2,1)} collective-permute-done((bf16[512,2048]{1,0:T(8,128)(2,1)S(1)}, bf16[512,2048]{1,0:T(8,128)(2,1)}, u32[]{:S(2)}, u32[]{:S(2)}) %collective-permute-start.3) | collective-permute-done | bytes 2097184 | tf_op jit(solution)/shard_map/ppermute | solution.py:163
  67.7 19.8 %all-gather.9.cloned.1.call-done.refs_8_ = bf16[2048,256]{1,0:T(8,128)(2,1)} async-done(((bf16[512,256]{1,0:T(8,128)(2,1)}), bf16[2048,256]{1,0:T(8,128)(2,1)}) %all-gather.9.cloned.1.call-update) | async-done | bytes 1048592 | tf_op jit(solution)/shard_map/all_gather | solution.py:167
  89.0 23.5 %collective-permute-done.9.refs_14_ = bf16[2048,512]{1,0:T(8,128)(2,1)} collective-permute-done((bf16[2048,512]{1,0:T(8,128)(2,1)}, bf16[2048,512]{1,0:T(8,128)(2,1)}, u32[]{:S(2)}, u32[]{:S(2)}) %collective-permute-start.9) | collective-permute-done | bytes 2097184 | tf_op jit(solution)/shard_map/ppermute | solution.py:163
  123.7 9.6 collective-permute-done.8.refs_10_
  133.3 5.6 add_convert_fusion.16.kh_ref.vh_ref
  145.5 5.5 add_convert_fusion.15.kh_ref.vh_ref
  151.1 5.6 add_convert_fusion.14.kh_ref.vh_ref
  157.6 11.8 %collective-permute-done.15.refs_6_ = bf16[2048,256]{1,0:T(8,128)(2,1)} collective-permute-done((bf16[2048,256]{1,0:T(8,128)(2,1)}, bf16[2048,256]{1,0:T(8,128)(2,1)}, u32[]{:S(2)}, u32[]{:S(2)}) %collective-permute-start.15) | collective-permute-done | bytes 1048608 | tf_op jit(solution)/shard_map/ppermute | solution.py:163
  178.9 6.6 attention_forward.5
  187.0 6.4 attention_forward.4
  193.5 6.4 attention_forward.7
  199.9 6.4 attention_forward.6
  206.3 8.3 sum_products.4
  218.3 15.6 %collective-permute-done.19.refs_10_ = bf16[2048,512]{1,0:T(8,128)(2,1)} collective-permute-done((bf16[2048,512]{1,0:T(8,128)(2,1)}, bf16[2048,512]{1,0:T(8,128)(2,1)}, u32[]{:S(2)}, u32[]{:S(2)}) %collective-permute-start.19) | collective-permute-done | bytes 2097184 | tf_op jit(solution)/shard_map/ppermute | solution.py:163
  235.9 26.7 %collective-permute-done.17 = bf16[512,2048]{1,0:T(8,128)(2,1)} collective-permute-done((bf16[512,2048]{1,0:T(8,128)(2,1)}, bf16[512,2048]{1,0:T(8,128)(2,1)}, u32[]{:S(2)}, u32[]{:S(2)}) %collective-permute-start.17) | collective-permute-done | bytes 2097184 | tf_op jit(solution)/shard_map/ppermute | solution.py:163
  262.6 4.9 fusion.137
  274.8 8.4 collective-permute-done.22.refs_14_
  283.2 5.0 multiply_convert_fusion.3
  292.5 11.3 %all-gather.21.cloned.1.call-done.refs_12_ = bf16[2048,512]{1,0:T(8,128)(2,1)} async-done(((bf16[512,512]{1,0:T(8,128)(2,1)}), bf16[2048,512]{1,0:T(8,128)(2,1)}) %all-gather.21.cloned.1.call-update) | async-done | bytes 2097168 | tf_op jit(solution)/shard_map/all_gather | solution.py:167
  303.8 46.6 %all-gather.23.cloned.1.call-done.refs_14_ = bf16[2048,512]{1,0:T(8,128)(2,1)} async-done(((bf16[512,512]{1,0:T(8,128)(2,1)}), bf16[2048,512]{1,0:T(8,128)(2,1)}) %all-gather.23.cloned.1.call-update) | async-done | bytes 2097168 | tf_op jit(solution)/shard_map/all_gather | solution.py:167
  351.0 5.0 multiply_convert_fusion.1
  373.2 15.2 %sum_products.5 = bf16[512,2048]{1,0:T(8,128)(2,1)} custom-call(bf16[512,512]{1,0:T(8,128)(2,1)} %get-tuple-element.257.refs_0_, bf16[512,512]{1,0:T(8,128)(2,1)} %get-tuple-element.259.refs_1_, bf16[512,512]{1,0:T(8,128)(2,1)} %get-tuple-element.261.refs_2_, bf16[512,512]{1,0:T(8,128)(2,1)} %get-tuple-element.263.refs_3_, ...), custom_call_target="tpu_custom_call" | custom-call | tf_op jit(solution)/shard_map/sum_products/pallas_call | solution.py:146
  390.1 46.6 %collective-permute-done.29 = bf16[512,2048]{1,0:T(8,128)(2,1)} collective-permute-done((bf16[512,2048]{1,0:T(8,128)(2,1)}, bf16[512,2048]{1,0:T(8,128)(2,1)}, u32[]{:S(2)}, u32[]{:S(2)}) %collective-permute-start.29) | collective-permute-done | bytes 2097184 | tf_op jit(solution)/shard_map/ppermute | solution.py:163
  436.8 5.1 fusion.135
  463.2 4.9 add_convert_fusion.10
  468.1 5.0 add_convert_fusion.9
  509.4 15.4 %sum_products.6 = bf16[512,2048]{1,0:T(8,128)(2,1)} custom-call(bf16[512,512]{1,0:T(8,128)(2,1)} %get-tuple-element.170.refs_0_, bf16[512,512]{1,0:T(8,128)(2,1)} %get-tuple-element.174.refs_1_, bf16[512,512]{1,0:T(8,128)(2,1)} %get-tuple-element.178.refs_2_, bf16[512,512]{1,0:T(8,128)(2,1)} %copy-done.81, bf16[512,512]{1,0:T(8,128)(2,1)} %get-tuple-element.172.refs_4_, ...), custom_call_target="tpu_custom_call" | custom-call | tf_op jit(solution)/shard_map/sum_products/pallas_call | solution.py:146
  536.8 36.5 %collective-permute-done.34 = bf16[512,2048]{1,0:T(8,128)(2,1)} collective-permute-done((bf16[512,2048]{1,0:T(8,128)(2,1)}, bf16[512,2048]{1,0:T(8,128)(2,1)}, u32[]{:S(2)}, u32[]{:S(2)}) %collective-permute-start.34) | collective-permute-done | bytes 2097184 | tf_op jit(solution)/shard_map/ppermute | solution.py:163
  573.2 7.2 multiply_reduce_fusion.3
  608.3 46.4 %collective-permute-done.84 = bf16[2048,512]{1,0:T(8,128)(2,1)S(1)} collective-permute-done((bf16[2048,512]{1,0:T(8,128)(2,1)}, bf16[2048,512]{1,0:T(8,128)(2,1)S(1)}, u32[]{:S(2)}, u32[]{:S(2)}) %collective-permute-start.84) | collective-permute-done | bytes 2097184 | tf_op jit(solution)/shard_map/ppermute | solution.py:163
  668.8 8.6 attention_backward.4
  681.2 8.7 attention_backward.5
  703.2 9.1 attention_backward.6
  716.4 8.8 attention_backward.7
  737.9 16.6 %collective-permute-done.68 = bf16[2048,256]{0,1:T(8,128)(2,1)} collective-permute-done((bf16[2048,256]{0,1:T(8,128)(2,1)}, bf16[2048,256]{0,1:T(8,128)(2,1)}, u32[]{:S(2)}, u32[]{:S(2)}) %collective-permute-start.68) | collective-permute-done | bytes 1048608 | tf_op jit(solution)/shard_map/ppermute | solution.py:163
  761.6 7.9 collective-permute-done.49
  769.7 9.4 collective-permute-done.47
  791.3 54.2 %collective-permute-done.42 = bf16[512,512]{1,0:T(8,128)(2,1)S(1)} collective-permute-done((bf16[512,512]{1,0:T(8,128)(2,1)S(1)}, bf16[512,512]{1,0:T(8,128)(2,1)S(1)}, u32[]{:S(2)}, u32[]{:S(2)}) %collective-permute-start.42) | collective-permute-done | bytes 524320 | tf_op jit(solution)/shard_map/ppermute | solution.py:163
  859.3 11.3 %collective-permute-done.56 = bf16[2048,256]{0,1:T(8,128)(2,1)} collective-permute-done((bf16[2048,256]{0,1:T(8,128)(2,1)}, bf16[2048,256]{0,1:T(8,128)(2,1)}, u32[]{:S(2)}, u32[]{:S(2)}) %collective-permute-start.56) | collective-permute-done | bytes 1048608 | tf_op jit(solution)/shard_map/ppermute | solution.py:163
  882.3 13.5 %sum_products.7 = bf16[512,2048]{1,0:T(8,128)(2,1)} custom-call(bf16[512,256]{1,0:T(8,128)(2,1)} %get-tuple-element.99.refs_0_, bf16[512,256]{1,0:T(8,128)(2,1)} %get-tuple-element.100.refs_1_, bf16[512,256]{1,0:T(8,128)(2,1)} %get-tuple-element.101.refs_2_, bf16[512,256]{1,0:T(8,128)(2,1)} %get-tuple-element.102.refs_3_, bf16[512,512]{1,0:T(8,128)(2,1)} %copy-done.37, ...), custom_call_target="tpu_custom_call" | custom-call | tf_op jit(solution)/shard_map/sum_products/pallas_call | solution.py:146
  895.8 9.2 collective-permute-done.94
  905.5 8.1 collective-permute-done.58
  913.6 14.6 %collective-permute-start.95 = (f32[152,128]{1,0:T(8,128)S(1)}, f32[152,128]{1,0:T(8,128)S(1)}, u32[]{:S(2)}, u32[]{:S(2)}) collective-permute-start(f32[152,128]{1,0:T(8,128)S(1)} %add.729), channel_id=1, source_target_pairs={{0,16},{8,24},{16,0},{24,8},{1,17},{9,25},{17,1},{25,9},{2,18},{10... | collective-permute-start | bytes 233480 | tf_op jit(solution)/shard_map/ppermute | solution.py:163
  945.5 10.2 collective-permute-done.82
  956.7 21.4 %collective-permute-done.88 = bf16[512,512]{1,0:T(8,128)(2,1)S(1)} collective-permute-done((bf16[512,512]{1,0:T(8,128)(2,1)S(1)}, bf16[512,512]{1,0:T(8,128)(2,1)S(1)}, u32[]{:S(2)}, u32[]{:S(2)}) %collective-permute-start.88) | collective-permute-done | bytes 524320 | tf_op jit(solution)/shard_map/ppermute | solution.py:163
  979.2 14.5 %collective-permute-done.60 = bf16[512,256]{0,1:T(8,128)(2,1)} collective-permute-done((bf16[512,256]{0,1:T(8,128)(2,1)S(1)}, bf16[512,256]{0,1:T(8,128)(2,1)}, u32[]{:S(2)}, u32[]{:S(2)}) %collective-permute-start.60) | collective-permute-done | bytes 262176 | tf_op jit(solution)/shard_map/ppermute | solution.py:163
  1036.7 6.8 convert_element_type.931
  1046.1 7.4 collective-permute-done.53
  (642 shorter events, 350.3 us)
Async XLA Ops:
  7.2 56.5 %all-gather.11.cloned.1.call-start = ((), (), s32[]{:S(2)}) async-start(), calls=%async_computation.8 | async-start | bytes 2621440 | tf_op jit(solution)/shard_map/all_gather | solution.py:167
  9.3 78.3 %all-gather.9.cloned.1.call-start = ((), (), s32[]{:S(2)}) async-start(), calls=%async_computation.7 | async-start | bytes 1310720 | tf_op jit(solution)/shard_map/all_gather | solution.py:167
  10.1 133.9 %all-gather.13.cloned.1.call-start = ((), (), s32[]{:S(2)}) async-start(), calls=%async_computation.9 | async-start | bytes 1310720 | tf_op jit(solution)/shard_map/all_gather | solution.py:167
  12.0 173.5 %all-gather.15.cloned.1.call-start = ((), (), s32[]{:S(2)}) async-start(), calls=%async_computation.10 | async-start | bytes 2621440 | tf_op jit(solution)/shard_map/all_gather | solution.py:167
  14.3 219.6 %all-gather.17.cloned.1.call-start = ((), (), s32[]{:S(2)}) async-start(), calls=%async_computation.11 | async-start | bytes 2621440 | tf_op jit(solution)/shard_map/all_gather | solution.py:167
  14.9 259.4 %all-gather.19.cloned.1.call-start = ((), (), s32[]{:S(2)}) async-start(), calls=%async_computation.12 | async-start | bytes 2621440 | tf_op jit(solution)/shard_map/all_gather | solution.py:167
  14.9 48.8 %collective-permute-start.3 = (bf16[512,2048]{1,0:T(8,128)(2,1)S(1)}, bf16[512,2048]{1,0:T(8,128)(2,1)}, u32[]{:S(2)}, u32[]{:S(2)}) collective-permute-start(bf16[512,2048]{1,0:T(8,128)(2,1)S(1)} %bitcast.274), channel_id=1, source_target_pairs={{0,4},{2,6},{4,0},{6,2},{1,5},{3,7},{5,1},{7,3},{8,12},{10,14},{12... | collective-permute-start | bytes 6291464 | tf_op jit(solution)/shard_map/ppermute | solution.py:163
  20.6 283.2 %all-gather.21.cloned.1.call-start = ((), (), s32[]{:S(2)}) async-start(), calls=%async_computation.13 | async-start | bytes 2621440 | tf_op jit(solution)/shard_map/all_gather | solution.py:167
  63.7 48.8 %collective-permute-start.9 = (bf16[2048,512]{1,0:T(8,128)(2,1)}, bf16[2048,512]{1,0:T(8,128)(2,1)}, u32[]{:S(2)}, u32[]{:S(2)}) collective-permute-start(bf16[2048,512]{1,0:T(8,128)(2,1)} %all-gather.11.cloned.1.call-done.refs_12_), channel_id=1, source_target_pairs={{0,4},{2,6},{4,0},{6,2},{1,5},{3,7},{5,1},{7,3},{8,12},{10,14},{12... | collective-permute-start | bytes 6291464 | tf_op jit(solution)/shard_map/ppermute | solution.py:163
  66.1 46.5 %collective-permute-start = (bf16[8,3072]{1,0:T(8,128)(2,1)S(1)}, bf16[8,3072]{1,0:T(8,128)(2,1)S(1)}, u32[]{:S(2)}, u32[]{:S(2)}) collective-permute-start(bf16[8,3072]{1,0:T(8,128)(2,1)S(1)} %dynamic_update_slice.5), channel_id=1, source_target_pairs={{0,1},{1,0},{2,3},{3,2},{4,5},{5,4},{6,7},{7,6},{8,9},{9,8},{10,11... | collective-permute-start | bytes 147464 | tf_op jit(solution)/shard_map/ppermute | solution.py:163
  67.7 282.7 %all-gather.23.cloned.1.call-start = ((), (), s32[]{:S(2)}) async-start(), calls=%async_computation.14 | async-start | bytes 2621440 | tf_op jit(solution)/shard_map/all_gather | solution.py:167
  87.5 45.8 %collective-permute-start.8 = (bf16[2048,256]{1,0:T(8,128)(2,1)}, bf16[2048,256]{1,0:T(8,128)(2,1)}, u32[]{:S(2)}, u32[]{:S(2)}) collective-permute-start(bf16[2048,256]{1,0:T(8,128)(2,1)} %all-gather.9.cloned.1.call-done.refs_8_), channel_id=1, source_target_pairs={{0,4},{2,6},{4,0},{6,2},{1,5},{3,7},{5,1},{7,3},{8,12},{10,14},{12... | collective-permute-start | bytes 3145736 | tf_op jit(solution)/shard_map/ppermute | solution.py:163
  157.1 42.8 %collective-permute-start.11 = (bf16[1024,512]{1,0:T(8,128)(2,1)S(1)}, bf16[1024,512]{1,0:T(8,128)(2,1)}, u32[]{:S(2)}, u32[]{:S(2)}) collective-permute-start(bf16[1024,512]{1,0:T(8,128)(2,1)S(1)} %add_convert_fusion.13.kh_ref.vh_ref), channel_id=1, source_target_pairs={{0,2},{2,0},{4,6},{6,4},{1,3},{3,1},{5,7},{7,5},{8,10},{10,8},{12,... | collective-permute-start | bytes 3145736 | tf_op jit(solution)/shard_map/ppermute | solution.py:163
  157.2 49.1 %collective-permute-start.14 = (bf16[2048,256]{1,0:T(8,128)(2,1)}, bf16[2048,256]{1,0:T(8,128)(2,1)}, u32[]{:S(2)}, u32[]{:S(2)}) collective-permute-start(bf16[2048,256]{1,0:T(8,128)(2,1)} %all-gather.13.cloned.1.call-done.refs_4_), channel_id=1, source_target_pairs={{0,2},{2,0},{4,6},{6,4},{1,3},{3,1},{5,7},{7,5},{8,10},{10,8},{12,... | collective-permute-start | bytes 3145736 | tf_op jit(solution)/shard_map/ppermute | solution.py:163
  185.4 48.5 %collective-permute-start.19 = (bf16[2048,512]{1,0:T(8,128)(2,1)}, bf16[2048,512]{1,0:T(8,128)(2,1)}, u32[]{:S(2)}, u32[]{:S(2)}) collective-permute-start(bf16[2048,512]{1,0:T(8,128)(2,1)} %all-gather.15.cloned.1.call-done.refs_8_), channel_id=1, source_target_pairs={{0,4},{2,6},{4,0},{6,2},{1,5},{3,7},{5,1},{7,3},{8,12},{10,14},{12... | collective-permute-start | bytes 6291464 | tf_op jit(solution)/shard_map/ppermute | solution.py:163
  214.6 48.1 %collective-permute-start.17 = (bf16[512,2048]{1,0:T(8,128)(2,1)}, bf16[512,2048]{1,0:T(8,128)(2,1)}, u32[]{:S(2)}, u32[]{:S(2)}) collective-permute-start(bf16[512,2048]{1,0:T(8,128)(2,1)} %sum_products.4), channel_id=1, source_target_pairs={{0,1},{1,0},{2,3},{3,2},{4,5},{5,4},{6,7},{7,6},{8,9},{9,8},{10,11... | collective-permute-start | bytes 6291464 | tf_op jit(solution)/shard_map/ppermute | solution.py:163
  216.1 666.0 %reduce-scatter.10.cloned.1.call-start = ((), (), s32[]{:S(2)}) async-start(), calls=%async_computation.16 | async-start | bytes 2621440 | tf_op jit(solution)/shard_map/reduce_scatter | solution.py:171
  218.2 85.6 %collective-permute-start.18 = (bf16[2048,512]{1,0:T(8,128)(2,1)}, bf16[2048,512]{1,0:T(8,128)(2,1)}, u32[]{:S(2)}, u32[]{:S(2)}) collective-permute-start(bf16[2048,512]{1,0:T(8,128)(2,1)} %all-gather.15.cloned.1.call-done.refs_8_), channel_id=1, source_target_pairs={{0,2},{2,0},{4,6},{6,4},{1,3},{3,1},{5,7},{7,5},{8,10},{10,8},{12,... | collective-permute-start | bytes 6291464 | tf_op jit(solution)/shard_map/ppermute | solution.py:163
  233.9 116.5 %collective-permute-start.20 = (bf16[2048,512]{1,0:T(8,128)(2,1)}, bf16[2048,512]{1,0:T(8,128)(2,1)}, u32[]{:S(2)}, u32[]{:S(2)}) collective-permute-start(bf16[2048,512]{1,0:T(8,128)(2,1)} %collective-permute-done.19.refs_10_), channel_id=1, source_target_pairs={{0,2},{2,0},{4,6},{6,4},{1,3},{3,1},{5,7},{7,5},{8,10},{10,8},{12,... | collective-permute-start | bytes 6291464 | tf_op jit(solution)/shard_map/ppermute | solution.py:163
  233.9 116.5 %collective-permute-start.21 = (bf16[2048,512]{1,0:T(8,128)(2,1)}, bf16[2048,512]{1,0:T(8,128)(2,1)}, u32[]{:S(2)}, u32[]{:S(2)}) collective-permute-start(bf16[2048,512]{1,0:T(8,128)(2,1)} %all-gather.17.cloned.1.call-done.refs_12_), channel_id=1, source_target_pairs={{0,2},{2,0},{4,6},{6,4},{1,3},{3,1},{5,7},{7,5},{8,10},{10,8},{12,... | collective-permute-start | bytes 6291464 | tf_op jit(solution)/shard_map/ppermute | solution.py:163
  234.4 48.8 %collective-permute-start.22 = (bf16[2048,512]{1,0:T(8,128)(2,1)}, bf16[2048,512]{1,0:T(8,128)(2,1)}, u32[]{:S(2)}, u32[]{:S(2)}) collective-permute-start(bf16[2048,512]{1,0:T(8,128)(2,1)} %all-gather.17.cloned.1.call-done.refs_12_), channel_id=1, source_target_pairs={{0,4},{2,6},{4,0},{6,2},{1,5},{3,7},{5,1},{7,3},{8,12},{10,14},{12... | collective-permute-start | bytes 6291464 | tf_op jit(solution)/shard_map/ppermute | solution.py:163
  274.3 76.6 %collective-permute-start.25 = (bf16[2048,512]{1,0:T(8,128)(2,1)}, bf16[2048,512]{1,0:T(8,128)(2,1)}, u32[]{:S(2)}, u32[]{:S(2)}) collective-permute-start(bf16[2048,512]{1,0:T(8,128)(2,1)} %all-gather.19.cloned.1.call-done.refs_8_), channel_id=1, source_target_pairs={{0,4},{2,6},{4,0},{6,2},{1,5},{3,7},{5,1},{7,3},{8,12},{10,14},{12... | collective-permute-start | bytes 6291464 | tf_op jit(solution)/shard_map/ppermute | solution.py:163
  283.2 85.5 %collective-permute-start.23 = (bf16[2048,512]{1,0:T(8,128)(2,1)}, bf16[2048,512]{1,0:T(8,128)(2,1)}, u32[]{:S(2)}, u32[]{:S(2)}) collective-permute-start(bf16[2048,512]{1,0:T(8,128)(2,1)} %collective-permute-done.22.refs_14_), channel_id=1, source_target_pairs={{0,2},{2,0},{4,6},{6,4},{1,3},{3,1},{5,7},{7,5},{8,10},{10,8},{12,... | collective-permute-start | bytes 6291464 | tf_op jit(solution)/shard_map/ppermute | solution.py:163
  303.8 69.4 %collective-permute-start.27 = (bf16[2048,512]{1,0:T(8,128)(2,1)}, bf16[2048,512]{1,0:T(8,128)(2,1)}, u32[]{:S(2)}, u32[]{:S(2)}) collective-permute-start(bf16[2048,512]{1,0:T(8,128)(2,1)} %all-gather.21.cloned.1.call-done.refs_12_), channel_id=1, source_target_pairs={{0,2},{2,0},{4,6},{6,4},{1,3},{3,1},{5,7},{7,5},{8,10},{10,8},{12,... | collective-permute-start | bytes 6291464 | tf_op jit(solution)/shard_map/ppermute | solution.py:163
  388.4 48.4 %collective-permute-start.29 = (bf16[512,2048]{1,0:T(8,128)(2,1)}, bf16[512,2048]{1,0:T(8,128)(2,1)}, u32[]{:S(2)}, u32[]{:S(2)}) collective-permute-start(bf16[512,2048]{1,0:T(8,128)(2,1)} %sum_products.5), channel_id=1, source_target_pairs={{0,1},{1,0},{2,3},{3,2},{4,5},{5,4},{6,7},{7,6},{8,9},{9,8},{10,11... | collective-permute-start | bytes 6291464 | tf_op jit(solution)/shard_map/ppermute | solution.py:163
  486.8 45.6 %collective-permute-start.38 = (bf16[2048,512]{1,0:T(8,128)(2,1)}, bf16[2048,512]{1,0:T(8,128)(2,1)}, u32[]{:S(2)}, u32[]{:S(2)}) collective-permute-start(bf16[2048,512]{1,0:T(8,128)(2,1)} %convolution_convert_fusion.8), channel_id=1, source_target_pairs={{0,2},{2,0},{4,6},{6,4},{1,3},{3,1},{5,7},{7,5},{8,10},{10,8},{12,... | collective-permute-start | bytes 6291464 | tf_op jit(solution)/shard_map/ppermute | solution.py:163
  524.8 48.4 %collective-permute-start.34 = (bf16[512,2048]{1,0:T(8,128)(2,1)}, bf16[512,2048]{1,0:T(8,128)(2,1)}, u32[]{:S(2)}, u32[]{:S(2)}) collective-permute-start(bf16[512,2048]{1,0:T(8,128)(2,1)} %sum_products.6), channel_id=1, source_target_pairs={{0,1},{1,0},{2,3},{3,2},{4,5},{5,4},{6,7},{7,6},{8,9},{9,8},{10,11... | collective-permute-start | bytes 6291464 | tf_op jit(solution)/shard_map/ppermute | solution.py:163
  529.5 54.5 %collective-permute-start.37 = (bf16[2048,512]{1,0:T(8,128)(2,1)S(1)}, bf16[2048,512]{1,0:T(8,128)(2,1)S(1)}, u32[]{:S(2)}, u32[]{:S(2)}) collective-permute-start(bf16[2048,512]{1,0:T(8,128)(2,1)S(1)} %convolution_convert_fusion.10), channel_id=1, source_target_pairs={{0,2},{2,0},{4,6},{6,4},{1,3},{3,1},{5,7},{7,5},{8,10},{10,8},{12,... | collective-permute-start | bytes 6291464 | tf_op jit(solution)/shard_map/ppermute | solution.py:163
  535.2 48.8 %collective-permute-start.39 = (bf16[2048,512]{1,0:T(8,128)(2,1)S(1)}, bf16[2048,512]{1,0:T(8,128)(2,1)S(1)}, u32[]{:S(2)}, u32[]{:S(2)}) collective-permute-start(bf16[2048,512]{1,0:T(8,128)(2,1)S(1)} %add_convert_fusion.6), channel_id=1, source_target_pairs={{0,4},{2,6},{4,0},{6,2},{1,5},{3,7},{5,1},{7,3},{8,12},{10,14},{12... | collective-permute-start | bytes 6291464 | tf_op jit(solution)/shard_map/ppermute | solution.py:163
  586.3 295.9 %reduce-scatter.14.cloned.1.call-start = ((), (), s32[]{:S(2)}) async-start(), calls=%async_computation.18 | async-start | bytes 2621440 | tf_op jit(solution)/shard_map/reduce_scatter | solution.py:171
  596.5 285.7 %reduce-scatter.12.cloned.1.call-start = ((), (), s32[]{:S(2)}) async-start(), calls=%async_computation.17 | async-start | bytes 2621440 | tf_op jit(solution)/shard_map/reduce_scatter | solution.py:171
  606.7 275.5 %reduce-scatter.16.cloned.1.call-start = ((), (), s32[]{:S(2)}) async-start(), calls=%async_computation.19 | async-start | bytes 2621440 | tf_op jit(solution)/shard_map/reduce_scatter | solution.py:171
  606.8 47.9 %collective-permute-start.84 = (bf16[2048,512]{1,0:T(8,128)(2,1)}, bf16[2048,512]{1,0:T(8,128)(2,1)S(1)}, u32[]{:S(2)}, u32[]{:S(2)}) collective-permute-start(bf16[2048,512]{1,0:T(8,128)(2,1)} %add_convert_fusion.8), channel_id=1, source_target_pairs={{0,4},{2,6},{4,0},{6,2},{1,5},{3,7},{5,1},{7,3},{8,12},{10,14},{12... | collective-permute-start | bytes 6291464 | tf_op jit(solution)/shard_map/ppermute | solution.py:163
  658.2 224.0 %reduce-scatter.20.cloned.1.call-start = ((), (), s32[]{:S(2)}) async-start(), calls=%async_computation.21 | async-start | bytes 2621440 | tf_op jit(solution)/shard_map/reduce_scatter | solution.py:171
  659.0 223.3 %reduce-scatter.18.cloned.1.call-start = ((), (), s32[]{:S(2)}) async-start(), calls=%async_computation.20 | async-start | bytes 2621440 | tf_op jit(solution)/shard_map/reduce_scatter | solution.py:171
  661.1 370.1 %reduce-scatter.8.cloned.1.call-start = ((), (), s32[]{:S(2)}) async-start(), calls=%async_computation.15 | async-start | bytes 2621440 | tf_op jit(solution)/shard_map/reduce_scatter | solution.py:171
  693.2 177.3 %collective-permute-start.54 = (bf16[2048,256]{0,1:T(8,128)(2,1)}, bf16[2048,256]{0,1:T(8,128)(2,1)}, u32[]{:S(2)}, u32[]{:S(2)}) collective-permute-start(bf16[2048,256]{0,1:T(8,128)(2,1)} %fusion.35), channel_id=1, source_target_pairs={{0,2},{2,0},{4,6},{6,4},{1,3},{3,1},{5,7},{7,5},{8,10},{10,8},{12,... | collective-permute-start | bytes 3145736 | tf_op jit(solution)/shard_map/ppermute | solution.py:163
  699.5 55.7 %collective-permute-start.66 = (bf16[2048,256]{0,1:T(8,128)(2,1)}, bf16[2048,256]{0,1:T(8,128)(2,1)}, u32[]{:S(2)}, u32[]{:S(2)}) collective-permute-start(bf16[2048,256]{0,1:T(8,128)(2,1)} %convolution_convert_fusion.22), channel_id=1, source_target_pairs={{0,2},{2,0},{4,6},{6,4},{1,3},{3,1},{5,7},{7,5},{8,10},{10,8},{12,... | collective-permute-start | bytes 3145736 | tf_op jit(solution)/shard_map/ppermute | solution.py:163
  736.8 45.0 %collective-permute-start.51 = (bf16[2048,512]{0,1:T(8,128)(2,1)}, bf16[2048,512]{0,1:T(8,128)(2,1)}, u32[]{:S(2)}, u32[]{:S(2)}) collective-permute-start(bf16[2048,512]{0,1:T(8,128)(2,1)} %fusion.14), channel_id=1, source_target_pairs={{0,2},{2,0},{4,6},{6,4},{1,3},{3,1},{5,7},{7,5},{8,10},{10,8},{12,... | collective-permute-start | bytes 6291464 | tf_op jit(solution)/shard_map/ppermute | solution.py:163
  781.8 68.1 %collective-permute-start.48 = (bf16[2048,512]{0,1:T(8,128)(2,1)}, bf16[2048,512]{0,1:T(8,128)(2,1)}, u32[]{:S(2)}, u32[]{:S(2)}) collective-permute-start(bf16[2048,512]{0,1:T(8,128)(2,1)} %fusion.13), channel_id=1, source_target_pairs={{0,2},{2,0},{4,6},{6,4},{1,3},{3,1},{5,7},{7,5},{8,10},{10,8},{12,... | collective-permute-start | bytes 6291464 | tf_op jit(solution)/shard_map/ppermute | solution.py:163
  786.0 68.1 %collective-permute-start.52 = (bf16[2048,512]{0,1:T(8,128)(2,1)}, bf16[2048,512]{0,1:T(8,128)(2,1)}, u32[]{:S(2)}, u32[]{:S(2)}) collective-permute-start(bf16[2048,512]{0,1:T(8,128)(2,1)} %fusion.9), channel_id=1, source_target_pairs={{0,4},{2,6},{4,0},{6,2},{1,5},{3,7},{5,1},{7,3},{8,12},{10,14},{12... | collective-permute-start | bytes 6291464 | tf_op jit(solution)/shard_map/ppermute | solution.py:163
  787.8 57.7 %collective-permute-start.42 = (bf16[512,512]{1,0:T(8,128)(2,1)S(1)}, bf16[512,512]{1,0:T(8,128)(2,1)S(1)}, u32[]{:S(2)}, u32[]{:S(2)}) collective-permute-start(bf16[512,512]{1,0:T(8,128)(2,1)S(1)} %fusion.105), channel_id=1, source_target_pairs={{0,4},{2,6},{4,0},{6,2},{1,5},{3,7},{5,1},{7,3},{8,12},{10,14},{12... | collective-permute-start | bytes 1572872 | tf_op jit(solution)/shard_map/ppermute | solution.py:163
  789.4 86.8 %collective-permute-start.69 = (bf16[512,256]{0,1:T(8,128)(2,1)}, bf16[512,256]{0,1:T(8,128)(2,1)}, u32[]{:S(2)}, u32[]{:S(2)}) collective-permute-start(bf16[512,256]{0,1:T(8,128)(2,1)} %get-tuple-element.212), channel_id=1, source_target_pairs={{0,8},{8,16},{16,24},{24,0},{1,9},{9,17},{17,25},{25,1},{2,10},{10... | collective-permute-start | bytes 786440 | tf_op jit(solution)/shard_map/ppermute | solution.py:183
  880.8 48.7 %collective-permute-start.72 = (bf16[512,256]{0,1:T(8,128)(2,1)S(1)}, bf16[512,256]{0,1:T(8,128)(2,1)}, u32[]{:S(2)}, u32[]{:S(2)}) collective-permute-start(bf16[512,256]{0,1:T(8,128)(2,1)S(1)} %add_convert_fusion.33), channel_id=1, source_target_pairs={{0,4},{2,6},{4,0},{6,2},{1,5},{3,7},{5,1},{7,3},{8,12},{10,14},{12... | collective-permute-start | bytes 786440 | tf_op jit(solution)/shard_map/ppermute | solution.py:163
  905.1 88.6 %collective-permute-start.75 = (bf16[512,512]{1,0:T(8,128)(2,1)S(1)}, bf16[512,512]{1,0:T(8,128)(2,1)}, u32[]{:S(2)}, u32[]{:S(2)}) collective-permute-start(bf16[512,512]{1,0:T(8,128)(2,1)S(1)} %copy-done.14), channel_id=1, source_target_pairs={{0,4},{2,6},{4,0},{6,2},{1,5},{3,7},{5,1},{7,3},{8,12},{10,14},{12... | collective-permute-start | bytes 1572872 | tf_op jit(solution)/shard_map/ppermute | solution.py:163
  913.6 91.5 %collective-permute-start.77 = (bf16[512,512]{1,0:T(8,128)(2,1)S(1)}, bf16[512,512]{1,0:T(8,128)(2,1)}, u32[]{:S(2)}, u32[]{:S(2)}) collective-permute-start(bf16[512,512]{1,0:T(8,128)(2,1)S(1)} %copy-done.14), channel_id=1, source_target_pairs={{0,2},{2,0},{4,6},{6,4},{1,3},{3,1},{5,7},{7,5},{8,10},{10,8},{12,... | collective-permute-start | bytes 1572872 | tf_op jit(solution)/shard_map/ppermute | solution.py:163
  939.3 69.1 %collective-permute-start.85 = (bf16[512,512]{1,0:T(8,128)(2,1)S(1)}, bf16[512,512]{1,0:T(8,128)(2,1)}, u32[]{:S(2)}, u32[]{:S(2)}) collective-permute-start(bf16[512,512]{1,0:T(8,128)(2,1)S(1)} %copy-done.15), channel_id=1, source_target_pairs={{0,4},{2,6},{4,0},{6,2},{1,5},{3,7},{5,1},{7,3},{8,12},{10,14},{12... | collective-permute-start | bytes 1572872 | tf_op jit(solution)/shard_map/ppermute | solution.py:163
  1005.5 47.9 %collective-permute-start.53 = (bf16[512,2048]{1,0:T(8,128)(2,1)}, bf16[512,2048]{1,0:T(8,128)(2,1)}, u32[]{:S(2)}, u32[]{:S(2)}) collective-permute-start(bf16[512,2048]{1,0:T(8,128)(2,1)} %sum_products.7), channel_id=1, source_target_pairs={{0,1},{1,0},{2,3},{3,2},{4,5},{5,4},{6,7},{7,6},{8,9},{9,8},{10,11... | collective-permute-start | bytes 6291464 | tf_op jit(solution)/shard_map/ppermute | solution.py:163
  (166 other events, 2278.5 us)
Sparse Core Ops, SparseCore 0:
  10.1 48.3 all-gather.10
  60.7 26.7 all-gather.8
  89.7 27.3 all-gather.12
  119.1 45.0 all-gather.14
  166.1 44.4 all-gather.16
  212.6 44.4 all-gather.18
  259.3 44.4 all-gather.20
  305.9 44.4 all-gather.22
  586.4 42.4 reduce-scatter.9
  631.6 42.8 reduce-scatter.13
  677.3 42.8 reduce-scatter.11
  722.9 42.8 reduce-scatter.15
  768.0 48.4 reduce-scatter.19
  818.6 49.7 reduce-scatter.17
  882.2 52.0 reduce-scatter.7
where the time goes:
time: 1080 us; the launch traced here: 1070 us
  waiting for transfers between devices  539 us (50%)
  matrix products  181 us (17%)
  Pallas kernels  113 us (10%)
  other arithmetic  107 us (10%)
  starting transfers between devices  77.6 us (7%)
  local copies, waits for them, and re-layouts  37.4 us (3%)
  between operations  16.1 us (1%)
    ppermute x90, waiting for transfers between devices, across(): return lax.ppermute(array, axis, [(at, at ^ step) for at in range(size)])  451 us
    dot_general x28, matrix products, product(): return jnp.dot(left, right, preferred_element_type=F32)  106 us
    all_gather x8, waiting for transfers between devices, collect(): return lax.all_gather(piece, 'shard', axis=0, tiled=True)  77.7 us
    dot_general x28, matrix products, transposed_times(): lax.dot_general(left, right, (((0,), (0,)), ((), ())), preferred_element_...  75.5 us
    ppermute x90, starting transfers between devices, across(): return lax.ppermute(array, axis, [(at, at ^ step) for at in range(size)])  70 us
    pallas_call x4, Pallas kernels, sum_products(): pl.pallas_call(sum_kernel, grid=(width // block,), in_specs=[pl.BlockSpec...  52.3 us
    pallas_call x4, Pallas kernels, attention_back(): pl.pallas_call(backward_kernel, grid=(heads, rows // block), in_specs=[ro...  35.2 us
    pallas_call x4, Pallas kernels, attention(): pl.pallas_call(forward_kernel, grid=(heads, rows // block), in_specs=[row...  25.8 us
  transfers between devices with their start and end apart: 111, of which 31 were waited for; matrix products, arithmetic and copies ran while one was open for 26% of the time, Pallas kernels for 9%

commit v1 on v0

--- a/solution.py
+++ b/solution.py
@@ -209,6 +209,11 @@
     if hold:
         got = after(got, *hold)
     return (own.astype(F32) + got.astype(F32)).astype(BF)
+
+
+def halves(array):
+    width = array.shape[1] // 2
+    return [array[:, :width], array[:, width:]]
 
 
 def join_pair(own, far):
@@ -291,15 +296,20 @@
     heads_here = 4 * heads_each
     ff_half = up_weight.shape[1] // 8
     kv_own = collect(jnp.concatenate([own_columns(key_weight), own_columns(value_weight)], axis=1))
-    query_own = collect(own_columns(query_weight))
-    output_own = collect(own_columns(output_weight))
+    pair_own = collect(
+        jnp.concatenate([own_columns(query_weight), own_columns(output_weight)], axis=1)
+    )
     up_piece = own_columns(up_weight)
     down_piece = own_columns(down_weight)
     up_own = [collect(up_piece[:, half * ff_half : (half + 1) * ff_half]) for half in range(2)]
     down_own = [collect(down_piece[:, half * ff_half : (half + 1) * ff_half]) for half in range(2)]
-    down_far = collect(own_columns(down_weight, 2)[:, ff_half:])
+    ff_part = ff_half // 2
+    down_far = collect(own_columns(down_weight, 2)[:, ff_half + ff_part :])
     key_value_w = fill(kv_own, across(after(kv_own, tokens_far), 2))
-    query_w = spread(query_own)
+    pair_far = after(across(pair_own, 2), kv_own)
+    pair_w = fill(pair_own, pair_far)
+    query_w = [item[:, :kv_width] for item in pair_w]
+    output_w = [item[:, kv_width:] for item in pair_w]
 
     tokens_two = jnp.concatenate([tokens, tokens_far], axis=0)
     zero_row = jnp.zeros((kv_width,), F32)
@@ -309,7 +319,6 @@
         ).astype(BF)
         for q in range(4)
     ]
-    output_w = spread(after(output_own, kv_here[3]))
     kv_near = [across(kv_here[q ^ 1], 1) for q in range(4)]
     queries = [(product(tokens, query_w[q]) + qv_vector[0, q]).astype(BF) for q in range(4)]
     attended, logsums = [], []
@@ -329,9 +338,11 @@
     up_rows = up_vector.reshape(4, 2, ff_half)
     pre_act = [product(hidden_low, up_w[half][q]) + up_rows[q, half] for half, q in pairs]
     activated = [gelu_tanh(item).astype(BF) for item in pre_act]
+    down_swapped = across(after(down_own[1], *activated)[:, :ff_part], 2)
+    down_last = jnp.concatenate([down_swapped, after(down_far, *activated)], axis=1)
     down_w = [
         spread(after(down_own[0], activated[0])),
-        fill(down_own[1], down_far),
+        fill(down_own[1], down_last),
     ]
     mlp_low = sum_products(activated, [down_w[half][q] for half, q in pairs])
     mlp_branch = tp_sum(mlp_low) + biases[2]
@@ -343,19 +354,24 @@
     down_parts = [transposed_times(grad_mlp, item).astype(BF) for item in activated]
     down_late = near_sums(down_parts[4:8])
     down_early = near_sums(down_parts[0:4])
-    grad_mlp_then = after(grad_mlp, *down_late, *down_early)
-    down_second = [scatter(item) for item in down_late]
+    down_late = jnp.concatenate(down_late, axis=1)
+    grad_mlp_then = after(grad_mlp, down_late, *down_early)
+    down_second = scatter(down_late)
     grad_pre = []
     for at, (half, q) in enumerate(pairs):
         _, gelu_pull = jax.vjp(gelu_tanh, pre_act[at])
         grad_pre.append(gelu_pull(product(grad_mlp_then, down_w[half][q]))[0].astype(BF))
     hidden_part = sum_products(grad_pre, [up_w[half][q] for half, q in pairs])
-    down_first = scatter(far_sum(*down_early, hidden_part))
-    grad_hidden = grad_second + tp_sum(hidden_part)
+    down_total = far_sum(*down_early, hidden_part)
+    down_first = scatter(down_total)
     up_parts = [transposed_times(hidden_low, item).astype(BF) for item in grad_pre]
-    up_late = near_sums(up_parts[4:8])
-    up_second = [scatter(item) for item in up_late]
     up_early = near_sums(up_parts[0:4])
+    up_late = jnp.concatenate(near_sums(up_parts[4:8]), axis=1)
+    up_second = scatter(up_late)
+    hidden_got = after(across(hidden_part, 1, "tp"), down_total, up_late, *up_early)
+    grad_hidden = grad_second + (hidden_part.astype(F32) + hidden_got.astype(F32))
+    down_second = halves(down_second)
+    down_pair = [far_sum(*down_second), far_sum(*down_second[::-1])]
     grad_first = norm_backward(grad_hidden * gains[0], normed_one, factor_one)
     grad_branch = grad_first.astype(BF)
     grad_attended = [product(grad_branch, output_w[q]).astype(BF) for q in range(4)]
@@ -365,6 +381,7 @@
         [transposed_times(grad_branch, attended[q]).astype(BF) for q in range(4)]
     )
     grad_attended[2:] = lax.optimization_barrier((*grad_attended[2:], up_total))[:-1]
+    down_far_first = across(down_first, 2)
     grad_q, here_parts, near_parts = [], [], []
     for q in range(4):
         dq, dk_here, dk_near, dv_here, dv_near = attention_back(
@@ -390,19 +407,16 @@
     ]
     output_direct = scatter_direct(far_sum(*output_early, *grad_q))
     query_early = near_sums([transposed_times(tokens, grad_q[q]).astype(BF) for q in range(4)])
-    kv_total = far_sum(
-        *near_sums([transposed_times(tokens, grad_kv[q]).astype(BF) for q in range(4)])
-    )
+    kv_parts = [transposed_times(tokens, grad_kv[q]).astype(BF) for q in range(4)]
+    kv_total = far_sum(*near_sums(kv_parts))
     kv_mine = scatter(kv_total)
     query_mine, query_got = scatter_direct(far_sum(*query_early, kv_total))
     output_mine, output_got = lax.optimization_barrier((*output_direct, kv_total))[:2]
-    down_first, up_first, grad_q_then = (
-        after(item, kv_total) for item in (down_first, up_first, grad_q[0])
-    )
-    down_second = [after(item, kv_total) for item in down_second]
-    up_second = [after(item, kv_total) for item in up_second]
-    down_grads = [spread(down_first), join_pair(*down_second)]
-    up_grads = [spread(up_first), join_pair(*up_second)]
+    up_first, up_second, grad_q_then = (
+        after(item, kv_total) for item in (up_first, up_second, grad_q[0])
+    )
+    down_grads = [fill(down_first, down_far_first), fill(*down_pair)]
+    up_grads = [spread(up_first), join_pair(*halves(up_second))]
     output_grads = spread(sum_direct(output_mine, output_got))
     query_grads = spread(sum_direct(query_mine, query_got))
     kv_grads = spread(kv_mine)

time: 1080 us -> 990 us (0.917)
  waiting for transfers between devices: 539 us -> 428 us
  local copies, waits for them, and re-layouts: 37.4 us -> 69 us
  other arithmetic: 107 us -> 121 us
  starting transfers between devices: 77.6 us -> 65 us
  matrix products: 181 us -> 169 us
    ppermute x90 -> x88, waiting for transfers between devices: 451 us -> 342 us  [across(): return lax.ppermute(array, axis, [(at, at ^ step) for at in range(size)])]
    slice x1 -> x9, local copies, waits for them, and re-layouts: 2.57 us -> 22.8 us  [the longest x4 12 us: shards(): query_w = [item[:, :kv_width] for item in pair_w]]
    ppermute x90 -> x88, starting transfers between devices: 70 us -> 56 us  [across(): return lax.ppermute(array, axis, [(at, at ^ step) for at in range(size)])]
    unnamed x217 -> x210, local copies, waits for them, and re-layouts: 19.6 us -> 32.1 us
    dot_general x28, matrix products: 75.5 us -> 63.3 us  [transposed_times(): lax.dot_general(left, right, (((0,), (0,)), ((), ())), preferred_element_...]
    convert_element_type x2 -> x0, other arithmetic: 11.3 us -> none  [whole_halves(): return jnp.concatenate([placed[half][q] for q in range(4) for half in ran...]
    all_gather x8 -> x7, waiting for transfers between devices: 77.7 us -> 73.8 us  [collect(): return lax.all_gather(piece, 'shard', axis=0, tiled=True)]
  transfers between devices with their start and end apart: 111 -> 106, of which waited for: 31 -> 29; matrix products, arithmetic and copies ran while one was open for 26% -> 33% of each run, Pallas kernels for 9% -> 10%
where the time goes in v1:
time: 990 us; the launch traced here: 980 us
  waiting for transfers between devices  428 us (43%)
  matrix products  169 us (17%)
  other arithmetic  121 us (12%)
  Pallas kernels  112 us (11%)
  local copies, waits for them, and re-layouts  69 us (7%)
  starting transfers between devices  65 us (7%)
  between operations  16.3 us (2%)
    ppermute x88, waiting for transfers between devices, across(): return lax.ppermute(array, axis, [(at, at ^ step) for at in range(size)])  342 us
    dot_general x28, matrix products, product(): return jnp.dot(left, right, preferred_element_type=F32)  105 us
    all_gather x7, waiting for transfers between devices, collect(): return lax.all_gather(piece, 'shard', axis=0, tiled=True)  73.8 us
    dot_general x28, matrix products, transposed_times(): lax.dot_general(left, right, (((0,), (0,)), ((), ())), preferred_element_...  63.3 us
    ppermute x88, starting transfers between devices, across(): return lax.ppermute(array, axis, [(at, at ^ step) for at in range(size)])  56 us
    pallas_call x4, Pallas kernels, sum_products(): pl.pallas_call(sum_kernel, grid=(width // block,), in_specs=[pl.BlockSpec...  51.7 us
    pallas_call x4, Pallas kernels, attention_back(): pl.pallas_call(backward_kernel, grid=(heads, rows // block), in_specs=[ro...  34.7 us
    unnamed x210, local copies, waits for them, and re-layouts  32.1 us
  transfers between devices with their start and end apart: 106, of which 29 were waited for; matrix products, arithmetic and copies ran while one was open for 33% of the time, Pallas kernels for 10%

profile of v1, /device:TPU:0, one launch (start us, length us, event | category | flops | bytes accessed | tf_op | source)
XLA Modules:
  0.0 980.3 jit_solution(18125201854800502510)
XLA Ops:
  26.1 6.5 collective-permute-done.1
  33.8 7.7 collective-permute-done.2
  41.5 23.7 %collective-permute-done.3 = bf16[512,2048]{1,0:T(8,128)(2,1)} collective-permute-done((bf16[512,2048]{1,0:T(8,128)(2,1)S(1)}, bf16[512,2048]{1,0:T(8,128)(2,1)}, u32[]{:S(2)}, u32[]{:S(2)}) %collective-permute-start.3) | collective-permute-done | bytes 2097184 | tf_op jit(solution)/shard_map/ppermute | solution.py:163
  67.9 39.4 %all-gather.8.cloned.1.call-done = bf16[2048,512]{1,0:T(8,128)(2,1)} async-done(((bf16[512,512]{1,0:T(8,128)(2,1)}), bf16[2048,512]{1,0:T(8,128)(2,1)}) %all-gather.8.cloned.1.call-update) | async-done | bytes 2097168 | tf_op jit(solution)/shard_map/all_gather | solution.py:167
  108.8 5.6 add_convert_fusion.16.kh_ref.vh_ref
  120.6 4.6 add_convert_fusion.14.kh_ref.vh_ref
  125.2 28.8 %all-gather.12.cloned.1.call-done.refs_8_ = bf16[2048,512]{1,0:T(8,128)(2,1)} async-done(((bf16[512,512]{1,0:T(8,128)(2,1)}), bf16[2048,512]{1,0:T(8,128)(2,1)}) %all-gather.12.cloned.1.call-update) | async-done | bytes 2097168 | tf_op jit(solution)/shard_map/all_gather | solution.py:167
  158.8 5.5 add_convert_fusion.15.kh_ref.vh_ref
  173.5 6.6 attention_forward.5
  180.1 5.5 add_convert_fusion.13.kh_ref.vh_ref
  188.8 6.4 attention_forward.4
  197.9 6.4 attention_forward.7
  207.9 6.4 attention_forward.6
  214.3 8.3 sum_products.4
  228.6 23.7 %collective-permute-done.19.refs_14_ = bf16[2048,512]{1,0:T(8,128)(2,1)} collective-permute-done((bf16[2048,512]{1,0:T(8,128)(2,1)}, bf16[2048,512]{1,0:T(8,128)(2,1)}, u32[]{:S(2)}, u32[]{:S(2)}) %collective-permute-start.19) | collective-permute-done | bytes 2097184 | tf_op jit(solution)/shard_map/ppermute | solution.py:163
  252.3 18.0 %collective-permute-done.14 = bf16[512,2048]{1,0:T(8,128)(2,1)} collective-permute-done((bf16[512,2048]{1,0:T(8,128)(2,1)}, bf16[512,2048]{1,0:T(8,128)(2,1)}, u32[]{:S(2)}, u32[]{:S(2)}) %collective-permute-start.14) | collective-permute-done | bytes 2097184 | tf_op jit(solution)/shard_map/ppermute | solution.py:163
  270.3 4.9 fusion.145
  308.2 4.5 multiply_convert_fusion
  316.1 5.7 all-gather.20.cloned.1.call-done
  321.8 28.8 %collective-permute-done.25 = bf16[2048,256]{1,0:T(8,128)(2,1)S(1)} collective-permute-done((bf16[2048,256]{1,0:T(8,128)(2,1)}, bf16[2048,256]{1,0:T(8,128)(2,1)S(1)}, u32[]{:S(2)}, u32[]{:S(2)}) %collective-permute-start.25) | collective-permute-done | bytes 1048608 | tf_op jit(solution)/shard_map/ppermute | solution.py:163
  358.4 15.2 %sum_products.5 = bf16[512,2048]{1,0:T(8,128)(2,1)} custom-call(bf16[512,512]{1,0:T(8,128)(2,1)} %get-tuple-element.270.refs_0_, bf16[512,512]{1,0:T(8,128)(2,1)} %get-tuple-element.272.refs_1_, bf16[512,512]{1,0:T(8,128)(2,1)} %get-tuple-element.274.refs_2_, bf16[512,512]{1,0:T(8,128)(2,1)} %get-tuple-element.276.refs_3_, ...), custom_call_target="tpu_custom_call" | custom-call | tf_op jit(solution)/shard_map/sum_products/pallas_call | solution.py:146
  375.2 46.3 %collective-permute-done.27 = bf16[512,2048]{1,0:T(8,128)(2,1)S(1)} collective-permute-done((bf16[512,2048]{1,0:T(8,128)(2,1)}, bf16[512,2048]{1,0:T(8,128)(2,1)S(1)}, u32[]{:S(2)}, u32[]{:S(2)}) %collective-permute-start.27) | collective-permute-done | bytes 2097184 | tf_op jit(solution)/shard_map/ppermute | solution.py:163
  421.5 4.8 fusion.143
  452.2 5.0 add_convert_fusion.9
  471.5 4.4 convert_reduce_fusion.4
  487.1 15.2 %sum_products.6 = bf16[512,2048]{1,0:T(8,128)(2,1)} custom-call(bf16[512,512]{1,0:T(8,128)(2,1)} %get-tuple-element.168.refs_0_, bf16[512,512]{1,0:T(8,128)(2,1)} %get-tuple-element.172.refs_1_, bf16[512,512]{1,0:T(8,128)(2,1)} %get-tuple-element.176.refs_2_, bf16[512,512]{1,0:T(8,128)(2,1)} %get-tuple-element.180.refs_3_, ...), custom_call_target="tpu_custom_call" | custom-call | tf_op jit(solution)/shard_map/sum_products/pallas_call | solution.py:146
  502.3 4.4 add_convert_fusion.7
  535.9 19.5 %collective-permute-done.32 = bf16[512,2048]{1,0:T(8,128)(2,1)} collective-permute-done((bf16[512,2048]{1,0:T(8,128)(2,1)}, bf16[512,2048]{1,0:T(8,128)(2,1)}, u32[]{:S(2)}, u32[]{:S(2)}) %collective-permute-start.32) | collective-permute-done | bytes 2097184 | tf_op jit(solution)/shard_map/ppermute | solution.py:163
  555.5 7.8 multiply_reduce_fusion.3
  566.4 9.0 collective-permute-done.40
  584.6 8.6 attention_backward.4
  596.5 8.7 attention_backward.5
  631.2 8.6 attention_backward.6
  640.4 8.8 attention_backward.7
  658.4 10.3 %collective-permute-done.51 = bf16[512,512]{1,0:T(8,128)(2,1)S(1)} collective-permute-done((bf16[512,512]{1,0:T(8,128)(2,1)S(1)}, bf16[512,512]{1,0:T(8,128)(2,1)S(1)}, u32[]{:S(2)}, u32[]{:S(2)}) %collective-permute-start.51) | collective-permute-done | bytes 524320 | tf_op jit(solution)/shard_map/ppermute | solution.py:163
  676.3 13.9 %collective-permute-done.48 = bf16[512,512]{1,0:T(8,128)(2,1)S(1)} collective-permute-done((bf16[512,512]{1,0:T(8,128)(2,1)S(1)}, bf16[512,512]{1,0:T(8,128)(2,1)S(1)}, u32[]{:S(2)}, u32[]{:S(2)}) %collective-permute-start.48) | collective-permute-done | bytes 524320 | tf_op jit(solution)/shard_map/ppermute | solution.py:163
  698.1 9.8 %collective-permute-done.43 = bf16[512,512]{1,0:T(8,128)(2,1)S(1)} collective-permute-done((bf16[512,512]{1,0:T(8,128)(2,1)S(1)}, bf16[512,512]{1,0:T(8,128)(2,1)S(1)}, u32[]{:S(2)}, u32[]{:S(2)}) %collective-permute-start.43) | collective-permute-done | bytes 524320 | tf_op jit(solution)/shard_map/ppermute | solution.py:163
  714.9 48.7 %collective-permute-done.83 = bf16[512,512]{0,1:T(8,128)(2,1)S(1)} collective-permute-done((bf16[512,512]{0,1:T(8,128)(2,1)}, bf16[512,512]{0,1:T(8,128)(2,1)S(1)}, u32[]{:S(2)}, u32[]{:S(2)}) %collective-permute-start.83) | collective-permute-done | bytes 524320 | tf_op jit(solution)/shard_map/ppermute | solution.py:163
  785.3 14.2 %collective-permute-done.57 = bf16[2048,256]{0,1:T(8,128)(2,1)} collective-permute-done((bf16[2048,256]{0,1:T(8,128)(2,1)}, bf16[2048,256]{0,1:T(8,128)(2,1)}, u32[]{:S(2)}, u32[]{:S(2)}) %collective-permute-start.57) | collective-permute-done | bytes 1048608 | tf_op jit(solution)/shard_map/ppermute | solution.py:163
  810.1 13.1 %sum_products.7 = bf16[512,2048]{1,0:T(8,128)(2,1)} custom-call(bf16[512,256]{1,0:T(8,128)(2,1)} %get-tuple-element.102.refs_0_, bf16[512,256]{1,0:T(8,128)(2,1)} %get-tuple-element.103.refs_1_, bf16[512,256]{1,0:T(8,128)(2,1)} %get-tuple-element.104.refs_2_, bf16[512,256]{1,0:T(8,128)(2,1)} %get-tuple-element.105.refs_3_, ...), custom_call_target="tpu_custom_call" | custom-call | tf_op jit(solution)/shard_map/sum_products/pallas_call | solution.py:146
  829.9 15.1 %collective-permute-done.92 = f32[152,128]{1,0:T(8,128)S(1)} collective-permute-done((f32[152,128]{1,0:T(8,128)S(1)}, f32[152,128]{1,0:T(8,128)S(1)}, u32[]{:S(2)}, u32[]{:S(2)}) %collective-permute-start.92) | collective-permute-done | bytes 77856 | tf_op jit(solution)/shard_map/ppermute | solution.py:163
  846.4 11.2 %collective-permute-done.59 = bf16[512,256]{0,1:T(8,128)(2,1)} collective-permute-done((bf16[512,256]{0,1:T(8,128)(2,1)}, bf16[512,256]{0,1:T(8,128)(2,1)}, u32[]{:S(2)}, u32[]{:S(2)}) %collective-permute-start.59) | collective-permute-done | bytes 262176 | tf_op jit(solution)/shard_map/ppermute | solution.py:183
  860.6 5.3 collective-permute-done.93
  894.6 7.0 copy.114
  913.9 4.8 collective-permute-done.81
  919.5 10.0 %collective-permute-done.79 = bf16[512,512]{0,1:T(8,128)(2,1)} collective-permute-done((bf16[512,512]{0,1:T(8,128)(2,1)S(1)}, bf16[512,512]{0,1:T(8,128)(2,1)}, u32[]{:S(2)}, u32[]{:S(2)}) %collective-permute-start.79) | collective-permute-done | bytes 524320 | tf_op jit(solution)/shard_map/ppermute | solution.py:163
  945.1 9.2 collective-permute-done.64
  957.7 7.0 copy.113
  (630 shorter events, 371.1 us)
Async XLA Ops:
  7.2 58.1 %all-gather.10.cloned.1.call-start = ((), (), s32[]{:S(2)}) async-start(), calls=%async_computation.6 | async-start | bytes 2621440 | tf_op jit(solution)/shard_map/all_gather | solution.py:167
  9.2 98.1 %all-gather.8.cloned.1.call-start = ((), (), s32[]{:S(2)}) async-start(), calls=%async_computation.5 | async-start | bytes 2621440 | tf_op jit(solution)/shard_map/all_gather | solution.py:167
  11.2 142.8 %all-gather.12.cloned.1.call-start = ((), (), s32[]{:S(2)}) async-start(), calls=%async_computation.7 | async-start | bytes 2621440 | tf_op jit(solution)/shard_map/all_gather | solution.py:167
  13.5 190.8 %all-gather.14.cloned.1.call-start = ((), (), s32[]{:S(2)}) async-start(), calls=%async_computation.8 | async-start | bytes 2621440 | tf_op jit(solution)/shard_map/all_gather | solution.py:167
  14.1 267.3 %all-gather.16.cloned.1.call-start = ((), (), s32[]{:S(2)}) async-start(), calls=%async_computation.9 | async-start | bytes 2621440 | tf_op jit(solution)/shard_map/all_gather | solution.py:167
  16.4 296.3 %all-gather.18.cloned.1.call-start = ((), (), s32[]{:S(2)}) async-start(), calls=%async_computation.10 | async-start | bytes 2621440 | tf_op jit(solution)/shard_map/all_gather | solution.py:167
  16.5 48.8 %collective-permute-start.3 = (bf16[512,2048]{1,0:T(8,128)(2,1)S(1)}, bf16[512,2048]{1,0:T(8,128)(2,1)}, u32[]{:S(2)}, u32[]{:S(2)}) collective-permute-start(bf16[512,2048]{1,0:T(8,128)(2,1)S(1)} %bitcast.266), channel_id=1, source_target_pairs={{0,4},{2,6},{4,0},{6,2},{1,5},{3,7},{5,1},{7,3},{8,12},{10,14},{12... | collective-permute-start | bytes 6291464 | tf_op jit(solution)/shard_map/ppermute | solution.py:163
  21.7 300.1 %all-gather.20.cloned.1.call-start = ((), (), s32[]{:S(2)}) async-start(), calls=%async_computation.11 | async-start | bytes 1310720 | tf_op jit(solution)/shard_map/all_gather | solution.py:167
  65.2 55.4 %collective-permute-start.9 = (bf16[2048,512]{1,0:T(8,128)(2,1)}, bf16[2048,512]{1,0:T(8,128)(2,1)}, u32[]{:S(2)}, u32[]{:S(2)}) collective-permute-start(bf16[2048,512]{1,0:T(8,128)(2,1)} %all-gather.10.cloned.1.call-done.refs_12_), channel_id=1, source_target_pairs={{0,4},{2,6},{4,0},{6,2},{1,5},{3,7},{5,1},{7,3},{8,12},{10,14},{12... | collective-permute-start | bytes 6291464 | tf_op jit(solution)/shard_map/ppermute | solution.py:163
  67.9 90.9 %collective-permute-start.4 = (bf16[2048,512]{1,0:T(8,128)(2,1)}, bf16[2048,512]{1,0:T(8,128)(2,1)}, u32[]{:S(2)}, u32[]{:S(2)}) collective-permute-start(bf16[2048,512]{1,0:T(8,128)(2,1)} %all-gather.10.cloned.1.call-done.refs_12_), channel_id=1, source_target_pairs={{0,2},{2,0},{4,6},{6,4},{1,3},{3,1},{5,7},{7,5},{8,10},{10,8},{12,... | collective-permute-start | bytes 6291464 | tf_op jit(solution)/shard_map/ppermute | solution.py:163
  107.3 50.0 %collective-permute-start.8 = (bf16[2048,512]{1,0:T(8,128)(2,1)}, bf16[2048,512]{1,0:T(8,128)(2,1)}, u32[]{:S(2)}, u32[]{:S(2)}) collective-permute-start(bf16[2048,512]{1,0:T(8,128)(2,1)} %all-gather.8.cloned.1.call-done), channel_id=1, source_target_pairs={{0,4},{2,6},{4,0},{6,2},{1,5},{3,7},{5,1},{7,3},{8,12},{10,14},{12... | collective-permute-start | bytes 6291464 | tf_op jit(solution)/shard_map/ppermute | solution.py:163
  114.4 59.1 %collective-permute-start.7 = (bf16[1024,512]{1,0:T(8,128)(2,1)}, bf16[1024,512]{1,0:T(8,128)(2,1)}, u32[]{:S(2)}, u32[]{:S(2)}) collective-permute-start(bf16[1024,512]{1,0:T(8,128)(2,1)} %add_convert_fusion.16.kh_ref.vh_ref), channel_id=1, source_target_pairs={{0,2},{2,0},{4,6},{6,4},{1,3},{3,1},{5,7},{7,5},{8,10},{10,8},{12,... | collective-permute-start | bytes 3145736 | tf_op jit(solution)/shard_map/ppermute | solution.py:163
  114.4 52.9 %collective-permute-start.6 = (bf16[2048,512]{1,0:T(8,128)(2,1)}, bf16[2048,512]{1,0:T(8,128)(2,1)}, u32[]{:S(2)}, u32[]{:S(2)}) collective-permute-start(bf16[2048,512]{1,0:T(8,128)(2,1)} %all-gather.8.cloned.1.call-done), channel_id=1, source_target_pairs={{0,2},{2,0},{4,6},{6,4},{1,3},{3,1},{5,7},{7,5},{8,10},{10,8},{12,... | collective-permute-start | bytes 6291464 | tf_op jit(solution)/shard_map/ppermute | solution.py:163
  120.6 59.5 %collective-permute-start.10 = (bf16[2048,512]{1,0:T(8,128)(2,1)}, bf16[2048,512]{1,0:T(8,128)(2,1)}, u32[]{:S(2)}, u32[]{:S(2)}) collective-permute-start(bf16[2048,512]{1,0:T(8,128)(2,1)} %collective-permute-done.9.refs_14_), channel_id=1, source_target_pairs={{0,2},{2,0},{4,6},{6,4},{1,3},{3,1},{5,7},{7,5},{8,10},{10,8},{12,... | collective-permute-start | bytes 6291464 | tf_op jit(solution)/shard_map/ppermute | solution.py:163
  157.3 70.7 %collective-permute-start.16 = (bf16[2048,512]{1,0:T(8,128)(2,1)}, bf16[2048,512]{1,0:T(8,128)(2,1)}, u32[]{:S(2)}, u32[]{:S(2)}) collective-permute-start(bf16[2048,512]{1,0:T(8,128)(2,1)} %all-gather.12.cloned.1.call-done.refs_8_), channel_id=1, source_target_pairs={{0,4},{2,6},{4,0},{6,2},{1,5},{3,7},{5,1},{7,3},{8,12},{10,14},{12... | collective-permute-start | bytes 6291464 | tf_op jit(solution)/shard_map/ppermute | solution.py:163
  158.8 36.5 %collective-permute-start.12 = (bf16[2048,512]{1,0:T(8,128)(2,1)}, bf16[2048,512]{1,0:T(8,128)(2,1)}, u32[]{:S(2)}, u32[]{:S(2)}) collective-permute-start(bf16[2048,512]{1,0:T(8,128)(2,1)} %collective-permute-done.8), channel_id=1, source_target_pairs={{0,2},{2,0},{4,6},{6,4},{1,3},{3,1},{5,7},{7,5},{8,10},{10,8},{12,... | collective-permute-start | bytes 6291464 | tf_op jit(solution)/shard_map/ppermute | solution.py:163
  204.3 48.0 %collective-permute-start.19 = (bf16[2048,512]{1,0:T(8,128)(2,1)}, bf16[2048,512]{1,0:T(8,128)(2,1)}, u32[]{:S(2)}, u32[]{:S(2)}) collective-permute-start(bf16[2048,512]{1,0:T(8,128)(2,1)} %all-gather.14.cloned.1.call-done.refs_12_), channel_id=1, source_target_pairs={{0,4},{2,6},{4,0},{6,2},{1,5},{3,7},{5,1},{7,3},{8,12},{10,14},{12... | collective-permute-start | bytes 6291464 | tf_op jit(solution)/shard_map/ppermute | solution.py:163
  222.6 47.7 %collective-permute-start.14 = (bf16[512,2048]{1,0:T(8,128)(2,1)}, bf16[512,2048]{1,0:T(8,128)(2,1)}, u32[]{:S(2)}, u32[]{:S(2)}) collective-permute-start(bf16[512,2048]{1,0:T(8,128)(2,1)} %sum_products.4), channel_id=1, source_target_pairs={{0,1},{1,0},{2,3},{3,2},{4,5},{5,4},{6,7},{7,6},{8,9},{9,8},{10,11... | collective-permute-start | bytes 6291464 | tf_op jit(solution)/shard_map/ppermute | solution.py:163
  225.8 483.0 %reduce-scatter.12.cloned.1.call-start = ((), (), s32[]{:S(2)}) async-start(), calls=%async_computation.15 | async-start | bytes 2621440 | tf_op jit(solution)/shard_map/reduce_scatter | solution.py:171
  227.9 67.6 %collective-permute-start.15 = (bf16[2048,512]{1,0:T(8,128)(2,1)}, bf16[2048,512]{1,0:T(8,128)(2,1)}, u32[]{:S(2)}, u32[]{:S(2)}) collective-permute-start(bf16[2048,512]{1,0:T(8,128)(2,1)} %all-gather.12.cloned.1.call-done.refs_8_), channel_id=1, source_target_pairs={{0,2},{2,0},{4,6},{6,4},{1,3},{3,1},{5,7},{7,5},{8,10},{10,8},{12,... | collective-permute-start | bytes 6291464 | tf_op jit(solution)/shard_map/ppermute | solution.py:163
  228.0 71.7 %collective-permute-start.17 = (bf16[2048,512]{1,0:T(8,128)(2,1)}, bf16[2048,512]{1,0:T(8,128)(2,1)}, u32[]{:S(2)}, u32[]{:S(2)}) collective-permute-start(bf16[2048,512]{1,0:T(8,128)(2,1)} %collective-permute-done.16.refs_10_), channel_id=1, source_target_pairs={{0,2},{2,0},{4,6},{6,4},{1,3},{3,1},{5,7},{7,5},{8,10},{10,8},{12,... | collective-permute-start | bytes 6291464 | tf_op jit(solution)/shard_map/ppermute | solution.py:163
  228.5 75.5 %collective-permute-start.18 = (bf16[2048,512]{1,0:T(8,128)(2,1)}, bf16[2048,512]{1,0:T(8,128)(2,1)}, u32[]{:S(2)}, u32[]{:S(2)}) collective-permute-start(bf16[2048,512]{1,0:T(8,128)(2,1)} %all-gather.14.cloned.1.call-done.refs_12_), channel_id=1, source_target_pairs={{0,2},{2,0},{4,6},{6,4},{1,3},{3,1},{5,7},{7,5},{8,10},{10,8},{12,... | collective-permute-start | bytes 6291464 | tf_op jit(solution)/shard_map/ppermute | solution.py:163
  252.3 56.0 %collective-permute-start.20 = (bf16[2048,512]{1,0:T(8,128)(2,1)}, bf16[2048,512]{1,0:T(8,128)(2,1)}, u32[]{:S(2)}, u32[]{:S(2)}) collective-permute-start(bf16[2048,512]{1,0:T(8,128)(2,1)} %collective-permute-done.19.refs_14_), channel_id=1, source_target_pairs={{0,2},{2,0},{4,6},{6,4},{1,3},{3,1},{5,7},{7,5},{8,10},{10,8},{12,... | collective-permute-start | bytes 6291464 | tf_op jit(solution)/shard_map/ppermute | solution.py:163
  281.4 69.4 %collective-permute-start.22 = (bf16[2048,512]{1,0:T(8,128)(2,1)}, bf16[2048,512]{1,0:T(8,128)(2,1)}, u32[]{:S(2)}, u32[]{:S(2)}) collective-permute-start(bf16[2048,512]{1,0:T(8,128)(2,1)} %all-gather.16.cloned.1.call-done.refs_8_), channel_id=1, source_target_pairs={{0,4},{2,6},{4,0},{6,2},{1,5},{3,7},{5,1},{7,3},{8,12},{10,14},{12... | collective-permute-start | bytes 6291464 | tf_op jit(solution)/shard_map/ppermute | solution.py:163
  315.1 35.5 %collective-permute-start.25 = (bf16[2048,256]{1,0:T(8,128)(2,1)}, bf16[2048,256]{1,0:T(8,128)(2,1)S(1)}, u32[]{:S(2)}, u32[]{:S(2)}) collective-permute-start(bf16[2048,256]{1,0:T(8,128)(2,1)} %slice.274), channel_id=1, source_target_pairs={{0,4},{2,6},{4,0},{6,2},{1,5},{3,7},{5,1},{7,3},{8,12},{10,14},{12... | collective-permute-start | bytes 3145736 | tf_op jit(solution)/shard_map/ppermute | solution.py:163
  315.6 35.8 %collective-permute-start.24 = (bf16[2048,512]{1,0:T(8,128)(2,1)S(1)}, bf16[2048,512]{1,0:T(8,128)(2,1)}, u32[]{:S(2)}, u32[]{:S(2)}) collective-permute-start(bf16[2048,512]{1,0:T(8,128)(2,1)S(1)} %copy-done.25), channel_id=1, source_target_pairs={{0,2},{2,0},{4,6},{6,4},{1,3},{3,1},{5,7},{7,5},{8,10},{10,8},{12,... | collective-permute-start | bytes 6291464 | tf_op jit(solution)/shard_map/ppermute | solution.py:163
  315.6 36.5 %collective-permute-start.21 = (bf16[2048,512]{1,0:T(8,128)(2,1)}, bf16[2048,512]{1,0:T(8,128)(2,1)}, u32[]{:S(2)}, u32[]{:S(2)}) collective-permute-start(bf16[2048,512]{1,0:T(8,128)(2,1)} %all-gather.16.cloned.1.call-done.refs_8_), channel_id=1, source_target_pairs={{0,2},{2,0},{4,6},{6,4},{1,3},{3,1},{5,7},{7,5},{8,10},{10,8},{12,... | collective-permute-start | bytes 6291464 | tf_op jit(solution)/shard_map/ppermute | solution.py:163
  373.6 47.9 %collective-permute-start.27 = (bf16[512,2048]{1,0:T(8,128)(2,1)}, bf16[512,2048]{1,0:T(8,128)(2,1)S(1)}, u32[]{:S(2)}, u32[]{:S(2)}) collective-permute-start(bf16[512,2048]{1,0:T(8,128)(2,1)} %sum_products.5), channel_id=1, source_target_pairs={{0,1},{1,0},{2,3},{3,2},{4,5},{5,4},{6,7},{7,6},{8,9},{9,8},{10,11... | collective-permute-start | bytes 6291464 | tf_op jit(solution)/shard_map/ppermute | solution.py:163
  445.3 57.0 %collective-permute-start.33 = (bf16[2048,512]{0,1:T(8,128)(2,1)}, bf16[2048,512]{0,1:T(8,128)(2,1)}, u32[]{:S(2)}, u32[]{:S(2)}) collective-permute-start(bf16[2048,512]{0,1:T(8,128)(2,1)} %add_convert_fusion.8), channel_id=1, source_target_pairs={{0,4},{2,6},{4,0},{6,2},{1,5},{3,7},{5,1},{7,3},{8,12},{10,14},{12... | collective-permute-start | bytes 6291464 | tf_op jit(solution)/shard_map/ppermute | solution.py:163
  506.8 271.2 %reduce-scatter.14.cloned.1.call-start = ((), (), s32[]{:S(2)}) async-start(), calls=%async_computation.16 | async-start | bytes 5242880 | tf_op jit(solution)/shard_map/reduce_scatter | solution.py:171
  507.5 302.5 %reduce-scatter.8.cloned.1.call-start = ((), (), s32[]{:S(2)}) async-start(), calls=%async_computation.13 | async-start | bytes 2621440 | tf_op jit(solution)/shard_map/reduce_scatter | solution.py:171
  507.8 47.6 %collective-permute-start.32 = (bf16[512,2048]{1,0:T(8,128)(2,1)}, bf16[512,2048]{1,0:T(8,128)(2,1)}, u32[]{:S(2)}, u32[]{:S(2)}) collective-permute-start(bf16[512,2048]{1,0:T(8,128)(2,1)} %sum_products.6), channel_id=1, source_target_pairs={{0,1},{1,0},{2,3},{3,2},{4,5},{5,4},{6,7},{7,6},{8,9},{9,8},{10,11... | collective-permute-start | bytes 6291464 | tf_op jit(solution)/shard_map/ppermute | solution.py:163
  527.5 47.9 %collective-permute-start.40 = (bf16[2048,512]{0,1:T(8,128)(2,1)}, bf16[2048,512]{0,1:T(8,128)(2,1)}, u32[]{:S(2)}, u32[]{:S(2)}) collective-permute-start(bf16[2048,512]{0,1:T(8,128)(2,1)} %add_convert_fusion.3), channel_id=1, source_target_pairs={{0,4},{2,6},{4,0},{6,2},{1,5},{3,7},{5,1},{7,3},{8,12},{10,14},{12... | collective-permute-start | bytes 6291464 | tf_op jit(solution)/shard_map/ppermute | solution.py:163
  579.2 322.5 %reduce-scatter.10.cloned.1.call-start = ((), (), s32[]{:S(2)}) async-start(), calls=%async_computation.14 | async-start | bytes 5242880 | tf_op jit(solution)/shard_map/reduce_scatter | solution.py:171
  615.3 324.8 %reduce-scatter.6.cloned.1.call-start = ((), (), s32[]{:S(2)}) async-start(), calls=%async_computation.12 | async-start | bytes 2621440 | tf_op jit(solution)/shard_map/reduce_scatter | solution.py:171
  619.2 182.0 %collective-permute-start.55 = (bf16[2048,256]{0,1:T(8,128)(2,1)}, bf16[2048,256]{0,1:T(8,128)(2,1)}, u32[]{:S(2)}, u32[]{:S(2)}) collective-permute-start(bf16[2048,256]{0,1:T(8,128)(2,1)} %fusion.35), channel_id=1, source_target_pairs={{0,2},{2,0},{4,6},{6,4},{1,3},{3,1},{5,7},{7,5},{8,10},{10,8},{12,... | collective-permute-start | bytes 3145736 | tf_op jit(solution)/shard_map/ppermute | solution.py:163
  621.2 48.9 %collective-permute-start.67 = (bf16[2048,256]{0,1:T(8,128)(2,1)}, bf16[2048,256]{0,1:T(8,128)(2,1)}, u32[]{:S(2)}, u32[]{:S(2)}) collective-permute-start(bf16[2048,256]{0,1:T(8,128)(2,1)} %convolution_convert_fusion.22), channel_id=1, source_target_pairs={{0,2},{2,0},{4,6},{6,4},{1,3},{3,1},{5,7},{7,5},{8,10},{10,8},{12,... | collective-permute-start | bytes 3145736 | tf_op jit(solution)/shard_map/ppermute | solution.py:163
  655.3 37.7 %collective-permute-start.50 = (bf16[512,512]{1,0:T(8,128)(2,1)S(1)}, bf16[512,512]{1,0:T(8,128)(2,1)S(1)}, u32[]{:S(2)}, u32[]{:S(2)}) collective-permute-start(bf16[512,512]{1,0:T(8,128)(2,1)S(1)} %copy-done.57), channel_id=1, source_target_pairs={{0,4},{2,6},{4,0},{6,2},{1,5},{3,7},{5,1},{7,3},{8,12},{10,14},{12... | collective-permute-start | bytes 1572872 | tf_op jit(solution)/shard_map/ppermute | solution.py:163
  676.0 35.9 %collective-permute-start.56 = (bf16[2048,256]{0,1:T(8,128)(2,1)}, bf16[2048,256]{0,1:T(8,128)(2,1)}, u32[]{:S(2)}, u32[]{:S(2)}) collective-permute-start(bf16[2048,256]{0,1:T(8,128)(2,1)} %fusion.36), channel_id=1, source_target_pairs={{0,2},{2,0},{4,6},{6,4},{1,3},{3,1},{5,7},{7,5},{8,10},{10,8},{12,... | collective-permute-start | bytes 3145736 | tf_op jit(solution)/shard_map/ppermute | solution.py:163
  693.0 72.8 %collective-permute-start.49 = (bf16[2048,512]{0,1:T(8,128)(2,1)}, bf16[2048,512]{0,1:T(8,128)(2,1)}, u32[]{:S(2)}, u32[]{:S(2)}) collective-permute-start(bf16[2048,512]{0,1:T(8,128)(2,1)} %fusion.13), channel_id=1, source_target_pairs={{0,2},{2,0},{4,6},{6,4},{1,3},{3,1},{5,7},{7,5},{8,10},{10,8},{12,... | collective-permute-start | bytes 6291464 | tf_op jit(solution)/shard_map/ppermute | solution.py:163
  697.4 83.0 %collective-permute-start.53 = (bf16[2048,512]{0,1:T(8,128)(2,1)}, bf16[2048,512]{0,1:T(8,128)(2,1)}, u32[]{:S(2)}, u32[]{:S(2)}) collective-permute-start(bf16[2048,512]{0,1:T(8,128)(2,1)} %fusion.9), channel_id=1, source_target_pairs={{0,4},{2,6},{4,0},{6,2},{1,5},{3,7},{5,1},{7,3},{8,12},{10,14},{12... | collective-permute-start | bytes 6291464 | tf_op jit(solution)/shard_map/ppermute | solution.py:163
  708.8 54.7 %collective-permute-start.83 = (bf16[512,512]{0,1:T(8,128)(2,1)}, bf16[512,512]{0,1:T(8,128)(2,1)S(1)}, u32[]{:S(2)}, u32[]{:S(2)}) collective-permute-start(bf16[512,512]{0,1:T(8,128)(2,1)} %reduce-scatter.12.cloned.1.call-done), channel_id=1, source_target_pairs={{0,4},{2,6},{4,0},{6,2},{1,5},{3,7},{5,1},{7,3},{8,12},{10,14},{12... | collective-permute-start | bytes 1572872 | tf_op jit(solution)/shard_map/ppermute | solution.py:163
  714.9 56.8 %collective-permute-start.85 = (bf16[512,512]{0,1:T(8,128)(2,1)S(1)}, bf16[512,512]{0,1:T(8,128)(2,1)}, u32[]{:S(2)}, u32[]{:S(2)}) collective-permute-start(bf16[512,512]{0,1:T(8,128)(2,1)S(1)} %copy-done.12), channel_id=1, source_target_pairs={{0,2},{2,0},{4,6},{6,4},{1,3},{3,1},{5,7},{7,5},{8,10},{10,8},{12,... | collective-permute-start | bytes 1572872 | tf_op jit(solution)/shard_map/ppermute | solution.py:163
  765.7 38.3 %collective-permute-start.70 = (bf16[512,256]{0,1:T(8,128)(2,1)}, bf16[512,256]{0,1:T(8,128)(2,1)}, u32[]{:S(2)}, u32[]{:S(2)}) collective-permute-start(bf16[512,256]{0,1:T(8,128)(2,1)} %get-tuple-element.225), channel_id=1, source_target_pairs={{0,8},{8,16},{16,24},{24,0},{1,9},{9,17},{17,25},{25,1},{2,10},{10... | collective-permute-start | bytes 786440 | tf_op jit(solution)/shard_map/ppermute | solution.py:183
  805.1 39.9 %collective-permute-start.60 = (bf16[512,256]{0,1:T(8,128)(2,1)}, bf16[512,256]{0,1:T(8,128)(2,1)}, u32[]{:S(2)}, u32[]{:S(2)}) collective-permute-start(bf16[512,256]{0,1:T(8,128)(2,1)} %get-tuple-element.232), channel_id=1, source_target_pairs={{0,24},{8,0},{16,8},{24,16},{1,25},{9,1},{17,9},{25,17},{2,26},{10... | collective-permute-start | bytes 786440 | tf_op jit(solution)/shard_map/ppermute | solution.py:183
  806.7 50.9 %collective-permute-start.59 = (bf16[512,256]{0,1:T(8,128)(2,1)}, bf16[512,256]{0,1:T(8,128)(2,1)}, u32[]{:S(2)}, u32[]{:S(2)}) collective-permute-start(bf16[512,256]{0,1:T(8,128)(2,1)} %get-tuple-element.233), channel_id=1, source_target_pairs={{0,16},{8,24},{16,0},{24,8},{1,17},{9,25},{17,1},{25,9},{2,18},{10... | collective-permute-start | bytes 786440 | tf_op jit(solution)/shard_map/ppermute | solution.py:183
  869.2 42.2 %collective-permute-start.78 = (bf16[512,512]{0,1:T(8,128)(2,1)}, bf16[512,512]{0,1:T(8,128)(2,1)}, u32[]{:S(2)}, u32[]{:S(2)}) collective-permute-start(bf16[512,512]{0,1:T(8,128)(2,1)} %reduce-scatter.8.cloned.1.call-done), channel_id=1, source_target_pairs={{0,2},{2,0},{4,6},{6,4},{1,3},{3,1},{5,7},{7,5},{8,10},{10,8},{12,... | collective-permute-start | bytes 1572872 | tf_op jit(solution)/shard_map/ppermute | solution.py:163
  878.3 53.3 %collective-permute-start.54 = (bf16[512,2048]{1,0:T(8,128)(2,1)S(1)}, bf16[512,2048]{1,0:T(8,128)(2,1)}, u32[]{:S(2)}, u32[]{:S(2)}) collective-permute-start(bf16[512,2048]{1,0:T(8,128)(2,1)S(1)} %copy-done.11), channel_id=1, source_target_pairs={{0,1},{1,0},{2,3},{3,2},{4,5},{5,4},{6,7},{7,6},{8,9},{9,8},{10,11... | collective-permute-start | bytes 6291464 | tf_op jit(solution)/shard_map/ppermute | solution.py:163
  (156 other events, 1630.4 us)
Sparse Core Ops, SparseCore 0:
  10.1 50.4 all-gather.9
  62.8 44.4 all-gather.7
  109.5 44.4 all-gather.11
  155.9 44.4 all-gather.13
  201.8 44.4 all-gather.15
  248.3 44.4 all-gather.17
  295.0 26.7 all-gather.19
  506.9 43.9 reduce-scatter.11
  553.2 76.0 reduce-scatter.13
  631.9 44.1 reduce-scatter.7
  678.4 75.9 reduce-scatter.9
  801.3 60.1 reduce-scatter.5

commit v2 on v1

--- a/solution.py
+++ b/solution.py
@@ -3,6 +3,7 @@
 from jax import lax
 from jax.experimental import pallas as pl
 from jax.experimental.pallas import tpu as pltpu
+from jax.experimental.layout import Layout, with_layout_constraint
 from jax.sharding import PartitionSpec as P
 
 
@@ -168,7 +169,8 @@
 
 
 def scatter(total):
-    return lax.psum_scatter(total, "shard", scatter_dimension=0, tiled=True)
+    mine = lax.psum_scatter(total, "shard", scatter_dimension=0, tiled=True)
+    return with_layout_constraint(mine, Layout((0, 1)))
 
 
 def scatter_direct(total):
@@ -187,7 +189,8 @@
 
 
 def sum_direct(mine, got):
-    return sum([item.astype(F32) for item in got], mine.astype(F32)).astype(BF)
+    total = sum([item.astype(F32) for item in got], mine.astype(F32)).astype(BF)
+    return with_layout_constraint(total, Layout((0, 1)))
 
 
 def fill(own, far):
@@ -338,7 +341,7 @@
     up_rows = up_vector.reshape(4, 2, ff_half)
     pre_act = [product(hidden_low, up_w[half][q]) + up_rows[q, half] for half, q in pairs]
     activated = [gelu_tanh(item).astype(BF) for item in pre_act]
-    down_swapped = across(after(down_own[1], *activated)[:, :ff_part], 2)
+    down_swapped = across(after(down_own[1], activated[0])[:, :ff_part], 2)
     down_last = jnp.concatenate([down_swapped, after(down_far, *activated)], axis=1)
     down_w = [
         spread(after(down_own[0], activated[0])),
@@ -380,6 +383,7 @@
     output_early = near_sums(
         [transposed_times(grad_branch, attended[q]).astype(BF) for q in range(4)]
     )
+    grad_attended[1:] = lax.optimization_barrier((*grad_attended[1:], *output_early))[:3]
     grad_attended[2:] = lax.optimization_barrier((*grad_attended[2:], up_total))[:-1]
     down_far_first = across(down_first, 2)
     grad_q, here_parts, near_parts = [], [], []
@@ -408,9 +412,12 @@
     output_direct = scatter_direct(far_sum(*output_early, *grad_q))
     query_early = near_sums([transposed_times(tokens, grad_q[q]).astype(BF) for q in range(4)])
     kv_parts = [transposed_times(tokens, grad_kv[q]).astype(BF) for q in range(4)]
-    kv_total = far_sum(*near_sums(kv_parts))
+    kv_early = near_sums(kv_parts)
+    kv_total = far_sum(*kv_early)
     kv_mine = scatter(kv_total)
-    query_mine, query_got = scatter_direct(far_sum(*query_early, kv_total))
+    query_mine, query_got = scatter_direct(
+        far_sum(query_early[0], after(query_early[1], kv_total))
+    )
     output_mine, output_got = lax.optimization_barrier((*output_direct, kv_total))[:2]
     up_first, up_second, grad_q_then = (
         after(item, kv_total) for item in (up_first, up_second, grad_q[0])
@@ -454,7 +461,7 @@
     ]
     sizes = [item.shape[0] for item in pieces]
     flat = jnp.concatenate(pieces + [jnp.zeros((-sum(sizes) % 1024,), F32)]).reshape(-1, 128)
-    flat = butterfly(after(flat, kv_total), ("ctx", "shard")).reshape(-1)
+    flat = butterfly(after(flat, *kv_early), ("ctx", "shard")).reshape(-1)
     totals = []
     at = 0
     for size in sizes:

time: 990 us -> 986 us (level)
  local copies, waits for them, and re-layouts: 69 us -> 45.1 us
  waiting for transfers between devices: 428 us -> 444 us
    unnamed x210 -> x194, local copies, waits for them, and re-layouts: 32.1 us -> 8.57 us
    ppermute x88, waiting for transfers between devices: 342 us -> 359 us  [across(): return lax.ppermute(array, axis, [(at, at ^ step) for at in range(size)])]
  transfers between devices with their start and end apart: 106 -> 106, of which waited for: 29 -> 30; matrix products, arithmetic and copies ran while one was open for 33% -> 31% of each run, Pallas kernels for 10% -> 10%
where the time goes in v2:
time: 986 us; the launch traced here: 975 us
  waiting for transfers between devices  444 us (45%)
  matrix products  173 us (18%)
  other arithmetic  117 us (12%)
  Pallas kernels  113 us (11%)
  starting transfers between devices  67.3 us (7%)
  local copies, waits for them, and re-layouts  45.1 us (5%)
  between operations  16.2 us (2%)
    ppermute x88, waiting for transfers between devices, across(): return lax.ppermute(array, axis, [(at, at ^ step) for at in range(size)])  359 us
    dot_general x28, matrix products, product(): return jnp.dot(left, right, preferred_element_type=F32)  108 us
    all_gather x7, waiting for transfers between devices, collect(): return lax.all_gather(piece, 'shard', axis=0, tiled=True)  69.5 us
    dot_general x28, matrix products, transposed_times(): lax.dot_general(left, right, (((0,), (0,)), ((), ())), preferred_element_...  64.7 us
    ppermute x88, starting transfers between devices, across(): return lax.ppermute(array, axis, [(at, at ^ step) for at in range(size)])  58.3 us
    pallas_call x4, Pallas kernels, sum_products(): pl.pallas_call(sum_kernel, grid=(width // block,), in_specs=[pl.BlockSpec...  51.8 us
    pallas_call x4, Pallas kernels, attention_back(): pl.pallas_call(backward_kernel, grid=(heads, rows // block), in_specs=[ro...  35.3 us
    pallas_call x4, Pallas kernels, attention(): pl.pallas_call(forward_kernel, grid=(heads, rows // block), in_specs=[row...  26.1 us
  transfers between devices with their start and end apart: 106, of which 30 were waited for; matrix products, arithmetic and copies ran while one was open for 31% of the time, Pallas kernels for 10%

profile of v2, /device:TPU:0, one launch (start us, length us, event | category | flops | bytes accessed | tf_op | source)
XLA Modules:
  0.0 975.5 jit_solution(11327713726302420423)
XLA Ops:
  26.1 6.5 collective-permute-done.1
  33.7 7.7 collective-permute-done.2
  41.5 23.7 %collective-permute-done.3 = bf16[512,2048]{1,0:T(8,128)(2,1)} collective-permute-done((bf16[512,2048]{1,0:T(8,128)(2,1)S(1)}, bf16[512,2048]{1,0:T(8,128)(2,1)}, u32[]{:S(2)}, u32[]{:S(2)}) %collective-permute-start.3) | collective-permute-done | bytes 2097184 | tf_op jit(solution)/shard_map/ppermute | solution.py:164
  67.9 39.4 %all-gather.8.cloned.1.call-done = bf16[2048,512]{1,0:T(8,128)(2,1)} async-done(((bf16[512,512]{1,0:T(8,128)(2,1)}), bf16[2048,512]{1,0:T(8,128)(2,1)}) %all-gather.8.cloned.1.call-update) | async-done | bytes 2097168 | tf_op jit(solution)/shard_map/all_gather | solution.py:168
  108.8 5.5 add_convert_fusion.17.kh_ref.vh_ref
  120.6 4.6 add_convert_fusion.15.kh_ref.vh_ref
  125.1 28.8 %all-gather.12.cloned.1.call-done.refs_8_ = bf16[2048,512]{1,0:T(8,128)(2,1)} async-done(((bf16[512,512]{1,0:T(8,128)(2,1)}), bf16[2048,512]{1,0:T(8,128)(2,1)}) %all-gather.12.cloned.1.call-update) | async-done | bytes 2097168 | tf_op jit(solution)/shard_map/all_gather | solution.py:168
  158.7 5.6 add_convert_fusion.16.kh_ref.vh_ref
  173.5 6.9 attention_forward.5
  180.4 5.5 add_convert_fusion.14.kh_ref.vh_ref
  189.0 6.4 attention_forward.4
  198.1 6.4 attention_forward.7
  208.1 6.4 attention_forward.6
  214.5 8.2 sum_products.4
  228.5 24.0 %collective-permute-done.19.refs_14_ = bf16[2048,512]{1,0:T(8,128)(2,1)} collective-permute-done((bf16[2048,512]{1,0:T(8,128)(2,1)}, bf16[2048,512]{1,0:T(8,128)(2,1)}, u32[]{:S(2)}, u32[]{:S(2)}) %collective-permute-start.19) | collective-permute-done | bytes 2097184 | tf_op jit(solution)/shard_map/ppermute | solution.py:164
  252.5 18.0 %collective-permute-done.14 = bf16[512,2048]{1,0:T(8,128)(2,1)} collective-permute-done((bf16[512,2048]{1,0:T(8,128)(2,1)}, bf16[512,2048]{1,0:T(8,128)(2,1)}, u32[]{:S(2)}, u32[]{:S(2)}) %collective-permute-start.14) | collective-permute-done | bytes 2097184 | tf_op jit(solution)/shard_map/ppermute | solution.py:164
  270.5 4.9 fusion.142
  299.8 5.1 multiply_convert_fusion.6
  313.9 36.9 %collective-permute-done.25 = bf16[2048,256]{1,0:T(8,128)(2,1)S(1)} collective-permute-done((bf16[2048,256]{1,0:T(8,128)(2,1)S(1)}, bf16[2048,256]{1,0:T(8,128)(2,1)S(1)}, u32[]{:S(2)}, u32[]{:S(2)}) %collective-permute-start.25) | collective-permute-done | bytes 1048608 | tf_op jit(solution)/shard_map/ppermute | solution.py:164
  351.9 4.7 multiply_convert_fusion
  366.3 15.2 %sum_products.5 = bf16[512,2048]{1,0:T(8,128)(2,1)} custom-call(bf16[512,512]{1,0:T(8,128)(2,1)} %get-tuple-element.237.refs_0_, bf16[512,512]{1,0:T(8,128)(2,1)} %get-tuple-element.239.refs_1_, bf16[512,512]{1,0:T(8,128)(2,1)} %get-tuple-element.241.refs_2_, bf16[512,512]{1,0:T(8,128)(2,1)} %get-tuple-element.243.refs_3_, ...), custom_call_target="tpu_custom_call" | custom-call | tf_op jit(solution)/shard_map/sum_products/pallas_call | solution.py:147
  383.2 46.2 %collective-permute-done.27 = bf16[512,2048]{1,0:T(8,128)(2,1)S(1)} collective-permute-done((bf16[512,2048]{1,0:T(8,128)(2,1)}, bf16[512,2048]{1,0:T(8,128)(2,1)S(1)}, u32[]{:S(2)}, u32[]{:S(2)}) %collective-permute-start.27) | collective-permute-done | bytes 2097184 | tf_op jit(solution)/shard_map/ppermute | solution.py:164
  429.4 4.8 fusion.140
  460.1 5.0 add_convert_fusion.9
  496.4 15.2 %sum_products.6 = bf16[512,2048]{1,0:T(8,128)(2,1)} custom-call(bf16[512,512]{1,0:T(8,128)(2,1)} %get-tuple-element.135.refs_0_, bf16[512,512]{1,0:T(8,128)(2,1)} %get-tuple-element.139.refs_1_, bf16[512,512]{1,0:T(8,128)(2,1)} %get-tuple-element.143.refs_2_, bf16[512,512]{1,0:T(8,128)(2,1)} %get-tuple-element.147.refs_3_, ...), custom_call_target="tpu_custom_call" | custom-call | tf_op jit(solution)/shard_map/sum_products/pallas_call | solution.py:147
  544.0 20.6 %collective-permute-done.32 = bf16[512,2048]{1,0:T(8,128)(2,1)} collective-permute-done((bf16[512,2048]{1,0:T(8,128)(2,1)}, bf16[512,2048]{1,0:T(8,128)(2,1)}, u32[]{:S(2)}, u32[]{:S(2)}) %collective-permute-start.32) | collective-permute-done | bytes 2097184 | tf_op jit(solution)/shard_map/ppermute | solution.py:164
  564.7 7.9 multiply_reduce_fusion.3
  576.1 8.2 collective-permute-done.42
  592.5 8.8 attention_backward.4
  620.6 9.1 attention_backward.5
  639.0 8.6 attention_backward.6
  648.2 8.8 attention_backward.7
  670.7 8.7 collective-permute-done.50
  685.3 11.5 %collective-permute-done.45 = bf16[512,512]{1,0:T(8,128)(2,1)S(1)} collective-permute-done((bf16[512,512]{1,0:T(8,128)(2,1)S(1)}, bf16[512,512]{1,0:T(8,128)(2,1)S(1)}, u32[]{:S(2)}, u32[]{:S(2)}) %collective-permute-start.45) | collective-permute-done | bytes 524320 | tf_op jit(solution)/shard_map/ppermute | solution.py:164
  702.1 4.5 fusion.9
  707.3 6.2 collective-permute-done.83
  722.4 36.5 %collective-permute-done.91 = f32[152,128]{1,0:T(8,128)S(1)} collective-permute-done((f32[152,128]{1,0:T(8,128)S(1)}, f32[152,128]{1,0:T(8,128)S(1)}, u32[]{:S(2)}, u32[]{:S(2)}) %collective-permute-start.91) | collective-permute-done | bytes 77856 | tf_op jit(solution)/shard_map/ppermute | solution.py:164
  775.3 16.9 %collective-permute-done.93 = f32[152,128]{1,0:T(8,128)S(1)} collective-permute-done((f32[152,128]{1,0:T(8,128)S(1)}, f32[152,128]{1,0:T(8,128)S(1)}, u32[]{:S(2)}, u32[]{:S(2)}) %collective-permute-start.93) | collective-permute-done | bytes 77856 | tf_op jit(solution)/shard_map/ppermute | solution.py:164
  806.7 21.2 %collective-permute-done.73 = bf16[512,256]{1,0:T(8,128)(2,1)} collective-permute-done((bf16[512,256]{1,0:T(8,128)(2,1)S(1)}, bf16[512,256]{1,0:T(8,128)(2,1)}, u32[]{:S(2)}, u32[]{:S(2)}) %collective-permute-start.73) | collective-permute-done | bytes 262176 | tf_op jit(solution)/shard_map/ppermute | solution.py:164
  831.9 13.2 %sum_products.7 = bf16[512,2048]{1,0:T(8,128)(2,1)} custom-call(bf16[512,256]{1,0:T(8,128)(2,1)} %get-tuple-element.108.refs_0_, bf16[512,256]{1,0:T(8,128)(2,1)} %get-tuple-element.109.refs_1_, bf16[512,256]{1,0:T(8,128)(2,1)} %get-tuple-element.110.refs_2_, bf16[512,256]{1,0:T(8,128)(2,1)} %get-tuple-element.111.refs_3_, bf16[512,512]{1,0:T(8,128)(2,1)} %copy-done.30, ...), custom_call_target="tpu_custom_call" | custom-call | tf_op jit(solution)/shard_map/sum_products/pallas_call | solution.py:147
  857.0 19.0 %collective-permute-done.59 = bf16[2048,256]{1,0:T(8,128)(2,1)S(1)} collective-permute-done((bf16[2048,256]{1,0:T(8,128)(2,1)S(1)}, bf16[2048,256]{1,0:T(8,128)(2,1)S(1)}, u32[]{:S(2)}, u32[]{:S(2)}) %collective-permute-start.59) | collective-permute-done | bytes 1048608 | tf_op jit(solution)/shard_map/ppermute | solution.py:164
  880.1 6.3 collective-permute-done.62
  893.1 7.9 collective-permute-done.61
  913.1 7.4 collective-permute-done.81
  920.5 10.1 %collective-permute-done.79 = bf16[512,512]{1,0:T(8,128)(2,1)S(1)} collective-permute-done((bf16[512,512]{1,0:T(8,128)(2,1)S(1)}, bf16[512,512]{1,0:T(8,128)(2,1)S(1)}, u32[]{:S(2)}, u32[]{:S(2)}) %collective-permute-start.79) | collective-permute-done | bytes 524320 | tf_op jit(solution)/shard_map/ppermute | solution.py:164
  931.5 4.7 fusion.35
  945.8 9.0 collective-permute-done.66
  958.3 6.7 convert_element_type.924
  (617 shorter events, 356.0 us)
Async XLA Ops:
  7.2 58.0 %all-gather.10.cloned.1.call-start = ((), (), s32[]{:S(2)}) async-start(), calls=%async_computation.6 | async-start | bytes 2621440 | tf_op jit(solution)/shard_map/all_gather | solution.py:168
  9.2 98.1 %all-gather.8.cloned.1.call-start = ((), (), s32[]{:S(2)}) async-start(), calls=%async_computation.5 | async-start | bytes 2621440 | tf_op jit(solution)/shard_map/all_gather | solution.py:168
  11.2 142.8 %all-gather.12.cloned.1.call-start = ((), (), s32[]{:S(2)}) async-start(), calls=%async_computation.7 | async-start | bytes 2621440 | tf_op jit(solution)/shard_map/all_gather | solution.py:168
  13.5 191.0 %all-gather.14.cloned.1.call-start = ((), (), s32[]{:S(2)}) async-start(), calls=%async_computation.8 | async-start | bytes 2621440 | tf_op jit(solution)/shard_map/all_gather | solution.py:168
  14.1 267.5 %all-gather.16.cloned.1.call-start = ((), (), s32[]{:S(2)}) async-start(), calls=%async_computation.9 | async-start | bytes 2621440 | tf_op jit(solution)/shard_map/all_gather | solution.py:168
  16.4 276.4 %all-gather.18.cloned.1.call-start = ((), (), s32[]{:S(2)}) async-start(), calls=%async_computation.10 | async-start | bytes 2621440 | tf_op jit(solution)/shard_map/all_gather | solution.py:168
  16.4 48.8 %collective-permute-start.3 = (bf16[512,2048]{1,0:T(8,128)(2,1)S(1)}, bf16[512,2048]{1,0:T(8,128)(2,1)}, u32[]{:S(2)}, u32[]{:S(2)}) collective-permute-start(bf16[512,2048]{1,0:T(8,128)(2,1)S(1)} %bitcast.266), channel_id=1, source_target_pairs={{0,4},{2,6},{4,0},{6,2},{1,5},{3,7},{5,1},{7,3},{8,12},{10,14},{12... | collective-permute-start | bytes 6291464 | tf_op jit(solution)/shard_map/ppermute | solution.py:164
  21.7 334.8 %all-gather.20.cloned.1.call-start = ((), (), s32[]{:S(2)}) async-start(), calls=%async_computation.11 | async-start | bytes 1310720 | tf_op jit(solution)/shard_map/all_gather | solution.py:168
  65.2 55.3 %collective-permute-start.9 = (bf16[2048,512]{1,0:T(8,128)(2,1)}, bf16[2048,512]{1,0:T(8,128)(2,1)}, u32[]{:S(2)}, u32[]{:S(2)}) collective-permute-start(bf16[2048,512]{1,0:T(8,128)(2,1)} %all-gather.10.cloned.1.call-done.refs_12_), channel_id=1, source_target_pairs={{0,4},{2,6},{4,0},{6,2},{1,5},{3,7},{5,1},{7,3},{8,12},{10,14},{12... | collective-permute-start | bytes 6291464 | tf_op jit(solution)/shard_map/ppermute | solution.py:164
  67.9 90.9 %collective-permute-start.4 = (bf16[2048,512]{1,0:T(8,128)(2,1)}, bf16[2048,512]{1,0:T(8,128)(2,1)}, u32[]{:S(2)}, u32[]{:S(2)}) collective-permute-start(bf16[2048,512]{1,0:T(8,128)(2,1)} %all-gather.10.cloned.1.call-done.refs_12_), channel_id=1, source_target_pairs={{0,2},{2,0},{4,6},{6,4},{1,3},{3,1},{5,7},{7,5},{8,10},{10,8},{12,... | collective-permute-start | bytes 6291464 | tf_op jit(solution)/shard_map/ppermute | solution.py:164
  107.3 50.0 %collective-permute-start.8 = (bf16[2048,512]{1,0:T(8,128)(2,1)}, bf16[2048,512]{1,0:T(8,128)(2,1)}, u32[]{:S(2)}, u32[]{:S(2)}) collective-permute-start(bf16[2048,512]{1,0:T(8,128)(2,1)} %all-gather.8.cloned.1.call-done), channel_id=1, source_target_pairs={{0,4},{2,6},{4,0},{6,2},{1,5},{3,7},{5,1},{7,3},{8,12},{10,14},{12... | collective-permute-start | bytes 6291464 | tf_op jit(solution)/shard_map/ppermute | solution.py:164
  114.3 59.1 %collective-permute-start.7 = (bf16[1024,512]{1,0:T(8,128)(2,1)}, bf16[1024,512]{1,0:T(8,128)(2,1)}, u32[]{:S(2)}, u32[]{:S(2)}) collective-permute-start(bf16[1024,512]{1,0:T(8,128)(2,1)} %add_convert_fusion.17.kh_ref.vh_ref), channel_id=1, source_target_pairs={{0,2},{2,0},{4,6},{6,4},{1,3},{3,1},{5,7},{7,5},{8,10},{10,8},{12,... | collective-permute-start | bytes 3145736 | tf_op jit(solution)/shard_map/ppermute | solution.py:164
  114.3 53.0 %collective-permute-start.6 = (bf16[2048,512]{1,0:T(8,128)(2,1)}, bf16[2048,512]{1,0:T(8,128)(2,1)}, u32[]{:S(2)}, u32[]{:S(2)}) collective-permute-start(bf16[2048,512]{1,0:T(8,128)(2,1)} %all-gather.8.cloned.1.call-done), channel_id=1, source_target_pairs={{0,2},{2,0},{4,6},{6,4},{1,3},{3,1},{5,7},{7,5},{8,10},{10,8},{12,... | collective-permute-start | bytes 6291464 | tf_op jit(solution)/shard_map/ppermute | solution.py:164
  120.6 59.8 %collective-permute-start.10 = (bf16[2048,512]{1,0:T(8,128)(2,1)}, bf16[2048,512]{1,0:T(8,128)(2,1)}, u32[]{:S(2)}, u32[]{:S(2)}) collective-permute-start(bf16[2048,512]{1,0:T(8,128)(2,1)} %collective-permute-done.9.refs_14_), channel_id=1, source_target_pairs={{0,2},{2,0},{4,6},{6,4},{1,3},{3,1},{5,7},{7,5},{8,10},{10,8},{12,... | collective-permute-start | bytes 6291464 | tf_op jit(solution)/shard_map/ppermute | solution.py:164
  157.3 70.6 %collective-permute-start.16 = (bf16[2048,512]{1,0:T(8,128)(2,1)}, bf16[2048,512]{1,0:T(8,128)(2,1)}, u32[]{:S(2)}, u32[]{:S(2)}) collective-permute-start(bf16[2048,512]{1,0:T(8,128)(2,1)} %all-gather.12.cloned.1.call-done.refs_8_), channel_id=1, source_target_pairs={{0,4},{2,6},{4,0},{6,2},{1,5},{3,7},{5,1},{7,3},{8,12},{10,14},{12... | collective-permute-start | bytes 6291464 | tf_op jit(solution)/shard_map/ppermute | solution.py:164
  158.7 36.7 %collective-permute-start.12 = (bf16[2048,512]{1,0:T(8,128)(2,1)}, bf16[2048,512]{1,0:T(8,128)(2,1)}, u32[]{:S(2)}, u32[]{:S(2)}) collective-permute-start(bf16[2048,512]{1,0:T(8,128)(2,1)} %collective-permute-done.8), channel_id=1, source_target_pairs={{0,2},{2,0},{4,6},{6,4},{1,3},{3,1},{5,7},{7,5},{8,10},{10,8},{12,... | collective-permute-start | bytes 6291464 | tf_op jit(solution)/shard_map/ppermute | solution.py:164
  204.5 48.0 %collective-permute-start.19 = (bf16[2048,512]{1,0:T(8,128)(2,1)}, bf16[2048,512]{1,0:T(8,128)(2,1)}, u32[]{:S(2)}, u32[]{:S(2)}) collective-permute-start(bf16[2048,512]{1,0:T(8,128)(2,1)} %all-gather.14.cloned.1.call-done.refs_12_), channel_id=1, source_target_pairs={{0,4},{2,6},{4,0},{6,2},{1,5},{3,7},{5,1},{7,3},{8,12},{10,14},{12... | collective-permute-start | bytes 6291464 | tf_op jit(solution)/shard_map/ppermute | solution.py:164
  222.8 47.7 %collective-permute-start.14 = (bf16[512,2048]{1,0:T(8,128)(2,1)}, bf16[512,2048]{1,0:T(8,128)(2,1)}, u32[]{:S(2)}, u32[]{:S(2)}) collective-permute-start(bf16[512,2048]{1,0:T(8,128)(2,1)} %sum_products.4), channel_id=1, source_target_pairs={{0,1},{1,0},{2,3},{3,2},{4,5},{5,4},{6,7},{7,6},{8,9},{9,8},{10,11... | collective-permute-start | bytes 6291464 | tf_op jit(solution)/shard_map/ppermute | solution.py:164
  226.0 472.5 %reduce-scatter.12.cloned.1.call-start = ((), (), s32[]{:S(2)}) async-start(), calls=%async_computation.15 | async-start | bytes 2621440 | tf_op jit(solution)/shard_map/reduce_scatter | solution.py:172
  227.8 70.5 %collective-permute-start.15 = (bf16[2048,512]{1,0:T(8,128)(2,1)}, bf16[2048,512]{1,0:T(8,128)(2,1)}, u32[]{:S(2)}, u32[]{:S(2)}) collective-permute-start(bf16[2048,512]{1,0:T(8,128)(2,1)} %all-gather.12.cloned.1.call-done.refs_8_), channel_id=1, source_target_pairs={{0,2},{2,0},{4,6},{6,4},{1,3},{3,1},{5,7},{7,5},{8,10},{10,8},{12,... | collective-permute-start | bytes 6291464 | tf_op jit(solution)/shard_map/ppermute | solution.py:164
  227.9 77.0 %collective-permute-start.17 = (bf16[2048,512]{1,0:T(8,128)(2,1)}, bf16[2048,512]{1,0:T(8,128)(2,1)}, u32[]{:S(2)}, u32[]{:S(2)}) collective-permute-start(bf16[2048,512]{1,0:T(8,128)(2,1)} %collective-permute-done.16.refs_10_), channel_id=1, source_target_pairs={{0,2},{2,0},{4,6},{6,4},{1,3},{3,1},{5,7},{7,5},{8,10},{10,8},{12,... | collective-permute-start | bytes 6291464 | tf_op jit(solution)/shard_map/ppermute | solution.py:164
  228.4 80.8 %collective-permute-start.18 = (bf16[2048,512]{1,0:T(8,128)(2,1)}, bf16[2048,512]{1,0:T(8,128)(2,1)}, u32[]{:S(2)}, u32[]{:S(2)}) collective-permute-start(bf16[2048,512]{1,0:T(8,128)(2,1)} %all-gather.14.cloned.1.call-done.refs_12_), channel_id=1, source_target_pairs={{0,2},{2,0},{4,6},{6,4},{1,3},{3,1},{5,7},{7,5},{8,10},{10,8},{12,... | collective-permute-start | bytes 6291464 | tf_op jit(solution)/shard_map/ppermute | solution.py:164
  252.5 99.4 %collective-permute-start.20 = (bf16[2048,512]{1,0:T(8,128)(2,1)}, bf16[2048,512]{1,0:T(8,128)(2,1)}, u32[]{:S(2)}, u32[]{:S(2)}) collective-permute-start(bf16[2048,512]{1,0:T(8,128)(2,1)} %collective-permute-done.19.refs_14_), channel_id=1, source_target_pairs={{0,2},{2,0},{4,6},{6,4},{1,3},{3,1},{5,7},{7,5},{8,10},{10,8},{12,... | collective-permute-start | bytes 6291464 | tf_op jit(solution)/shard_map/ppermute | solution.py:164
  281.6 77.2 %collective-permute-start.22 = (bf16[2048,512]{1,0:T(8,128)(2,1)}, bf16[2048,512]{1,0:T(8,128)(2,1)}, u32[]{:S(2)}, u32[]{:S(2)}) collective-permute-start(bf16[2048,512]{1,0:T(8,128)(2,1)} %all-gather.16.cloned.1.call-done.refs_8_), channel_id=1, source_target_pairs={{0,4},{2,6},{4,0},{6,2},{1,5},{3,7},{5,1},{7,3},{8,12},{10,14},{12... | collective-permute-start | bytes 6291464 | tf_op jit(solution)/shard_map/ppermute | solution.py:164
  298.3 52.5 %collective-permute-start.25 = (bf16[2048,256]{1,0:T(8,128)(2,1)S(1)}, bf16[2048,256]{1,0:T(8,128)(2,1)S(1)}, u32[]{:S(2)}, u32[]{:S(2)}) collective-permute-start(bf16[2048,256]{1,0:T(8,128)(2,1)S(1)} %slice.274), channel_id=1, source_target_pairs={{0,4},{2,6},{4,0},{6,2},{1,5},{3,7},{5,1},{7,3},{8,12},{10,14},{12... | collective-permute-start | bytes 3145736 | tf_op jit(solution)/shard_map/ppermute | solution.py:164
  304.9 54.4 %collective-permute-start.24 = (bf16[2048,512]{1,0:T(8,128)(2,1)S(1)}, bf16[2048,512]{1,0:T(8,128)(2,1)}, u32[]{:S(2)}, u32[]{:S(2)}) collective-permute-start(bf16[2048,512]{1,0:T(8,128)(2,1)S(1)} %copy-done.23), channel_id=1, source_target_pairs={{0,2},{2,0},{4,6},{6,4},{1,3},{3,1},{5,7},{7,5},{8,10},{10,8},{12,... | collective-permute-start | bytes 6291464 | tf_op jit(solution)/shard_map/ppermute | solution.py:164
  309.2 50.1 %collective-permute-start.21 = (bf16[2048,512]{1,0:T(8,128)(2,1)}, bf16[2048,512]{1,0:T(8,128)(2,1)}, u32[]{:S(2)}, u32[]{:S(2)}) collective-permute-start(bf16[2048,512]{1,0:T(8,128)(2,1)} %all-gather.16.cloned.1.call-done.refs_8_), channel_id=1, source_target_pairs={{0,2},{2,0},{4,6},{6,4},{1,3},{3,1},{5,7},{7,5},{8,10},{10,8},{12,... | collective-permute-start | bytes 6291464 | tf_op jit(solution)/shard_map/ppermute | solution.py:164
  381.5 47.9 %collective-permute-start.27 = (bf16[512,2048]{1,0:T(8,128)(2,1)}, bf16[512,2048]{1,0:T(8,128)(2,1)S(1)}, u32[]{:S(2)}, u32[]{:S(2)}) collective-permute-start(bf16[512,2048]{1,0:T(8,128)(2,1)} %sum_products.5), channel_id=1, source_target_pairs={{0,1},{1,0},{2,3},{3,2},{4,5},{5,4},{6,7},{7,6},{8,9},{9,8},{10,11... | collective-permute-start | bytes 6291464 | tf_op jit(solution)/shard_map/ppermute | solution.py:164
  453.1 58.5 %collective-permute-start.33 = (bf16[2048,512]{1,0:T(8,128)(2,1)}, bf16[2048,512]{1,0:T(8,128)(2,1)}, u32[]{:S(2)}, u32[]{:S(2)}) collective-permute-start(bf16[2048,512]{1,0:T(8,128)(2,1)} %add_convert_fusion.8), channel_id=1, source_target_pairs={{0,4},{2,6},{4,0},{6,2},{1,5},{3,7},{5,1},{7,3},{8,12},{10,14},{12... | collective-permute-start | bytes 6291464 | tf_op jit(solution)/shard_map/ppermute | solution.py:164
  515.7 277.8 %reduce-scatter.14.cloned.1.call-start = ((), (), s32[]{:S(2)}) async-start(), calls=%async_computation.16 | async-start | bytes 5242880 | tf_op jit(solution)/shard_map/reduce_scatter | solution.py:172
  516.5 290.1 %reduce-scatter.8.cloned.1.call-start = ((), (), s32[]{:S(2)}) async-start(), calls=%async_computation.13 | async-start | bytes 2621440 | tf_op jit(solution)/shard_map/reduce_scatter | solution.py:172
  517.0 47.6 %collective-permute-start.32 = (bf16[512,2048]{1,0:T(8,128)(2,1)}, bf16[512,2048]{1,0:T(8,128)(2,1)}, u32[]{:S(2)}, u32[]{:S(2)}) collective-permute-start(bf16[512,2048]{1,0:T(8,128)(2,1)} %sum_products.6), channel_id=1, source_target_pairs={{0,1},{1,0},{2,3},{3,2},{4,5},{5,4},{6,7},{7,6},{8,9},{9,8},{10,11... | collective-permute-start | bytes 6291464 | tf_op jit(solution)/shard_map/ppermute | solution.py:164
  536.4 47.9 %collective-permute-start.42 = (bf16[2048,512]{1,0:T(8,128)(2,1)}, bf16[2048,512]{1,0:T(8,128)(2,1)}, u32[]{:S(2)}, u32[]{:S(2)}) collective-permute-start(bf16[2048,512]{1,0:T(8,128)(2,1)} %add_convert_fusion.3), channel_id=1, source_target_pairs={{0,4},{2,6},{4,0},{6,2},{1,5},{3,7},{5,1},{7,3},{8,12},{10,14},{12... | collective-permute-start | bytes 6291464 | tf_op jit(solution)/shard_map/ppermute | solution.py:164
  587.8 314.8 %reduce-scatter.10.cloned.1.call-start = ((), (), s32[]{:S(2)}) async-start(), calls=%async_computation.14 | async-start | bytes 5242880 | tf_op jit(solution)/shard_map/reduce_scatter | solution.py:172
  605.9 334.8 %reduce-scatter.6.cloned.1.call-start = ((), (), s32[]{:S(2)}) async-start(), calls=%async_computation.12 | async-start | bytes 2621440 | tf_op jit(solution)/shard_map/reduce_scatter | solution.py:172
  617.0 44.9 %collective-permute-start.69 = (bf16[2048,256]{1,0:T(8,128)(2,1)}, bf16[2048,256]{1,0:T(8,128)(2,1)}, u32[]{:S(2)}, u32[]{:S(2)}) collective-permute-start(bf16[2048,256]{1,0:T(8,128)(2,1)} %fusion.20), channel_id=1, source_target_pairs={{0,4},{2,6},{4,0},{6,2},{1,5},{3,7},{5,1},{7,3},{8,12},{10,14},{12... | collective-permute-start | bytes 3145736 | tf_op jit(solution)/shard_map/ppermute | solution.py:164
  638.4 45.6 %collective-permute-start.52 = (bf16[512,512]{1,0:T(8,128)(2,1)}, bf16[512,512]{1,0:T(8,128)(2,1)}, u32[]{:S(2)}, u32[]{:S(2)}) collective-permute-start(bf16[512,512]{1,0:T(8,128)(2,1)} %pad_maximum_fusion.5), channel_id=1, source_target_pairs={{0,4},{2,6},{4,0},{6,2},{1,5},{3,7},{5,1},{7,3},{8,12},{10,14},{12... | collective-permute-start | bytes 1572872 | tf_op jit(solution)/shard_map/ppermute | solution.py:164
  663.7 96.8 %collective-permute-start.58 = (bf16[2048,256]{1,0:T(8,128)(2,1)}, bf16[2048,256]{1,0:T(8,128)(2,1)}, u32[]{:S(2)}, u32[]{:S(2)}) collective-permute-start(bf16[2048,256]{1,0:T(8,128)(2,1)} %fusion.33), channel_id=1, source_target_pairs={{0,2},{2,0},{4,6},{6,4},{1,3},{3,1},{5,7},{7,5},{8,10},{10,8},{12,... | collective-permute-start | bytes 3145736 | tf_op jit(solution)/shard_map/ppermute | solution.py:164
  702.1 70.1 %collective-permute-start.85 = (bf16[512,512]{1,0:T(8,128)(2,1)}, bf16[512,512]{1,0:T(8,128)(2,1)S(1)}, u32[]{:S(2)}, u32[]{:S(2)}) collective-permute-start(bf16[512,512]{1,0:T(8,128)(2,1)} %reduce-scatter.12.cloned.1.call-done), channel_id=1, source_target_pairs={{0,2},{2,0},{4,6},{6,4},{1,3},{3,1},{5,7},{7,5},{8,10},{10,8},{12,... | collective-permute-start | bytes 1572872 | tf_op jit(solution)/shard_map/ppermute | solution.py:164
  706.7 91.2 %collective-permute-start.55 = (bf16[2048,512]{1,0:T(8,128)(2,1)}, bf16[2048,512]{1,0:T(8,128)(2,1)}, u32[]{:S(2)}, u32[]{:S(2)}) collective-permute-start(bf16[2048,512]{1,0:T(8,128)(2,1)} %fusion.9), channel_id=1, source_target_pairs={{0,4},{2,6},{4,0},{6,2},{1,5},{3,7},{5,1},{7,3},{8,12},{10,14},{12... | collective-permute-start | bytes 6291464 | tf_op jit(solution)/shard_map/ppermute | solution.py:164
  713.6 59.2 %collective-permute-start.84 = (bf16[512,512]{1,0:T(8,128)(2,1)S(1)}, bf16[512,512]{1,0:T(8,128)(2,1)S(1)}, u32[]{:S(2)}, u32[]{:S(2)}) collective-permute-start(bf16[512,512]{1,0:T(8,128)(2,1)S(1)} %collective-permute-done.83), channel_id=1, source_target_pairs={{0,2},{2,0},{4,6},{6,4},{1,3},{3,1},{5,7},{7,5},{8,10},{10,8},{12,... | collective-permute-start | bytes 1572872 | tf_op jit(solution)/shard_map/ppermute | solution.py:164
  720.0 39.0 %collective-permute-start.91 = (f32[152,128]{1,0:T(8,128)S(1)}, f32[152,128]{1,0:T(8,128)S(1)}, u32[]{:S(2)}, u32[]{:S(2)}) collective-permute-start(f32[152,128]{1,0:T(8,128)S(1)} %add.723), channel_id=1, source_target_pairs={{0,4},{2,6},{4,0},{6,2},{1,5},{3,7},{5,1},{7,3},{8,12},{10,14},{12... | collective-permute-start | bytes 233480 | tf_op jit(solution)/shard_map/ppermute | solution.py:164
  758.9 42.5 %collective-permute-start.70 = (bf16[512,256]{1,0:T(8,128)(2,1)}, bf16[512,256]{1,0:T(8,128)(2,1)}, u32[]{:S(2)}, u32[]{:S(2)}) collective-permute-start(bf16[512,256]{1,0:T(8,128)(2,1)} %get-tuple-element.192), channel_id=1, source_target_pairs={{0,8},{8,16},{16,24},{24,0},{1,9},{9,17},{17,25},{25,1},{2,10},{10... | collective-permute-start | bytes 786440 | tf_op jit(solution)/shard_map/ppermute | solution.py:185
  806.6 38.5 %collective-permute-start.75 = (bf16[512,256]{1,0:T(8,128)(2,1)S(1)}, bf16[512,256]{1,0:T(8,128)(2,1)}, u32[]{:S(2)}, u32[]{:S(2)}) collective-permute-start(bf16[512,256]{1,0:T(8,128)(2,1)S(1)} %add_convert_fusion.34), channel_id=1, source_target_pairs={{0,2},{2,0},{4,6},{6,4},{1,3},{3,1},{5,7},{7,5},{8,10},{10,8},{12,... | collective-permute-start | bytes 786440 | tf_op jit(solution)/shard_map/ppermute | solution.py:164
  806.6 42.0 %collective-permute-start.76 = (bf16[512,512]{1,0:T(8,128)(2,1)}, bf16[512,512]{1,0:T(8,128)(2,1)}, u32[]{:S(2)}, u32[]{:S(2)}) collective-permute-start(bf16[512,512]{1,0:T(8,128)(2,1)} %reduce-scatter.8.cloned.1.call-done), channel_id=1, source_target_pairs={{0,4},{2,6},{4,0},{6,2},{1,5},{3,7},{5,1},{7,3},{8,12},{10,14},{12... | collective-permute-start | bytes 1572872 | tf_op jit(solution)/shard_map/ppermute | solution.py:164
  845.5 58.4 %collective-permute-start.78 = (bf16[512,512]{1,0:T(8,128)(2,1)}, bf16[512,512]{1,0:T(8,128)(2,1)}, u32[]{:S(2)}, u32[]{:S(2)}) collective-permute-start(bf16[512,512]{1,0:T(8,128)(2,1)} %reduce-scatter.8.cloned.1.call-done), channel_id=1, source_target_pairs={{0,2},{2,0},{4,6},{6,4},{1,3},{3,1},{5,7},{7,5},{8,10},{10,8},{12,... | collective-permute-start | bytes 1572872 | tf_op jit(solution)/shard_map/ppermute | solution.py:164
  848.6 82.9 %collective-permute-start.56 = (bf16[512,2048]{1,0:T(8,128)(2,1)}, bf16[512,2048]{1,0:T(8,128)(2,1)}, u32[]{:S(2)}, u32[]{:S(2)}) collective-permute-start(bf16[512,2048]{1,0:T(8,128)(2,1)} %sum_products.7), channel_id=1, source_target_pairs={{0,1},{1,0},{2,3},{3,2},{4,5},{5,4},{6,7},{7,6},{8,9},{9,8},{10,11... | collective-permute-start | bytes 6291464 | tf_op jit(solution)/shard_map/ppermute | solution.py:164
  852.3 52.2 %collective-permute-start.77 = (bf16[512,512]{1,0:T(8,128)(2,1)}, bf16[512,512]{1,0:T(8,128)(2,1)}, u32[]{:S(2)}, u32[]{:S(2)}) collective-permute-start(bf16[512,512]{1,0:T(8,128)(2,1)} %collective-permute-done.76), channel_id=1, source_target_pairs={{0,2},{2,0},{4,6},{6,4},{1,3},{3,1},{5,7},{7,5},{8,10},{10,8},{12,... | collective-permute-start | bytes 1572872 | tf_op jit(solution)/shard_map/ppermute | solution.py:164
  (151 other events, 1949.1 us)
Sparse Core Ops, SparseCore 0:
  10.1 50.4 all-gather.9
  62.8 44.4 all-gather.7
  109.4 44.4 all-gather.11
  155.9 44.4 all-gather.13
  201.8 44.4 all-gather.15
  248.3 44.4 all-gather.17
  295.0 26.7 all-gather.19
  515.8 43.9 reduce-scatter.11
  562.2 75.9 reduce-scatter.13
  640.9 44.1 reduce-scatter.7
  687.4 75.9 reduce-scatter.9
  832.0 44.4 reduce-scatter.5

commit v3 on v2

--- a/solution.py
+++ b/solution.py
@@ -344,7 +344,7 @@
     down_swapped = across(after(down_own[1], activated[0])[:, :ff_part], 2)
     down_last = jnp.concatenate([down_swapped, after(down_far, *activated)], axis=1)
     down_w = [
-        spread(after(down_own[0], activated[0])),
+        spread(after(down_own[0], attn_low)),
         fill(down_own[1], down_last),
     ]
     mlp_low = sum_products(activated, [down_w[half][q] for half, q in pairs])
@@ -405,6 +405,7 @@
         for q in range(4)
     ]
     far_sums = [across(two_sums[q][local_rows:], 2) for q in range(4)]
+    far_sums = lax.optimization_barrier((*far_sums, *two_sums))[:4]
     grad_kv = [
         (two_sums[q][:local_rows].astype(F32) + far_sums[q ^ 2].astype(F32)).astype(BF)
         for q in range(4)
@@ -413,11 +414,12 @@
     query_early = near_sums([transposed_times(tokens, grad_q[q]).astype(BF) for q in range(4)])
     kv_parts = [transposed_times(tokens, grad_kv[q]).astype(BF) for q in range(4)]
     kv_early = near_sums(kv_parts)
-    kv_total = far_sum(*kv_early)
+    kv_got = across(kv_early[1], 2)
+    kv_total = (kv_early[0].astype(F32) + kv_got.astype(F32)).astype(BF)
     kv_mine = scatter(kv_total)
-    query_mine, query_got = scatter_direct(
-        far_sum(query_early[0], after(query_early[1], kv_total))
-    )
+    query_far = after(across(after(query_early[1], *grad_kv), 2), *kv_early)
+    query_total = (query_early[0].astype(F32) + query_far.astype(F32)).astype(BF)
+    query_mine, query_got = scatter_direct(query_total)
     output_mine, output_got = lax.optimization_barrier((*output_direct, kv_total))[:2]
     up_first, up_second, grad_q_then = (
         after(item, kv_total) for item in (up_first, up_second, grad_q[0])

time: 986 us -> 933 us (0.946)
  waiting for transfers between devices: 444 us -> 399 us
    ppermute x88, waiting for transfers between devices: 359 us -> 302 us  [across(): return lax.ppermute(array, axis, [(at, at ^ step) for at in range(size)])]
    all_gather x7, waiting for transfers between devices: 69.5 us -> 91.3 us  [collect(): return lax.all_gather(piece, 'shard', axis=0, tiled=True)]
    ppermute x6, waiting for transfers between devices: 14.2 us -> 4.2 us  [scatter_direct(): lax.ppermute(block(step), 'shard', [(at, (at + step) % size) for at in ra...]
  transfers between devices with their start and end apart: 106 -> 106, of which waited for: 30 -> 32; matrix products, arithmetic and copies ran while one was open for 31% -> 33% of each run, Pallas kernels for 10% -> 11%
where the time goes in v3:
time: 933 us; the launch traced here: 924 us
  waiting for transfers between devices  399 us (43%)
  matrix products  170 us (18%)
  other arithmetic  122 us (13%)
  Pallas kernels  113 us (12%)
  starting transfers between devices  59.8 us (6%)
  local copies, waits for them, and re-layouts  43.7 us (5%)
  between operations  16 us (2%)
    ppermute x88, waiting for transfers between devices, across(): return lax.ppermute(array, axis, [(at, at ^ step) for at in range(size)])  302 us
    dot_general x28, matrix products, product(): return jnp.dot(left, right, preferred_element_type=F32)  106 us
    all_gather x7, waiting for transfers between devices, collect(): return lax.all_gather(piece, 'shard', axis=0, tiled=True)  91.3 us
    dot_general x28, matrix products, transposed_times(): lax.dot_general(left, right, (((0,), (0,)), ((), ())), preferred_element_...  64.4 us
    ppermute x88, starting transfers between devices, across(): return lax.ppermute(array, axis, [(at, at ^ step) for at in range(size)])  53.1 us
    pallas_call x4, Pallas kernels, sum_products(): pl.pallas_call(sum_kernel, grid=(width // block,), in_specs=[pl.BlockSpec...  51.7 us
    pallas_call x4, Pallas kernels, attention_back(): pl.pallas_call(backward_kernel, grid=(heads, rows // block), in_specs=[ro...  35 us
    pallas_call x4, Pallas kernels, attention(): pl.pallas_call(forward_kernel, grid=(heads, rows // block), in_specs=[row...  26.1 us
  transfers between devices with their start and end apart: 106, of which 32 were waited for; matrix products, arithmetic and copies ran while one was open for 33% of the time, Pallas kernels for 11%

profile of v3, /device:TPU:0, one launch (start us, length us, event | category | flops | bytes accessed | tf_op | source)
XLA Modules:
  0.0 923.8 jit_solution(1941526992723271867)
XLA Ops:
  26.1 6.5 collective-permute-done.1
  33.8 7.7 collective-permute-done.2
  41.5 23.7 %collective-permute-done.3 = bf16[512,2048]{1,0:T(8,128)(2,1)} collective-permute-done((bf16[512,2048]{1,0:T(8,128)(2,1)S(1)}, bf16[512,2048]{1,0:T(8,128)(2,1)}, u32[]{:S(2)}, u32[]{:S(2)}) %collective-permute-start.3) | collective-permute-done | bytes 2097184 | tf_op jit(solution)/shard_map/ppermute | solution.py:164
  67.9 39.4 %all-gather.8.cloned.1.call-done = bf16[2048,512]{1,0:T(8,128)(2,1)} async-done(((bf16[512,512]{1,0:T(8,128)(2,1)}), bf16[2048,512]{1,0:T(8,128)(2,1)}) %all-gather.8.cloned.1.call-update) | async-done | bytes 2097168 | tf_op jit(solution)/shard_map/all_gather | solution.py:168
  108.8 5.5 add_convert_fusion.17.kh_ref.vh_ref
  120.6 4.6 add_convert_fusion.15.kh_ref.vh_ref
  125.2 28.8 %all-gather.12.cloned.1.call-done.refs_8_ = bf16[2048,512]{1,0:T(8,128)(2,1)} async-done(((bf16[512,512]{1,0:T(8,128)(2,1)}), bf16[2048,512]{1,0:T(8,128)(2,1)}) %all-gather.12.cloned.1.call-update) | async-done | bytes 2097168 | tf_op jit(solution)/shard_map/all_gather | solution.py:168
  158.8 5.5 add_convert_fusion.16.kh_ref.vh_ref
  173.5 6.9 attention_forward.5
  180.4 5.5 add_convert_fusion.14.kh_ref.vh_ref
  189.1 6.4 attention_forward.4
  198.1 6.4 attention_forward.7
  208.2 6.5 attention_forward.6
  214.6 8.3 sum_products.4
  228.6 18.3 %all-gather.16.cloned.1.call-done.refs_8_ = bf16[2048,512]{1,0:T(8,128)(2,1)} async-done(((bf16[512,512]{1,0:T(8,128)(2,1)}), bf16[2048,512]{1,0:T(8,128)(2,1)}) %all-gather.16.cloned.1.call-update) | async-done | bytes 2097168 | tf_op jit(solution)/shard_map/all_gather | solution.py:168
  246.9 5.6 collective-permute-done.19.refs_14_
  253.1 17.4 %collective-permute-done.14 = bf16[512,2048]{1,0:T(8,128)(2,1)} collective-permute-done((bf16[512,2048]{1,0:T(8,128)(2,1)}, bf16[512,2048]{1,0:T(8,128)(2,1)}, u32[]{:S(2)}, u32[]{:S(2)}) %collective-permute-start.14) | collective-permute-done | bytes 2097184 | tf_op jit(solution)/shard_map/ppermute | solution.py:164
  270.5 4.9 fusion.146
  288.6 4.8 all-gather.18.cloned.1.call-done.refs_12_
  300.4 5.1 multiply_convert_fusion.6
  314.7 9.0 collective-permute-done.25
  324.7 4.7 multiply_convert_fusion
  336.1 15.2 %sum_products.5 = bf16[512,2048]{1,0:T(8,128)(2,1)} custom-call(bf16[512,512]{1,0:T(8,128)(2,1)} %get-tuple-element.247.refs_0_, bf16[512,512]{1,0:T(8,128)(2,1)} %get-tuple-element.249.refs_1_, bf16[512,512]{1,0:T(8,128)(2,1)} %get-tuple-element.251.refs_2_, bf16[512,512]{1,0:T(8,128)(2,1)} %get-tuple-element.253.refs_3_, ...), custom_call_target="tpu_custom_call" | custom-call | tf_op jit(solution)/shard_map/sum_products/pallas_call | solution.py:147
  353.1 46.2 %collective-permute-done.27 = bf16[512,2048]{1,0:T(8,128)(2,1)S(1)} collective-permute-done((bf16[512,2048]{1,0:T(8,128)(2,1)}, bf16[512,2048]{1,0:T(8,128)(2,1)S(1)}, u32[]{:S(2)}, u32[]{:S(2)}) %collective-permute-start.27) | collective-permute-done | bytes 2097184 | tf_op jit(solution)/shard_map/ppermute | solution.py:164
  399.3 4.7 fusion.144
  429.9 5.0 add_convert_fusion.9
  466.2 15.2 %sum_products.6 = bf16[512,2048]{1,0:T(8,128)(2,1)} custom-call(bf16[512,512]{1,0:T(8,128)(2,1)} %get-tuple-element.145.refs_0_, bf16[512,512]{1,0:T(8,128)(2,1)} %get-tuple-element.149.refs_1_, bf16[512,512]{1,0:T(8,128)(2,1)} %get-tuple-element.153.refs_2_, bf16[512,512]{1,0:T(8,128)(2,1)} %get-tuple-element.157.refs_3_, ...), custom_call_target="tpu_custom_call" | custom-call | tf_op jit(solution)/shard_map/sum_products/pallas_call | solution.py:147
  513.9 20.6 %collective-permute-done.32 = bf16[512,2048]{1,0:T(8,128)(2,1)} collective-permute-done((bf16[512,2048]{1,0:T(8,128)(2,1)}, bf16[512,2048]{1,0:T(8,128)(2,1)}, u32[]{:S(2)}, u32[]{:S(2)}) %collective-permute-start.32) | collective-permute-done | bytes 2097184 | tf_op jit(solution)/shard_map/ppermute | solution.py:164
  534.5 8.5 multiply_reduce_fusion.3
  546.6 7.5 collective-permute-done.46
  567.4 8.6 attention_backward.4
  591.4 9.0 attention_backward.5
  610.7 8.6 attention_backward.7
  620.0 8.8 attention_backward.6
  640.8 5.7 collective-permute-done.42
  646.5 11.2 %collective-permute-done.49 = bf16[512,512]{1,0:T(8,128)(2,1)S(1)} collective-permute-done((bf16[512,512]{1,0:T(8,128)(2,1)S(1)}, bf16[512,512]{1,0:T(8,128)(2,1)S(1)}, u32[]{:S(2)}, u32[]{:S(2)}) %collective-permute-start.49) | collective-permute-done | bytes 524320 | tf_op jit(solution)/shard_map/ppermute | solution.py:164
  657.7 10.7 %collective-permute-done.52 = bf16[512,512]{1,0:T(8,128)(2,1)S(1)} collective-permute-done((bf16[512,512]{1,0:T(8,128)(2,1)S(1)}, bf16[512,512]{1,0:T(8,128)(2,1)S(1)}, u32[]{:S(2)}, u32[]{:S(2)}) %collective-permute-start.52) | collective-permute-done | bytes 524320 | tf_op jit(solution)/shard_map/ppermute | solution.py:164
  685.1 9.1 collective-permute-done.83
  704.2 12.6 %collective-permute-done.59 = bf16[2048,256]{1,0:T(8,128)(2,1)} collective-permute-done((bf16[2048,256]{1,0:T(8,128)(2,1)}, bf16[2048,256]{1,0:T(8,128)(2,1)}, u32[]{:S(2)}, u32[]{:S(2)}) %collective-permute-start.59) | collective-permute-done | bytes 1048608 | tf_op jit(solution)/shard_map/ppermute | solution.py:164
  722.0 40.8 %collective-permute-done.91 = f32[152,128]{1,0:T(8,128)S(1)} collective-permute-done((f32[152,128]{1,0:T(8,128)S(1)}, f32[152,128]{1,0:T(8,128)S(1)}, u32[]{:S(2)}, u32[]{:S(2)}) %collective-permute-start.91) | collective-permute-done | bytes 77856 | tf_op jit(solution)/shard_map/ppermute | solution.py:164
  767.7 9.2 collective-permute-done.92
  798.6 9.0 collective-permute-done.88
  807.6 10.8 %collective-permute-done.86 = bf16[512,512]{1,0:T(8,128)(2,1)S(1)} collective-permute-done((bf16[512,512]{1,0:T(8,128)(2,1)S(1)}, bf16[512,512]{1,0:T(8,128)(2,1)S(1)}, u32[]{:S(2)}, u32[]{:S(2)}) %collective-permute-start.86) | collective-permute-done | bytes 524320 | tf_op jit(solution)/shard_map/ppermute | solution.py:164
  826.2 13.0 %sum_products.7 = bf16[512,2048]{1,0:T(8,128)(2,1)} custom-call(bf16[512,256]{1,0:T(8,128)(2,1)} %get-tuple-element.117.refs_0_, bf16[512,256]{1,0:T(8,128)(2,1)} %get-tuple-element.118.refs_1_, bf16[512,256]{1,0:T(8,128)(2,1)} %get-tuple-element.119.refs_2_, bf16[512,256]{1,0:T(8,128)(2,1)} %get-tuple-element.120.refs_3_, ...), custom_call_target="tpu_custom_call" | custom-call | tf_op jit(solution)/shard_map/sum_products/pallas_call | solution.py:147
  854.3 6.8 convert_element_type.931
  863.8 10.5 %collective-permute-done.79 = bf16[512,512]{1,0:T(8,128)(2,1)S(1)} collective-permute-done((bf16[512,512]{1,0:T(8,128)(2,1)S(1)}, bf16[512,512]{1,0:T(8,128)(2,1)S(1)}, u32[]{:S(2)}, u32[]{:S(2)}) %collective-permute-start.79) | collective-permute-done | bytes 524320 | tf_op jit(solution)/shard_map/ppermute | solution.py:164
  891.5 6.8 convert_element_type.924
  900.8 8.5 collective-permute-done.56
  (623 shorter events, 353.6 us)
Async XLA Ops:
  7.2 58.1 %all-gather.10.cloned.1.call-start = ((), (), s32[]{:S(2)}) async-start(), calls=%async_computation.6 | async-start | bytes 2621440 | tf_op jit(solution)/shard_map/all_gather | solution.py:168
  9.2 98.1 %all-gather.8.cloned.1.call-start = ((), (), s32[]{:S(2)}) async-start(), calls=%async_computation.5 | async-start | bytes 2621440 | tf_op jit(solution)/shard_map/all_gather | solution.py:168
  11.2 142.8 %all-gather.12.cloned.1.call-start = ((), (), s32[]{:S(2)}) async-start(), calls=%async_computation.7 | async-start | bytes 2621440 | tf_op jit(solution)/shard_map/all_gather | solution.py:168
  13.5 191.0 %all-gather.14.cloned.1.call-start = ((), (), s32[]{:S(2)}) async-start(), calls=%async_computation.8 | async-start | bytes 2621440 | tf_op jit(solution)/shard_map/all_gather | solution.py:168
  14.1 232.8 %all-gather.16.cloned.1.call-start = ((), (), s32[]{:S(2)}) async-start(), calls=%async_computation.9 | async-start | bytes 2621440 | tf_op jit(solution)/shard_map/all_gather | solution.py:168
  16.4 277.0 %all-gather.18.cloned.1.call-start = ((), (), s32[]{:S(2)}) async-start(), calls=%async_computation.10 | async-start | bytes 2621440 | tf_op jit(solution)/shard_map/all_gather | solution.py:168
  16.5 48.8 %collective-permute-start.3 = (bf16[512,2048]{1,0:T(8,128)(2,1)S(1)}, bf16[512,2048]{1,0:T(8,128)(2,1)}, u32[]{:S(2)}, u32[]{:S(2)}) collective-permute-start(bf16[512,2048]{1,0:T(8,128)(2,1)S(1)} %bitcast.266), channel_id=1, source_target_pairs={{0,4},{2,6},{4,0},{6,2},{1,5},{3,7},{5,1},{7,3},{8,12},{10,14},{12... | collective-permute-start | bytes 6291464 | tf_op jit(solution)/shard_map/ppermute | solution.py:164
  21.7 307.7 %all-gather.20.cloned.1.call-start = ((), (), s32[]{:S(2)}) async-start(), calls=%async_computation.11 | async-start | bytes 1310720 | tf_op jit(solution)/shard_map/all_gather | solution.py:168
  65.2 55.3 %collective-permute-start.9 = (bf16[2048,512]{1,0:T(8,128)(2,1)}, bf16[2048,512]{1,0:T(8,128)(2,1)}, u32[]{:S(2)}, u32[]{:S(2)}) collective-permute-start(bf16[2048,512]{1,0:T(8,128)(2,1)} %all-gather.10.cloned.1.call-done.refs_12_), channel_id=1, source_target_pairs={{0,4},{2,6},{4,0},{6,2},{1,5},{3,7},{5,1},{7,3},{8,12},{10,14},{12... | collective-permute-start | bytes 6291464 | tf_op jit(solution)/shard_map/ppermute | solution.py:164
  67.9 90.9 %collective-permute-start.4 = (bf16[2048,512]{1,0:T(8,128)(2,1)}, bf16[2048,512]{1,0:T(8,128)(2,1)}, u32[]{:S(2)}, u32[]{:S(2)}) collective-permute-start(bf16[2048,512]{1,0:T(8,128)(2,1)} %all-gather.10.cloned.1.call-done.refs_12_), channel_id=1, source_target_pairs={{0,2},{2,0},{4,6},{6,4},{1,3},{3,1},{5,7},{7,5},{8,10},{10,8},{12,... | collective-permute-start | bytes 6291464 | tf_op jit(solution)/shard_map/ppermute | solution.py:164
  107.3 50.0 %collective-permute-start.8 = (bf16[2048,512]{1,0:T(8,128)(2,1)}, bf16[2048,512]{1,0:T(8,128)(2,1)}, u32[]{:S(2)}, u32[]{:S(2)}) collective-permute-start(bf16[2048,512]{1,0:T(8,128)(2,1)} %all-gather.8.cloned.1.call-done), channel_id=1, source_target_pairs={{0,4},{2,6},{4,0},{6,2},{1,5},{3,7},{5,1},{7,3},{8,12},{10,14},{12... | collective-permute-start | bytes 6291464 | tf_op jit(solution)/shard_map/ppermute | solution.py:164
  114.4 59.1 %collective-permute-start.7 = (bf16[1024,512]{1,0:T(8,128)(2,1)}, bf16[1024,512]{1,0:T(8,128)(2,1)}, u32[]{:S(2)}, u32[]{:S(2)}) collective-permute-start(bf16[1024,512]{1,0:T(8,128)(2,1)} %add_convert_fusion.17.kh_ref.vh_ref), channel_id=1, source_target_pairs={{0,2},{2,0},{4,6},{6,4},{1,3},{3,1},{5,7},{7,5},{8,10},{10,8},{12,... | collective-permute-start | bytes 3145736 | tf_op jit(solution)/shard_map/ppermute | solution.py:164
  114.4 52.9 %collective-permute-start.6 = (bf16[2048,512]{1,0:T(8,128)(2,1)}, bf16[2048,512]{1,0:T(8,128)(2,1)}, u32[]{:S(2)}, u32[]{:S(2)}) collective-permute-start(bf16[2048,512]{1,0:T(8,128)(2,1)} %all-gather.8.cloned.1.call-done), channel_id=1, source_target_pairs={{0,2},{2,0},{4,6},{6,4},{1,3},{3,1},{5,7},{7,5},{8,10},{10,8},{12,... | collective-permute-start | bytes 6291464 | tf_op jit(solution)/shard_map/ppermute | solution.py:164
  120.6 59.8 %collective-permute-start.10 = (bf16[2048,512]{1,0:T(8,128)(2,1)}, bf16[2048,512]{1,0:T(8,128)(2,1)}, u32[]{:S(2)}, u32[]{:S(2)}) collective-permute-start(bf16[2048,512]{1,0:T(8,128)(2,1)} %collective-permute-done.9.refs_14_), channel_id=1, source_target_pairs={{0,2},{2,0},{4,6},{6,4},{1,3},{3,1},{5,7},{7,5},{8,10},{10,8},{12,... | collective-permute-start | bytes 6291464 | tf_op jit(solution)/shard_map/ppermute | solution.py:164
  157.3 70.8 %collective-permute-start.16 = (bf16[2048,512]{1,0:T(8,128)(2,1)}, bf16[2048,512]{1,0:T(8,128)(2,1)}, u32[]{:S(2)}, u32[]{:S(2)}) collective-permute-start(bf16[2048,512]{1,0:T(8,128)(2,1)} %all-gather.12.cloned.1.call-done.refs_8_), channel_id=1, source_target_pairs={{0,4},{2,6},{4,0},{6,2},{1,5},{3,7},{5,1},{7,3},{8,12},{10,14},{12... | collective-permute-start | bytes 6291464 | tf_op jit(solution)/shard_map/ppermute | solution.py:164
  158.7 36.7 %collective-permute-start.12 = (bf16[2048,512]{1,0:T(8,128)(2,1)}, bf16[2048,512]{1,0:T(8,128)(2,1)}, u32[]{:S(2)}, u32[]{:S(2)}) collective-permute-start(bf16[2048,512]{1,0:T(8,128)(2,1)} %collective-permute-done.8), channel_id=1, source_target_pairs={{0,2},{2,0},{4,6},{6,4},{1,3},{3,1},{5,7},{7,5},{8,10},{10,8},{12,... | collective-permute-start | bytes 6291464 | tf_op jit(solution)/shard_map/ppermute | solution.py:164
  204.5 48.0 %collective-permute-start.19 = (bf16[2048,512]{1,0:T(8,128)(2,1)}, bf16[2048,512]{1,0:T(8,128)(2,1)}, u32[]{:S(2)}, u32[]{:S(2)}) collective-permute-start(bf16[2048,512]{1,0:T(8,128)(2,1)} %all-gather.14.cloned.1.call-done.refs_12_), channel_id=1, source_target_pairs={{0,4},{2,6},{4,0},{6,2},{1,5},{3,7},{5,1},{7,3},{8,12},{10,14},{12... | collective-permute-start | bytes 6291464 | tf_op jit(solution)/shard_map/ppermute | solution.py:164
  222.9 47.6 %collective-permute-start.14 = (bf16[512,2048]{1,0:T(8,128)(2,1)}, bf16[512,2048]{1,0:T(8,128)(2,1)}, u32[]{:S(2)}, u32[]{:S(2)}) collective-permute-start(bf16[512,2048]{1,0:T(8,128)(2,1)} %sum_products.4), channel_id=1, source_target_pairs={{0,1},{1,0},{2,3},{3,2},{4,5},{5,4},{6,7},{7,6},{8,9},{9,8},{10,11... | collective-permute-start | bytes 6291464 | tf_op jit(solution)/shard_map/ppermute | solution.py:164
  226.2 453.1 %reduce-scatter.12.cloned.1.call-start = ((), (), s32[]{:S(2)}) async-start(), calls=%async_computation.15 | async-start | bytes 2621440 | tf_op jit(solution)/shard_map/reduce_scatter | solution.py:172
  228.0 70.9 %collective-permute-start.15 = (bf16[2048,512]{1,0:T(8,128)(2,1)}, bf16[2048,512]{1,0:T(8,128)(2,1)}, u32[]{:S(2)}, u32[]{:S(2)}) collective-permute-start(bf16[2048,512]{1,0:T(8,128)(2,1)} %all-gather.12.cloned.1.call-done.refs_8_), channel_id=1, source_target_pairs={{0,2},{2,0},{4,6},{6,4},{1,3},{3,1},{5,7},{7,5},{8,10},{10,8},{12,... | collective-permute-start | bytes 6291464 | tf_op jit(solution)/shard_map/ppermute | solution.py:164
  228.1 77.4 %collective-permute-start.17 = (bf16[2048,512]{1,0:T(8,128)(2,1)}, bf16[2048,512]{1,0:T(8,128)(2,1)}, u32[]{:S(2)}, u32[]{:S(2)}) collective-permute-start(bf16[2048,512]{1,0:T(8,128)(2,1)} %collective-permute-done.16.refs_10_), channel_id=1, source_target_pairs={{0,2},{2,0},{4,6},{6,4},{1,3},{3,1},{5,7},{7,5},{8,10},{10,8},{12,... | collective-permute-start | bytes 6291464 | tf_op jit(solution)/shard_map/ppermute | solution.py:164
  228.6 81.2 %collective-permute-start.18 = (bf16[2048,512]{1,0:T(8,128)(2,1)}, bf16[2048,512]{1,0:T(8,128)(2,1)}, u32[]{:S(2)}, u32[]{:S(2)}) collective-permute-start(bf16[2048,512]{1,0:T(8,128)(2,1)} %all-gather.14.cloned.1.call-done.refs_12_), channel_id=1, source_target_pairs={{0,2},{2,0},{4,6},{6,4},{1,3},{3,1},{5,7},{7,5},{8,10},{10,8},{12,... | collective-permute-start | bytes 6291464 | tf_op jit(solution)/shard_map/ppermute | solution.py:164
  252.5 57.8 %collective-permute-start.22 = (bf16[2048,512]{1,0:T(8,128)(2,1)}, bf16[2048,512]{1,0:T(8,128)(2,1)}, u32[]{:S(2)}, u32[]{:S(2)}) collective-permute-start(bf16[2048,512]{1,0:T(8,128)(2,1)} %all-gather.16.cloned.1.call-done.refs_8_), channel_id=1, source_target_pairs={{0,4},{2,6},{4,0},{6,2},{1,5},{3,7},{5,1},{7,3},{8,12},{10,14},{12... | collective-permute-start | bytes 6291464 | tf_op jit(solution)/shard_map/ppermute | solution.py:164
  270.5 54.2 %collective-permute-start.20 = (bf16[2048,512]{1,0:T(8,128)(2,1)}, bf16[2048,512]{1,0:T(8,128)(2,1)}, u32[]{:S(2)}, u32[]{:S(2)}) collective-permute-start(bf16[2048,512]{1,0:T(8,128)(2,1)} %collective-permute-done.19.refs_14_), channel_id=1, source_target_pairs={{0,2},{2,0},{4,6},{6,4},{1,3},{3,1},{5,7},{7,5},{8,10},{10,8},{12,... | collective-permute-start | bytes 6291464 | tf_op jit(solution)/shard_map/ppermute | solution.py:164
  351.3 47.9 %collective-permute-start.27 = (bf16[512,2048]{1,0:T(8,128)(2,1)}, bf16[512,2048]{1,0:T(8,128)(2,1)S(1)}, u32[]{:S(2)}, u32[]{:S(2)}) collective-permute-start(bf16[512,2048]{1,0:T(8,128)(2,1)} %sum_products.5), channel_id=1, source_target_pairs={{0,1},{1,0},{2,3},{3,2},{4,5},{5,4},{6,7},{7,6},{8,9},{9,8},{10,11... | collective-permute-start | bytes 6291464 | tf_op jit(solution)/shard_map/ppermute | solution.py:164
  422.8 58.6 %collective-permute-start.33 = (bf16[2048,512]{1,0:T(8,128)(2,1)}, bf16[2048,512]{1,0:T(8,128)(2,1)}, u32[]{:S(2)}, u32[]{:S(2)}) collective-permute-start(bf16[2048,512]{1,0:T(8,128)(2,1)} %add_convert_fusion.8), channel_id=1, source_target_pairs={{0,4},{2,6},{4,0},{6,2},{1,5},{3,7},{5,1},{7,3},{8,12},{10,14},{12... | collective-permute-start | bytes 6291464 | tf_op jit(solution)/shard_map/ppermute | solution.py:164
  485.6 305.9 %reduce-scatter.14.cloned.1.call-start = ((), (), s32[]{:S(2)}) async-start(), calls=%async_computation.16 | async-start | bytes 5242880 | tf_op jit(solution)/shard_map/reduce_scatter | solution.py:172
  486.3 338.3 %reduce-scatter.8.cloned.1.call-start = ((), (), s32[]{:S(2)}) async-start(), calls=%async_computation.13 | async-start | bytes 2621440 | tf_op jit(solution)/shard_map/reduce_scatter | solution.py:172
  486.9 47.6 %collective-permute-start.32 = (bf16[512,2048]{1,0:T(8,128)(2,1)}, bf16[512,2048]{1,0:T(8,128)(2,1)}, u32[]{:S(2)}, u32[]{:S(2)}) collective-permute-start(bf16[512,2048]{1,0:T(8,128)(2,1)} %sum_products.6), channel_id=1, source_target_pairs={{0,1},{1,0},{2,3},{3,2},{4,5},{5,4},{6,7},{7,6},{8,9},{9,8},{10,11... | collective-permute-start | bytes 6291464 | tf_op jit(solution)/shard_map/ppermute | solution.py:164
  506.2 47.9 %collective-permute-start.46 = (bf16[2048,512]{1,0:T(8,128)(2,1)}, bf16[2048,512]{1,0:T(8,128)(2,1)}, u32[]{:S(2)}, u32[]{:S(2)}) collective-permute-start(bf16[2048,512]{1,0:T(8,128)(2,1)} %add_convert_fusion.3), channel_id=1, source_target_pairs={{0,4},{2,6},{4,0},{6,2},{1,5},{3,7},{5,1},{7,3},{8,12},{10,14},{12... | collective-permute-start | bytes 6291464 | tf_op jit(solution)/shard_map/ppermute | solution.py:164
  557.6 290.1 %reduce-scatter.10.cloned.1.call-start = ((), (), s32[]{:S(2)}) async-start(), calls=%async_computation.14 | async-start | bytes 5242880 | tf_op jit(solution)/shard_map/reduce_scatter | solution.py:172
  576.6 309.4 %reduce-scatter.6.cloned.1.call-start = ((), (), s32[]{:S(2)}) async-start(), calls=%async_computation.12 | async-start | bytes 2621440 | tf_op jit(solution)/shard_map/reduce_scatter | solution.py:172
  587.8 43.8 %collective-permute-start.69 = (bf16[2048,256]{1,0:T(8,128)(2,1)}, bf16[2048,256]{1,0:T(8,128)(2,1)}, u32[]{:S(2)}, u32[]{:S(2)}) collective-permute-start(bf16[2048,256]{1,0:T(8,128)(2,1)} %fusion.20), channel_id=1, source_target_pairs={{0,4},{2,6},{4,0},{6,2},{1,5},{3,7},{5,1},{7,3},{8,12},{10,14},{12... | collective-permute-start | bytes 3145736 | tf_op jit(solution)/shard_map/ppermute | solution.py:164
  605.4 35.4 %collective-permute-start.45 = (bf16[512,512]{1,0:T(8,128)(2,1)}, bf16[512,512]{1,0:T(8,128)(2,1)}, u32[]{:S(2)}, u32[]{:S(2)}) collective-permute-start(bf16[512,512]{1,0:T(8,128)(2,1)} %fusion.104), channel_id=1, source_target_pairs={{0,4},{2,6},{4,0},{6,2},{1,5},{3,7},{5,1},{7,3},{8,12},{10,14},{12... | collective-permute-start | bytes 1572872 | tf_op jit(solution)/shard_map/ppermute | solution.py:164
  608.7 108.1 %collective-permute-start.57 = (bf16[2048,256]{1,0:T(8,128)(2,1)}, bf16[2048,256]{1,0:T(8,128)(2,1)}, u32[]{:S(2)}, u32[]{:S(2)}) collective-permute-start(bf16[2048,256]{1,0:T(8,128)(2,1)} %fusion.32), channel_id=1, source_target_pairs={{0,2},{2,0},{4,6},{6,4},{1,3},{3,1},{5,7},{7,5},{8,10},{10,8},{12,... | collective-permute-start | bytes 3145736 | tf_op jit(solution)/shard_map/ppermute | solution.py:164
  637.3 31.1 %collective-permute-start.52 = (bf16[512,512]{1,0:T(8,128)(2,1)S(1)}, bf16[512,512]{1,0:T(8,128)(2,1)S(1)}, u32[]{:S(2)}, u32[]{:S(2)}) collective-permute-start(bf16[512,512]{1,0:T(8,128)(2,1)S(1)} %fusion.100), channel_id=1, source_target_pairs={{0,4},{2,6},{4,0},{6,2},{1,5},{3,7},{5,1},{7,3},{8,12},{10,14},{12... | collective-permute-start | bytes 1572872 | tf_op jit(solution)/shard_map/ppermute | solution.py:164
  640.8 36.5 %collective-permute-start.58 = (bf16[2048,256]{1,0:T(8,128)(2,1)S(1)}, bf16[2048,256]{1,0:T(8,128)(2,1)S(1)}, u32[]{:S(2)}, u32[]{:S(2)}) collective-permute-start(bf16[2048,256]{1,0:T(8,128)(2,1)S(1)} %fusion.33), channel_id=1, source_target_pairs={{0,2},{2,0},{4,6},{6,4},{1,3},{3,1},{5,7},{7,5},{8,10},{10,8},{12,... | collective-permute-start | bytes 3145736 | tf_op jit(solution)/shard_map/ppermute | solution.py:164
  679.9 36.9 %collective-permute-start.59 = (bf16[2048,256]{1,0:T(8,128)(2,1)}, bf16[2048,256]{1,0:T(8,128)(2,1)}, u32[]{:S(2)}, u32[]{:S(2)}) collective-permute-start(bf16[2048,256]{1,0:T(8,128)(2,1)} %fusion.31), channel_id=1, source_target_pairs={{0,4},{2,6},{4,0},{6,2},{1,5},{3,7},{5,1},{7,3},{8,12},{10,14},{12... | collective-permute-start | bytes 3145736 | tf_op jit(solution)/shard_map/ppermute | solution.py:164
  694.2 69.9 %collective-permute-start.85 = (bf16[512,512]{1,0:T(8,128)(2,1)}, bf16[512,512]{1,0:T(8,128)(2,1)S(1)}, u32[]{:S(2)}, u32[]{:S(2)}) collective-permute-start(bf16[512,512]{1,0:T(8,128)(2,1)} %reduce-scatter.12.cloned.1.call-done), channel_id=1, source_target_pairs={{0,2},{2,0},{4,6},{6,4},{1,3},{3,1},{5,7},{7,5},{8,10},{10,8},{12,... | collective-permute-start | bytes 1572872 | tf_op jit(solution)/shard_map/ppermute | solution.py:164
  694.2 70.9 %collective-permute-start.84 = (bf16[512,512]{1,0:T(8,128)(2,1)S(1)}, bf16[512,512]{1,0:T(8,128)(2,1)S(1)}, u32[]{:S(2)}, u32[]{:S(2)}) collective-permute-start(bf16[512,512]{1,0:T(8,128)(2,1)S(1)} %collective-permute-done.83), channel_id=1, source_target_pairs={{0,2},{2,0},{4,6},{6,4},{1,3},{3,1},{5,7},{7,5},{8,10},{10,8},{12,... | collective-permute-start | bytes 1572872 | tf_op jit(solution)/shard_map/ppermute | solution.py:164
  699.3 119.5 %collective-permute-start.55 = (bf16[2048,512]{1,0:T(8,128)(2,1)}, bf16[2048,512]{1,0:T(8,128)(2,1)}, u32[]{:S(2)}, u32[]{:S(2)}) collective-permute-start(bf16[2048,512]{1,0:T(8,128)(2,1)} %fusion.9), channel_id=1, source_target_pairs={{0,4},{2,6},{4,0},{6,2},{1,5},{3,7},{5,1},{7,3},{8,12},{10,14},{12... | collective-permute-start | bytes 6291464 | tf_op jit(solution)/shard_map/ppermute | solution.py:164
  719.4 43.4 %collective-permute-start.91 = (f32[152,128]{1,0:T(8,128)S(1)}, f32[152,128]{1,0:T(8,128)S(1)}, u32[]{:S(2)}, u32[]{:S(2)}) collective-permute-start(f32[152,128]{1,0:T(8,128)S(1)} %add.723), channel_id=1, source_target_pairs={{0,4},{2,6},{4,0},{6,2},{1,5},{3,7},{5,1},{7,3},{8,12},{10,14},{12... | collective-permute-start | bytes 233480 | tf_op jit(solution)/shard_map/ppermute | solution.py:164
  720.2 58.8 %collective-permute-start.62 = (bf16[512,256]{1,0:T(8,128)(2,1)S(1)}, bf16[512,256]{1,0:T(8,128)(2,1)S(1)}, u32[]{:S(2)}, u32[]{:S(2)}) collective-permute-start(bf16[512,256]{1,0:T(8,128)(2,1)S(1)} %get-tuple-element.209), channel_id=1, source_target_pairs={{0,24},{8,0},{16,8},{24,16},{1,25},{9,1},{17,9},{25,17},{2,26},{10... | collective-permute-start | bytes 786440 | tf_op jit(solution)/shard_map/ppermute | solution.py:185
  795.5 27.3 %collective-permute-start.70 = (bf16[512,256]{1,0:T(8,128)(2,1)}, bf16[512,256]{1,0:T(8,128)(2,1)}, u32[]{:S(2)}, u32[]{:S(2)}) collective-permute-start(bf16[512,256]{1,0:T(8,128)(2,1)} %get-tuple-element.202), channel_id=1, source_target_pairs={{0,8},{8,16},{16,24},{24,0},{1,9},{9,17},{17,25},{25,1},{2,10},{10... | collective-permute-start | bytes 786440 | tf_op jit(solution)/shard_map/ppermute | solution.py:185
  824.0 37.1 %collective-permute-start.73 = (bf16[512,256]{1,0:T(8,128)(2,1)S(1)}, bf16[512,256]{1,0:T(8,128)(2,1)}, u32[]{:S(2)}, u32[]{:S(2)}) collective-permute-start(bf16[512,256]{1,0:T(8,128)(2,1)S(1)} %add_convert_fusion.34), channel_id=1, source_target_pairs={{0,4},{2,6},{4,0},{6,2},{1,5},{3,7},{5,1},{7,3},{8,12},{10,14},{12... | collective-permute-start | bytes 786440 | tf_op jit(solution)/shard_map/ppermute | solution.py:164
  824.5 50.1 %collective-permute-start.75 = (bf16[512,256]{1,0:T(8,128)(2,1)S(1)}, bf16[512,256]{1,0:T(8,128)(2,1)}, u32[]{:S(2)}, u32[]{:S(2)}) collective-permute-start(bf16[512,256]{1,0:T(8,128)(2,1)S(1)} %add_convert_fusion.34), channel_id=1, source_target_pairs={{0,2},{2,0},{4,6},{6,4},{1,3},{3,1},{5,7},{7,5},{8,10},{10,8},{12,... | collective-permute-start | bytes 786440 | tf_op jit(solution)/shard_map/ppermute | solution.py:164
  824.6 36.5 %collective-permute-start.76 = (bf16[512,512]{1,0:T(8,128)(2,1)}, bf16[512,512]{1,0:T(8,128)(2,1)}, u32[]{:S(2)}, u32[]{:S(2)}) collective-permute-start(bf16[512,512]{1,0:T(8,128)(2,1)} %reduce-scatter.8.cloned.1.call-done), channel_id=1, source_target_pairs={{0,4},{2,6},{4,0},{6,2},{1,5},{3,7},{5,1},{7,3},{8,12},{10,14},{12... | collective-permute-start | bytes 1572872 | tf_op jit(solution)/shard_map/ppermute | solution.py:164
  861.1 48.1 %collective-permute-start.56 = (bf16[512,2048]{1,0:T(8,128)(2,1)S(1)}, bf16[512,2048]{1,0:T(8,128)(2,1)}, u32[]{:S(2)}, u32[]{:S(2)}) collective-permute-start(bf16[512,2048]{1,0:T(8,128)(2,1)S(1)} %copy-done.8), channel_id=1, source_target_pairs={{0,1},{1,0},{2,3},{3,2},{4,5},{5,4},{6,7},{7,6},{8,9},{9,8},{10,11... | collective-permute-start | bytes 6291464 | tf_op jit(solution)/shard_map/ppermute | solution.py:164
  (154 other events, 1848.5 us)
Sparse Core Ops, SparseCore 0:
  10.1 50.4 all-gather.9
  62.8 44.4 all-gather.7
  109.4 44.4 all-gather.11
  155.9 44.4 all-gather.13
  202.4 44.4 all-gather.15
  248.9 44.4 all-gather.17
  295.5 26.7 all-gather.19
  485.7 42.1 reduce-scatter.11
  530.2 75.9 reduce-scatter.13
  608.9 44.1 reduce-scatter.7
  655.4 81.4 reduce-scatter.9
  824.7 42.0 reduce-scatter.5

commit v4 on v3

--- a/solution.py
+++ b/solution.py
@@ -341,11 +341,12 @@
     up_rows = up_vector.reshape(4, 2, ff_half)
     pre_act = [product(hidden_low, up_w[half][q]) + up_rows[q, half] for half, q in pairs]
     activated = [gelu_tanh(item).astype(BF) for item in pre_act]
-    down_swapped = across(after(down_own[1], activated[0])[:, :ff_part], 2)
+    down_held = after(down_own[1], activated[0])
+    down_swapped = across(down_held[:, :ff_part], 2)
     down_last = jnp.concatenate([down_swapped, after(down_far, *activated)], axis=1)
     down_w = [
         spread(after(down_own[0], attn_low)),
-        fill(down_own[1], down_last),
+        fill(down_held, down_last),
     ]
     mlp_low = sum_products(activated, [down_w[half][q] for half, q in pairs])
     mlp_branch = tp_sum(mlp_low) + biases[2]
@@ -417,7 +418,7 @@
     kv_got = across(kv_early[1], 2)
     kv_total = (kv_early[0].astype(F32) + kv_got.astype(F32)).astype(BF)
     kv_mine = scatter(kv_total)
-    query_far = after(across(after(query_early[1], *grad_kv), 2), *kv_early)
+    query_far = across(after(query_early[1], kv_total), 2)
     query_total = (query_early[0].astype(F32) + query_far.astype(F32)).astype(BF)
     query_mine, query_got = scatter_direct(query_total)
     output_mine, output_got = lax.optimization_barrier((*output_direct, kv_total))[:2]

time: 933 us -> 922 us (0.988)
  waiting for transfers between devices: 399 us -> 378 us
    ppermute x88, waiting for transfers between devices: 302 us -> 274 us  [across(): return lax.ppermute(array, axis, [(at, at ^ step) for at in range(size)])]
  transfers between devices with their start and end apart: 106 -> 106, of which waited for: 32 -> 32; matrix products, arithmetic and copies ran while one was open for 33% -> 35% of each run, Pallas kernels for 11% -> 11%
where the time goes in v4:
time: 922 us; the launch traced here: 912 us
  waiting for transfers between devices  378 us (41%)
  matrix products  172 us (19%)
  other arithmetic  128 us (14%)
  Pallas kernels  113 us (12%)
  starting transfers between devices  60.6 us (7%)
  local copies, waits for them, and re-layouts  44.2 us (5%)
  between operations  16.1 us (2%)
    ppermute x88, waiting for transfers between devices, across(): return lax.ppermute(array, axis, [(at, at ^ step) for at in range(size)])  274 us
    dot_general x28, matrix products, product(): return jnp.dot(left, right, preferred_element_type=F32)  106 us
    all_gather x7, waiting for transfers between devices, collect(): return lax.all_gather(piece, 'shard', axis=0, tiled=True)  91.3 us
    dot_general x28, matrix products, transposed_times(): lax.dot_general(left, right, (((0,), (0,)), ((), ())), preferred_element_...  66.5 us
    pallas_call x4, Pallas kernels, sum_products(): pl.pallas_call(sum_kernel, grid=(width // block,), in_specs=[pl.BlockSpec...  51.9 us
    ppermute x88, starting transfers between devices, across(): return lax.ppermute(array, axis, [(at, at ^ step) for at in range(size)])  48.6 us
    pallas_call x4, Pallas kernels, attention_back(): pl.pallas_call(backward_kernel, grid=(heads, rows // block), in_specs=[ro...  35.1 us
    pallas_call x4, Pallas kernels, attention(): pl.pallas_call(forward_kernel, grid=(heads, rows // block), in_specs=[row...  26.1 us
  transfers between devices with their start and end apart: 106, of which 32 were waited for; matrix products, arithmetic and copies ran while one was open for 35% of the time, Pallas kernels for 11%

profile of v4, /device:TPU:0, one launch (start us, length us, event | category | flops | bytes accessed | tf_op | source)
XLA Modules:
  0.0 912.4 jit_solution(16750214378516261154)
XLA Ops:
  26.1 6.5 collective-permute-done.1
  33.8 7.7 collective-permute-done.2
  41.5 23.7 %collective-permute-done.3 = bf16[512,2048]{1,0:T(8,128)(2,1)} collective-permute-done((bf16[512,2048]{1,0:T(8,128)(2,1)S(1)}, bf16[512,2048]{1,0:T(8,128)(2,1)}, u32[]{:S(2)}, u32[]{:S(2)}) %collective-permute-start.3) | collective-permute-done | bytes 2097184 | tf_op jit(solution)/shard_map/ppermute | solution.py:164
  67.9 39.4 %all-gather.8.cloned.1.call-done = bf16[2048,512]{1,0:T(8,128)(2,1)} async-done(((bf16[512,512]{1,0:T(8,128)(2,1)}), bf16[2048,512]{1,0:T(8,128)(2,1)}) %all-gather.8.cloned.1.call-update) | async-done | bytes 2097168 | tf_op jit(solution)/shard_map/all_gather | solution.py:168
  108.8 5.5 add_convert_fusion.17.kh_ref.vh_ref
  125.2 28.8 %all-gather.12.cloned.1.call-done.refs_8_ = bf16[2048,512]{1,0:T(8,128)(2,1)} async-done(((bf16[512,512]{1,0:T(8,128)(2,1)}), bf16[2048,512]{1,0:T(8,128)(2,1)}) %all-gather.12.cloned.1.call-update) | async-done | bytes 2097168 | tf_op jit(solution)/shard_map/all_gather | solution.py:168
  158.8 5.5 add_convert_fusion.16.kh_ref.vh_ref
  173.5 6.9 attention_forward.5
  180.4 5.5 add_convert_fusion.14.kh_ref.vh_ref
  189.1 6.4 attention_forward.4
  198.1 6.4 attention_forward.7
  208.1 6.5 attention_forward.6
  214.6 8.3 sum_products.4
  228.6 18.3 %all-gather.16.cloned.1.call-done.refs_8_ = bf16[2048,512]{1,0:T(8,128)(2,1)} async-done(((bf16[512,512]{1,0:T(8,128)(2,1)}), bf16[2048,512]{1,0:T(8,128)(2,1)}) %all-gather.16.cloned.1.call-update) | async-done | bytes 2097168 | tf_op jit(solution)/shard_map/all_gather | solution.py:168
  246.9 5.6 collective-permute-done.19.refs_14_
  253.0 17.4 %collective-permute-done.14 = bf16[512,2048]{1,0:T(8,128)(2,1)} collective-permute-done((bf16[512,2048]{1,0:T(8,128)(2,1)}, bf16[512,2048]{1,0:T(8,128)(2,1)}, u32[]{:S(2)}, u32[]{:S(2)}) %collective-permute-start.14) | collective-permute-done | bytes 2097184 | tf_op jit(solution)/shard_map/ppermute | solution.py:164
  270.5 4.9 fusion.146
  288.5 4.9 all-gather.18.cloned.1.call-done.refs_12_
  304.7 5.0 multiply_convert_fusion.4
  314.5 9.1 collective-permute-done.25
  336.1 15.2 %sum_products.5 = bf16[512,2048]{1,0:T(8,128)(2,1)} custom-call(bf16[512,512]{1,0:T(8,128)(2,1)} %get-tuple-element.245.refs_0_, bf16[512,512]{1,0:T(8,128)(2,1)} %get-tuple-element.247.refs_1_, bf16[512,512]{1,0:T(8,128)(2,1)} %get-tuple-element.249.refs_2_, bf16[512,512]{1,0:T(8,128)(2,1)} %get-tuple-element.251.refs_3_, ...), custom_call_target="tpu_custom_call" | custom-call | tf_op jit(solution)/shard_map/sum_products/pallas_call | solution.py:147
  353.0 46.2 %collective-permute-done.27 = bf16[512,2048]{1,0:T(8,128)(2,1)S(1)} collective-permute-done((bf16[512,2048]{1,0:T(8,128)(2,1)}, bf16[512,2048]{1,0:T(8,128)(2,1)S(1)}, u32[]{:S(2)}, u32[]{:S(2)}) %collective-permute-start.27) | collective-permute-done | bytes 2097184 | tf_op jit(solution)/shard_map/ppermute | solution.py:164
  399.2 4.8 fusion.144
  429.9 5.0 add_convert_fusion.9
  466.1 15.2 %sum_products.6 = bf16[512,2048]{1,0:T(8,128)(2,1)} custom-call(bf16[512,512]{1,0:T(8,128)(2,1)} %get-tuple-element.143.refs_0_, bf16[512,512]{1,0:T(8,128)(2,1)} %get-tuple-element.147.refs_1_, bf16[512,512]{1,0:T(8,128)(2,1)} %get-tuple-element.151.refs_2_, bf16[512,512]{1,0:T(8,128)(2,1)} %get-tuple-element.155.refs_3_, ...), custom_call_target="tpu_custom_call" | custom-call | tf_op jit(solution)/shard_map/sum_products/pallas_call | solution.py:147
  513.9 20.6 %collective-permute-done.32 = bf16[512,2048]{1,0:T(8,128)(2,1)} collective-permute-done((bf16[512,2048]{1,0:T(8,128)(2,1)}, bf16[512,2048]{1,0:T(8,128)(2,1)}, u32[]{:S(2)}, u32[]{:S(2)}) %collective-permute-start.32) | collective-permute-done | bytes 2097184 | tf_op jit(solution)/shard_map/ppermute | solution.py:164
  534.5 8.6 multiply_reduce_fusion.3
  546.6 7.5 collective-permute-done.46
  567.3 8.7 attention_backward.4
  591.4 8.8 attention_backward.5
  606.5 8.7 attention_backward.7
  617.9 9.0 attention_backward.6
  637.3 10.5 %collective-permute-done.49 = bf16[512,512]{1,0:T(8,128)(2,1)S(1)} collective-permute-done((bf16[512,512]{1,0:T(8,128)(2,1)S(1)}, bf16[512,512]{1,0:T(8,128)(2,1)S(1)}, u32[]{:S(2)}, u32[]{:S(2)}) %collective-permute-start.49) | collective-permute-done | bytes 524320 | tf_op jit(solution)/shard_map/ppermute | solution.py:164
  647.7 10.3 %collective-permute-done.52 = bf16[512,512]{1,0:T(8,128)(2,1)S(1)} collective-permute-done((bf16[512,512]{1,0:T(8,128)(2,1)S(1)}, bf16[512,512]{1,0:T(8,128)(2,1)S(1)}, u32[]{:S(2)}, u32[]{:S(2)}) %collective-permute-start.52) | collective-permute-done | bytes 524320 | tf_op jit(solution)/shard_map/ppermute | solution.py:164
  676.8 8.7 collective-permute-done.83
  685.5 4.7 fusion.9
  705.0 10.7 %collective-permute-done.92 = f32[152,128]{1,0:T(8,128)S(1)} collective-permute-done((f32[152,128]{1,0:T(8,128)S(1)}, f32[152,128]{1,0:T(8,128)S(1)}, u32[]{:S(2)}, u32[]{:S(2)}) %collective-permute-start.92) | collective-permute-done | bytes 77856 | tf_op jit(solution)/shard_map/ppermute | solution.py:164
  715.7 7.1 collective-permute-start.71
  724.0 27.0 %collective-permute-done.93 = f32[152,128]{1,0:T(8,128)S(1)} collective-permute-done((f32[152,128]{1,0:T(8,128)S(1)}, f32[152,128]{1,0:T(8,128)S(1)}, u32[]{:S(2)}, u32[]{:S(2)}) %collective-permute-start.93) | collective-permute-done | bytes 77856 | tf_op jit(solution)/shard_map/ppermute | solution.py:164
  757.8 10.2 %collective-permute-done.88 = bf16[512,512]{1,0:T(8,128)(2,1)S(1)} collective-permute-done((bf16[512,512]{1,0:T(8,128)(2,1)S(1)}, bf16[512,512]{1,0:T(8,128)(2,1)S(1)}, u32[]{:S(2)}, u32[]{:S(2)}) %collective-permute-start.88) | collective-permute-done | bytes 524320 | tf_op jit(solution)/shard_map/ppermute | solution.py:164
  769.5 8.9 collective-permute-done.86
  786.5 13.2 %sum_products.7 = bf16[512,2048]{1,0:T(8,128)(2,1)} custom-call(bf16[512,256]{1,0:T(8,128)(2,1)} %get-tuple-element.116.refs_0_, bf16[512,256]{1,0:T(8,128)(2,1)} %get-tuple-element.117.refs_1_, bf16[512,256]{1,0:T(8,128)(2,1)} %get-tuple-element.118.refs_2_, bf16[512,256]{1,0:T(8,128)(2,1)} %get-tuple-element.119.refs_3_, ...), custom_call_target="tpu_custom_call" | custom-call | tf_op jit(solution)/shard_map/sum_products/pallas_call | solution.py:147
  813.5 6.8 convert_element_type.931
  820.3 5.8 collective-permute-done.59
  840.9 11.0 %collective-permute-done.61 = bf16[512,256]{1,0:T(8,128)(2,1)} collective-permute-done((bf16[512,256]{1,0:T(8,128)(2,1)}, bf16[512,256]{1,0:T(8,128)(2,1)}, u32[]{:S(2)}, u32[]{:S(2)}) %collective-permute-start.61) | collective-permute-done | bytes 262176 | tf_op jit(solution)/shard_map/ppermute | solution.py:185
  855.1 4.7 collective-permute-done.79
  879.4 6.8 convert_element_type.924
  888.9 8.9 collective-permute-done.56
  (627 shorter events, 360.5 us)
Async XLA Ops:
  7.2 58.1 %all-gather.10.cloned.1.call-start = ((), (), s32[]{:S(2)}) async-start(), calls=%async_computation.6 | async-start | bytes 2621440 | tf_op jit(solution)/shard_map/all_gather | solution.py:168
  9.2 98.1 %all-gather.8.cloned.1.call-start = ((), (), s32[]{:S(2)}) async-start(), calls=%async_computation.5 | async-start | bytes 2621440 | tf_op jit(solution)/shard_map/all_gather | solution.py:168
  11.2 142.8 %all-gather.12.cloned.1.call-start = ((), (), s32[]{:S(2)}) async-start(), calls=%async_computation.7 | async-start | bytes 2621440 | tf_op jit(solution)/shard_map/all_gather | solution.py:168
  13.5 191.0 %all-gather.14.cloned.1.call-start = ((), (), s32[]{:S(2)}) async-start(), calls=%async_computation.8 | async-start | bytes 2621440 | tf_op jit(solution)/shard_map/all_gather | solution.py:168
  14.1 232.8 %all-gather.16.cloned.1.call-start = ((), (), s32[]{:S(2)}) async-start(), calls=%async_computation.9 | async-start | bytes 2621440 | tf_op jit(solution)/shard_map/all_gather | solution.py:168
  16.4 277.0 %all-gather.18.cloned.1.call-start = ((), (), s32[]{:S(2)}) async-start(), calls=%async_computation.10 | async-start | bytes 2621440 | tf_op jit(solution)/shard_map/all_gather | solution.py:168
  16.5 48.8 %collective-permute-start.3 = (bf16[512,2048]{1,0:T(8,128)(2,1)S(1)}, bf16[512,2048]{1,0:T(8,128)(2,1)}, u32[]{:S(2)}, u32[]{:S(2)}) collective-permute-start(bf16[512,2048]{1,0:T(8,128)(2,1)S(1)} %bitcast.266), channel_id=1, source_target_pairs={{0,4},{2,6},{4,0},{6,2},{1,5},{3,7},{5,1},{7,3},{8,12},{10,14},{12... | collective-permute-start | bytes 6291464 | tf_op jit(solution)/shard_map/ppermute | solution.py:164
  21.7 307.6 %all-gather.20.cloned.1.call-start = ((), (), s32[]{:S(2)}) async-start(), calls=%async_computation.11 | async-start | bytes 1310720 | tf_op jit(solution)/shard_map/all_gather | solution.py:168
  65.2 55.4 %collective-permute-start.9 = (bf16[2048,512]{1,0:T(8,128)(2,1)}, bf16[2048,512]{1,0:T(8,128)(2,1)}, u32[]{:S(2)}, u32[]{:S(2)}) collective-permute-start(bf16[2048,512]{1,0:T(8,128)(2,1)} %all-gather.10.cloned.1.call-done.refs_12_), channel_id=1, source_target_pairs={{0,4},{2,6},{4,0},{6,2},{1,5},{3,7},{5,1},{7,3},{8,12},{10,14},{12... | collective-permute-start | bytes 6291464 | tf_op jit(solution)/shard_map/ppermute | solution.py:164
  67.9 90.9 %collective-permute-start.4 = (bf16[2048,512]{1,0:T(8,128)(2,1)}, bf16[2048,512]{1,0:T(8,128)(2,1)}, u32[]{:S(2)}, u32[]{:S(2)}) collective-permute-start(bf16[2048,512]{1,0:T(8,128)(2,1)} %all-gather.10.cloned.1.call-done.refs_12_), channel_id=1, source_target_pairs={{0,2},{2,0},{4,6},{6,4},{1,3},{3,1},{5,7},{7,5},{8,10},{10,8},{12,... | collective-permute-start | bytes 6291464 | tf_op jit(solution)/shard_map/ppermute | solution.py:164
  107.3 50.0 %collective-permute-start.8 = (bf16[2048,512]{1,0:T(8,128)(2,1)}, bf16[2048,512]{1,0:T(8,128)(2,1)}, u32[]{:S(2)}, u32[]{:S(2)}) collective-permute-start(bf16[2048,512]{1,0:T(8,128)(2,1)} %all-gather.8.cloned.1.call-done), channel_id=1, source_target_pairs={{0,4},{2,6},{4,0},{6,2},{1,5},{3,7},{5,1},{7,3},{8,12},{10,14},{12... | collective-permute-start | bytes 6291464 | tf_op jit(solution)/shard_map/ppermute | solution.py:164
  114.4 59.1 %collective-permute-start.7 = (bf16[1024,512]{1,0:T(8,128)(2,1)}, bf16[1024,512]{1,0:T(8,128)(2,1)}, u32[]{:S(2)}, u32[]{:S(2)}) collective-permute-start(bf16[1024,512]{1,0:T(8,128)(2,1)} %add_convert_fusion.17.kh_ref.vh_ref), channel_id=1, source_target_pairs={{0,2},{2,0},{4,6},{6,4},{1,3},{3,1},{5,7},{7,5},{8,10},{10,8},{12,... | collective-permute-start | bytes 3145736 | tf_op jit(solution)/shard_map/ppermute | solution.py:164
  114.4 52.9 %collective-permute-start.6 = (bf16[2048,512]{1,0:T(8,128)(2,1)}, bf16[2048,512]{1,0:T(8,128)(2,1)}, u32[]{:S(2)}, u32[]{:S(2)}) collective-permute-start(bf16[2048,512]{1,0:T(8,128)(2,1)} %all-gather.8.cloned.1.call-done), channel_id=1, source_target_pairs={{0,2},{2,0},{4,6},{6,4},{1,3},{3,1},{5,7},{7,5},{8,10},{10,8},{12,... | collective-permute-start | bytes 6291464 | tf_op jit(solution)/shard_map/ppermute | solution.py:164
  120.6 59.8 %collective-permute-start.10 = (bf16[2048,512]{1,0:T(8,128)(2,1)}, bf16[2048,512]{1,0:T(8,128)(2,1)}, u32[]{:S(2)}, u32[]{:S(2)}) collective-permute-start(bf16[2048,512]{1,0:T(8,128)(2,1)} %collective-permute-done.9.refs_14_), channel_id=1, source_target_pairs={{0,2},{2,0},{4,6},{6,4},{1,3},{3,1},{5,7},{7,5},{8,10},{10,8},{12,... | collective-permute-start | bytes 6291464 | tf_op jit(solution)/shard_map/ppermute | solution.py:164
  157.3 70.8 %collective-permute-start.16 = (bf16[2048,512]{1,0:T(8,128)(2,1)}, bf16[2048,512]{1,0:T(8,128)(2,1)}, u32[]{:S(2)}, u32[]{:S(2)}) collective-permute-start(bf16[2048,512]{1,0:T(8,128)(2,1)} %all-gather.12.cloned.1.call-done.refs_8_), channel_id=1, source_target_pairs={{0,4},{2,6},{4,0},{6,2},{1,5},{3,7},{5,1},{7,3},{8,12},{10,14},{12... | collective-permute-start | bytes 6291464 | tf_op jit(solution)/shard_map/ppermute | solution.py:164
  158.7 36.7 %collective-permute-start.12 = (bf16[2048,512]{1,0:T(8,128)(2,1)}, bf16[2048,512]{1,0:T(8,128)(2,1)}, u32[]{:S(2)}, u32[]{:S(2)}) collective-permute-start(bf16[2048,512]{1,0:T(8,128)(2,1)} %collective-permute-done.8), channel_id=1, source_target_pairs={{0,2},{2,0},{4,6},{6,4},{1,3},{3,1},{5,7},{7,5},{8,10},{10,8},{12,... | collective-permute-start | bytes 6291464 | tf_op jit(solution)/shard_map/ppermute | solution.py:164
  204.5 48.0 %collective-permute-start.19 = (bf16[2048,512]{1,0:T(8,128)(2,1)}, bf16[2048,512]{1,0:T(8,128)(2,1)}, u32[]{:S(2)}, u32[]{:S(2)}) collective-permute-start(bf16[2048,512]{1,0:T(8,128)(2,1)} %all-gather.14.cloned.1.call-done.refs_12_), channel_id=1, source_target_pairs={{0,4},{2,6},{4,0},{6,2},{1,5},{3,7},{5,1},{7,3},{8,12},{10,14},{12... | collective-permute-start | bytes 6291464 | tf_op jit(solution)/shard_map/ppermute | solution.py:164
  222.9 47.6 %collective-permute-start.14 = (bf16[512,2048]{1,0:T(8,128)(2,1)}, bf16[512,2048]{1,0:T(8,128)(2,1)}, u32[]{:S(2)}, u32[]{:S(2)}) collective-permute-start(bf16[512,2048]{1,0:T(8,128)(2,1)} %sum_products.4), channel_id=1, source_target_pairs={{0,1},{1,0},{2,3},{3,2},{4,5},{5,4},{6,7},{7,6},{8,9},{9,8},{10,11... | collective-permute-start | bytes 6291464 | tf_op jit(solution)/shard_map/ppermute | solution.py:164
  226.1 445.2 %reduce-scatter.12.cloned.1.call-start = ((), (), s32[]{:S(2)}) async-start(), calls=%async_computation.15 | async-start | bytes 2621440 | tf_op jit(solution)/shard_map/reduce_scatter | solution.py:172
  228.0 70.9 %collective-permute-start.15 = (bf16[2048,512]{1,0:T(8,128)(2,1)}, bf16[2048,512]{1,0:T(8,128)(2,1)}, u32[]{:S(2)}, u32[]{:S(2)}) collective-permute-start(bf16[2048,512]{1,0:T(8,128)(2,1)} %all-gather.12.cloned.1.call-done.refs_8_), channel_id=1, source_target_pairs={{0,2},{2,0},{4,6},{6,4},{1,3},{3,1},{5,7},{7,5},{8,10},{10,8},{12,... | collective-permute-start | bytes 6291464 | tf_op jit(solution)/shard_map/ppermute | solution.py:164
  228.1 76.6 %collective-permute-start.17 = (bf16[2048,512]{1,0:T(8,128)(2,1)}, bf16[2048,512]{1,0:T(8,128)(2,1)}, u32[]{:S(2)}, u32[]{:S(2)}) collective-permute-start(bf16[2048,512]{1,0:T(8,128)(2,1)} %collective-permute-done.16.refs_10_), channel_id=1, source_target_pairs={{0,2},{2,0},{4,6},{6,4},{1,3},{3,1},{5,7},{7,5},{8,10},{10,8},{12,... | collective-permute-start | bytes 6291464 | tf_op jit(solution)/shard_map/ppermute | solution.py:164
  228.5 81.1 %collective-permute-start.18 = (bf16[2048,512]{1,0:T(8,128)(2,1)}, bf16[2048,512]{1,0:T(8,128)(2,1)}, u32[]{:S(2)}, u32[]{:S(2)}) collective-permute-start(bf16[2048,512]{1,0:T(8,128)(2,1)} %all-gather.14.cloned.1.call-done.refs_12_), channel_id=1, source_target_pairs={{0,2},{2,0},{4,6},{6,4},{1,3},{3,1},{5,7},{7,5},{8,10},{10,8},{12,... | collective-permute-start | bytes 6291464 | tf_op jit(solution)/shard_map/ppermute | solution.py:164
  252.5 57.7 %collective-permute-start.22 = (bf16[2048,512]{1,0:T(8,128)(2,1)}, bf16[2048,512]{1,0:T(8,128)(2,1)}, u32[]{:S(2)}, u32[]{:S(2)}) collective-permute-start(bf16[2048,512]{1,0:T(8,128)(2,1)} %all-gather.16.cloned.1.call-done.refs_8_), channel_id=1, source_target_pairs={{0,4},{2,6},{4,0},{6,2},{1,5},{3,7},{5,1},{7,3},{8,12},{10,14},{12... | collective-permute-start | bytes 6291464 | tf_op jit(solution)/shard_map/ppermute | solution.py:164
  270.5 54.2 %collective-permute-start.20 = (bf16[2048,512]{1,0:T(8,128)(2,1)}, bf16[2048,512]{1,0:T(8,128)(2,1)}, u32[]{:S(2)}, u32[]{:S(2)}) collective-permute-start(bf16[2048,512]{1,0:T(8,128)(2,1)} %collective-permute-done.19.refs_14_), channel_id=1, source_target_pairs={{0,2},{2,0},{4,6},{6,4},{1,3},{3,1},{5,7},{7,5},{8,10},{10,8},{12,... | collective-permute-start | bytes 6291464 | tf_op jit(solution)/shard_map/ppermute | solution.py:164
  304.7 26.9 %collective-permute-start.21 = (bf16[2048,512]{1,0:T(8,128)(2,1)}, bf16[2048,512]{1,0:T(8,128)(2,1)}, u32[]{:S(2)}, u32[]{:S(2)}) collective-permute-start(bf16[2048,512]{1,0:T(8,128)(2,1)} %all-gather.16.cloned.1.call-done.refs_8_), channel_id=1, source_target_pairs={{0,2},{2,0},{4,6},{6,4},{1,3},{3,1},{5,7},{7,5},{8,10},{10,8},{12,... | collective-permute-start | bytes 6291464 | tf_op jit(solution)/shard_map/ppermute | solution.py:164
  351.3 48.0 %collective-permute-start.27 = (bf16[512,2048]{1,0:T(8,128)(2,1)}, bf16[512,2048]{1,0:T(8,128)(2,1)S(1)}, u32[]{:S(2)}, u32[]{:S(2)}) collective-permute-start(bf16[512,2048]{1,0:T(8,128)(2,1)} %sum_products.5), channel_id=1, source_target_pairs={{0,1},{1,0},{2,3},{3,2},{4,5},{5,4},{6,7},{7,6},{8,9},{9,8},{10,11... | collective-permute-start | bytes 6291464 | tf_op jit(solution)/shard_map/ppermute | solution.py:164
  422.9 58.5 %collective-permute-start.33 = (bf16[2048,512]{1,0:T(8,128)(2,1)}, bf16[2048,512]{1,0:T(8,128)(2,1)}, u32[]{:S(2)}, u32[]{:S(2)}) collective-permute-start(bf16[2048,512]{1,0:T(8,128)(2,1)} %add_convert_fusion.8), channel_id=1, source_target_pairs={{0,4},{2,6},{4,0},{6,2},{1,5},{3,7},{5,1},{7,3},{8,12},{10,14},{12... | collective-permute-start | bytes 6291464 | tf_op jit(solution)/shard_map/ppermute | solution.py:164
  485.5 266.3 %reduce-scatter.14.cloned.1.call-start = ((), (), s32[]{:S(2)}) async-start(), calls=%async_computation.16 | async-start | bytes 5242880 | tf_op jit(solution)/shard_map/reduce_scatter | solution.py:172
  486.3 300.3 %reduce-scatter.8.cloned.1.call-start = ((), (), s32[]{:S(2)}) async-start(), calls=%async_computation.13 | async-start | bytes 2621440 | tf_op jit(solution)/shard_map/reduce_scatter | solution.py:172
  486.8 47.6 %collective-permute-start.32 = (bf16[512,2048]{1,0:T(8,128)(2,1)}, bf16[512,2048]{1,0:T(8,128)(2,1)}, u32[]{:S(2)}, u32[]{:S(2)}) collective-permute-start(bf16[512,2048]{1,0:T(8,128)(2,1)} %sum_products.6), channel_id=1, source_target_pairs={{0,1},{1,0},{2,3},{3,2},{4,5},{5,4},{6,7},{7,6},{8,9},{9,8},{10,11... | collective-permute-start | bytes 6291464 | tf_op jit(solution)/shard_map/ppermute | solution.py:164
  506.2 47.9 %collective-permute-start.46 = (bf16[2048,512]{1,0:T(8,128)(2,1)}, bf16[2048,512]{1,0:T(8,128)(2,1)}, u32[]{:S(2)}, u32[]{:S(2)}) collective-permute-start(bf16[2048,512]{1,0:T(8,128)(2,1)} %add_convert_fusion.3), channel_id=1, source_target_pairs={{0,4},{2,6},{4,0},{6,2},{1,5},{3,7},{5,1},{7,3},{8,12},{10,14},{12... | collective-permute-start | bytes 6291464 | tf_op jit(solution)/shard_map/ppermute | solution.py:164
  557.6 273.0 %reduce-scatter.10.cloned.1.call-start = ((), (), s32[]{:S(2)}) async-start(), calls=%async_computation.14 | async-start | bytes 5242880 | tf_op jit(solution)/shard_map/reduce_scatter | solution.py:172
  576.6 298.1 %reduce-scatter.6.cloned.1.call-start = ((), (), s32[]{:S(2)}) async-start(), calls=%async_computation.12 | async-start | bytes 2621440 | tf_op jit(solution)/shard_map/reduce_scatter | solution.py:172
  587.8 78.3 %collective-permute-start.69 = (bf16[2048,256]{1,0:T(8,128)(2,1)}, bf16[2048,256]{1,0:T(8,128)(2,1)}, u32[]{:S(2)}, u32[]{:S(2)}) collective-permute-start(bf16[2048,256]{1,0:T(8,128)(2,1)} %fusion.20), channel_id=1, source_target_pairs={{0,4},{2,6},{4,0},{6,2},{1,5},{3,7},{5,1},{7,3},{8,12},{10,14},{12... | collective-permute-start | bytes 3145736 | tf_op jit(solution)/shard_map/ppermute | solution.py:164
  605.1 32.1 %collective-permute-start.45 = (bf16[512,512]{1,0:T(8,128)(2,1)}, bf16[512,512]{1,0:T(8,128)(2,1)}, u32[]{:S(2)}, u32[]{:S(2)}) collective-permute-start(bf16[512,512]{1,0:T(8,128)(2,1)} %fusion.104), channel_id=1, source_target_pairs={{0,4},{2,6},{4,0},{6,2},{1,5},{3,7},{5,1},{7,3},{8,12},{10,14},{12... | collective-permute-start | bytes 1572872 | tf_op jit(solution)/shard_map/ppermute | solution.py:164
  637.3 64.4 %collective-permute-start.58 = (bf16[2048,256]{1,0:T(8,128)(2,1)}, bf16[2048,256]{1,0:T(8,128)(2,1)}, u32[]{:S(2)}, u32[]{:S(2)}) collective-permute-start(bf16[2048,256]{1,0:T(8,128)(2,1)} %fusion.33), channel_id=1, source_target_pairs={{0,2},{2,0},{4,6},{6,4},{1,3},{3,1},{5,7},{7,5},{8,10},{10,8},{12,... | collective-permute-start | bytes 3145736 | tf_op jit(solution)/shard_map/ppermute | solution.py:164
  676.8 46.0 %collective-permute-start.85 = (bf16[512,512]{1,0:T(8,128)(2,1)}, bf16[512,512]{1,0:T(8,128)(2,1)S(1)}, u32[]{:S(2)}, u32[]{:S(2)}) collective-permute-start(bf16[512,512]{1,0:T(8,128)(2,1)} %reduce-scatter.12.cloned.1.call-done), channel_id=1, source_target_pairs={{0,2},{2,0},{4,6},{6,4},{1,3},{3,1},{5,7},{7,5},{8,10},{10,8},{12,... | collective-permute-start | bytes 1572872 | tf_op jit(solution)/shard_map/ppermute | solution.py:164
  685.5 37.4 %collective-permute-start.84 = (bf16[512,512]{1,0:T(8,128)(2,1)S(1)}, bf16[512,512]{1,0:T(8,128)(2,1)S(1)}, u32[]{:S(2)}, u32[]{:S(2)}) collective-permute-start(bf16[512,512]{1,0:T(8,128)(2,1)S(1)} %collective-permute-done.83), channel_id=1, source_target_pairs={{0,2},{2,0},{4,6},{6,4},{1,3},{3,1},{5,7},{7,5},{8,10},{10,8},{12,... | collective-permute-start | bytes 1572872 | tf_op jit(solution)/shard_map/ppermute | solution.py:164
  698.2 84.6 %collective-permute-start.70 = (bf16[512,256]{1,0:T(8,128)(2,1)}, bf16[512,256]{1,0:T(8,128)(2,1)}, u32[]{:S(2)}, u32[]{:S(2)}) collective-permute-start(bf16[512,256]{1,0:T(8,128)(2,1)} %get-tuple-element.200), channel_id=1, source_target_pairs={{0,8},{8,16},{16,24},{24,0},{1,9},{9,17},{17,25},{25,1},{2,10},{10... | collective-permute-start | bytes 786440 | tf_op jit(solution)/shard_map/ppermute | solution.py:185
  701.0 77.8 %collective-permute-start.55 = (bf16[2048,512]{1,0:T(8,128)(2,1)}, bf16[2048,512]{1,0:T(8,128)(2,1)}, u32[]{:S(2)}, u32[]{:S(2)}) collective-permute-start(bf16[2048,512]{1,0:T(8,128)(2,1)} %fusion.9), channel_id=1, source_target_pairs={{0,4},{2,6},{4,0},{6,2},{1,5},{3,7},{5,1},{7,3},{8,12},{10,14},{12... | collective-permute-start | bytes 6291464 | tf_op jit(solution)/shard_map/ppermute | solution.py:164
  715.7 67.2 %collective-permute-start.71 = (bf16[512,256]{1,0:T(8,128)(2,1)}, bf16[512,256]{1,0:T(8,128)(2,1)}, u32[]{:S(2)}, u32[]{:S(2)}) collective-permute-start(bf16[512,256]{1,0:T(8,128)(2,1)} %get-tuple-element.199), channel_id=1, source_target_pairs={{0,16},{8,24},{16,0},{24,8},{1,17},{9,25},{17,1},{25,9},{2,18},{10... | collective-permute-start | bytes 786440 | tf_op jit(solution)/shard_map/ppermute | solution.py:185
  722.8 28.2 %collective-permute-start.93 = (f32[152,128]{1,0:T(8,128)S(1)}, f32[152,128]{1,0:T(8,128)S(1)}, u32[]{:S(2)}, u32[]{:S(2)}) collective-permute-start(f32[152,128]{1,0:T(8,128)S(1)} %add.725), channel_id=1, source_target_pairs={{0,16},{8,24},{16,0},{24,8},{1,17},{9,25},{17,1},{25,9},{2,18},{10... | collective-permute-start | bytes 233480 | tf_op jit(solution)/shard_map/ppermute | solution.py:164
  782.8 37.5 %collective-permute-start.57 = (bf16[2048,256]{1,0:T(8,128)(2,1)}, bf16[2048,256]{1,0:T(8,128)(2,1)}, u32[]{:S(2)}, u32[]{:S(2)}) collective-permute-start(bf16[2048,256]{1,0:T(8,128)(2,1)} %fusion.32), channel_id=1, source_target_pairs={{0,2},{2,0},{4,6},{6,4},{1,3},{3,1},{5,7},{7,5},{8,10},{10,8},{12,... | collective-permute-start | bytes 3145736 | tf_op jit(solution)/shard_map/ppermute | solution.py:164
  784.9 35.4 %collective-permute-start.73 = (bf16[512,256]{1,0:T(8,128)(2,1)}, bf16[512,256]{1,0:T(8,128)(2,1)}, u32[]{:S(2)}, u32[]{:S(2)}) collective-permute-start(bf16[512,256]{1,0:T(8,128)(2,1)} %add_convert_fusion.34), channel_id=1, source_target_pairs={{0,4},{2,6},{4,0},{6,2},{1,5},{3,7},{5,1},{7,3},{8,12},{10,14},{12... | collective-permute-start | bytes 786440 | tf_op jit(solution)/shard_map/ppermute | solution.py:164
  786.3 45.5 %collective-permute-start.75 = (bf16[512,256]{1,0:T(8,128)(2,1)}, bf16[512,256]{1,0:T(8,128)(2,1)}, u32[]{:S(2)}, u32[]{:S(2)}) collective-permute-start(bf16[512,256]{1,0:T(8,128)(2,1)} %add_convert_fusion.34), channel_id=1, source_target_pairs={{0,2},{2,0},{4,6},{6,4},{1,3},{3,1},{5,7},{7,5},{8,10},{10,8},{12,... | collective-permute-start | bytes 786440 | tf_op jit(solution)/shard_map/ppermute | solution.py:164
  799.7 26.3 %collective-permute-start.59 = (bf16[2048,256]{1,0:T(8,128)(2,1)}, bf16[2048,256]{1,0:T(8,128)(2,1)S(1)}, u32[]{:S(2)}, u32[]{:S(2)}) collective-permute-start(bf16[2048,256]{1,0:T(8,128)(2,1)} %fusion.31), channel_id=1, source_target_pairs={{0,4},{2,6},{4,0},{6,2},{1,5},{3,7},{5,1},{7,3},{8,12},{10,14},{12... | collective-permute-start | bytes 3145736 | tf_op jit(solution)/shard_map/ppermute | solution.py:164
  800.4 37.0 %collective-permute-start.76 = (bf16[512,512]{1,0:T(8,128)(2,1)}, bf16[512,512]{1,0:T(8,128)(2,1)}, u32[]{:S(2)}, u32[]{:S(2)}) collective-permute-start(bf16[512,512]{1,0:T(8,128)(2,1)} %reduce-scatter.8.cloned.1.call-done), channel_id=1, source_target_pairs={{0,4},{2,6},{4,0},{6,2},{1,5},{3,7},{5,1},{7,3},{8,12},{10,14},{12... | collective-permute-start | bytes 1572872 | tf_op jit(solution)/shard_map/ppermute | solution.py:164
  851.8 46.0 %collective-permute-start.56 = (bf16[512,2048]{1,0:T(8,128)(2,1)S(1)}, bf16[512,2048]{1,0:T(8,128)(2,1)}, u32[]{:S(2)}, u32[]{:S(2)}) collective-permute-start(bf16[512,2048]{1,0:T(8,128)(2,1)S(1)} %copy-done.8), channel_id=1, source_target_pairs={{0,1},{1,0},{2,3},{3,2},{4,5},{5,4},{6,7},{7,6},{8,9},{9,8},{10,11... | collective-permute-start | bytes 6291464 | tf_op jit(solution)/shard_map/ppermute | solution.py:164
  (156 other events, 1920.5 us)
Sparse Core Ops, SparseCore 0:
  10.1 50.4 all-gather.9
  62.8 44.4 all-gather.7
  109.4 44.4 all-gather.11
  155.9 44.4 all-gather.13
  202.4 44.4 all-gather.15
  248.9 44.4 all-gather.17
  295.5 26.7 all-gather.19
  485.6 42.1 reduce-scatter.11
  530.1 75.9 reduce-scatter.13
  608.9 44.1 reduce-scatter.7
  655.4 90.2 reduce-scatter.9
  786.6 41.7 reduce-scatter.5
